TPU v7x, 256 devices: a whole 4x4x8 slice. The times are simulated.
256 devices in a mesh: depth: 8 (over y_lo, x), gx: 32 (over z, y_hi, core).
Axes of the slice: x: 4, y: 4 (y_hi: 2, y_lo: 2; y = y_hi * 2 + y_lo), z: 8, core: 2. Of those that a mesh axis runs over, the one named last changes fastest.
Arguments:
- offset_image: bfloat16 [64, 128, 128, 256], P(None, 'depth', 'gx'), may hold values from -6 to 6
- dip_class: int32 [128, 128, 256], P('depth', 'gx'), may hold values from 0 to 7
- slant_taper: bfloat16 [64, 64, 33], replicated, may hold values from -0.3125 to 0.3125
- band_offsets: int32 [64], replicated, may hold values from -14 to 14
- coefficients: float32 [8, 27], replicated, may hold values from -1.25 to 1.25
Outputs:
- smoothed: bfloat16 [64, 128, 128, 256], P(None, 'depth', 'gx')
All inputs are finite; a program needn't handle non-finite values.
Results may differ from a plain program's by a relative error of at most 0.0049.
Values may be sent and summed in bfloat16 or wider, within the bound.
No kernel may reach another device: no remote copies, remote signals or barrier semaphores. Data moves between devices by JAX's collectives and lax.ppermute only.
A program may use at most 64 MiB of HBM per device.

v0:
```python
import functools

import jax
import jax.numpy as jnp
from jax import lax
from jax.experimental import pallas as pl
from jax.experimental.pallas import tpu as pltpu
from jax.sharding import PartitionSpec as P


R = 16
BAND = 2
RX = 4
RY = 1
REACH = R - BAND
ZB = 4
HALVES = 2
LAST_PARTS = (8, 8)
PART = 32
SIDES = 2 * RY + 1
BF = jnp.bfloat16
F32 = jnp.float32


def reach_tables(offsets, steps):
    before, after = [], []
    for k in range(1, steps + 1):
        low = [h for h in range(offsets) if -((-REACH * h) // offsets) + BAND >= k]
        high = [h for h in range(offsets) if (REACH * h) // offsets + BAND >= k]
        if low:
            before.append(low[0])
        if high:
            after.append(high[0])
    return before, after


def segments(firsts, offsets):
    out, at = [], 0
    for first in firsts:
        out.append((at, offsets - first))
        at += offsets - first
    return out, at


def spec():
    return pl.BlockSpec(memory_space=pltpu.VMEM)


def params(mib):
    return pltpu.CompilerParams(vmem_limit_bytes=mib << 20)


def cost(flops, moved):
    return pl.CostEstimate(flops=flops, bytes_accessed=moved, transcendentals=0)


def struct(shape, kind=BF):
    return jax.ShapeDtypeStruct(shape, kind)


def swap_matrix(offsets, columns):
    n = offsets * columns
    row = lax.broadcasted_iota(jnp.int32, (n, n), 0)
    col = lax.broadcasted_iota(jnp.int32, (n, n), 1)
    hit = col == (row % offsets) * columns + row // offsets
    return jnp.where(hit, 1.0, 0.0).astype(BF)


def unswap_matrix(angles, columns):
    n = angles * columns
    row = lax.broadcasted_iota(jnp.int32, (n, n), 0)
    col = lax.broadcasted_iota(jnp.int32, (n, n), 1)
    hit = row == (col % angles) * columns + col // angles
    return jnp.where(hit, 1.0, 0.0).astype(BF)


def pack_half(before, after, half, image, up, down):
    h, z, _, y = image.shape
    width = y // HALVES
    lanes = slice(half * width, (half + 1) * width)
    for k, (at, n) in enumerate(segments(before, h)[0]):
        up[at : at + n] = image[h - n : h, z - 1 - k, :, lanes]
    for k, (at, n) in enumerate(segments(after, h)[0]):
        down[at : at + n] = image[h - n : h, k, :, lanes]


def pack_shapes(image, before, after):
    h, _, x, y = image.shape
    n_up, n_down = segments(before, h)[1], segments(after, h)[1]
    return struct((n_up, x, y // HALVES)), struct((n_down, x, y // HALVES))


def pack(image, before, after):
    return pl.pallas_call(
        functools.partial(pack_half, before, after, 0),
        out_shape=pack_shapes(image, before, after),
        in_specs=[spec()],
        out_specs=(spec(),) * 2,
        compiler_params=params(14),
        name="pack",
    )(image)


def prepare_kernel(before, after, image, coefficients, dip, slant, up, down, *outs):
    columns, (matrix, weights) = outs[:HALVES], outs[HALVES:]
    h, z, x, y = image.shape
    width = y // HALVES
    pack_half(before, after, 1, image, up, down)
    swap = swap_matrix(h, x)
    for level in range(z):
        plane = image[:, level].reshape(h * x, y)
        moved = jnp.dot(swap, plane, preferred_element_type=F32).astype(BF)
        for half in range(HALVES):
            for c in range(x):
                at = (c % 2) * width
                columns[half][c // 2, level * h : (level + 1) * h, at : at + width] = moved[
                    c * h : (c + 1) * h, half * width : (half + 1) * width
                ]
    steps, angles, _ = slant.shape
    zero = jnp.zeros((angles, h), BF)
    for j in range(ZB):
        for t in range((steps + ZB - 1) // 2):
            pair = [slant[d] if 0 <= d < steps else zero for d in (2 * t - j, 2 * t + 1 - j)]
            matrix[j * angles : (j + 1) * angles, 2 * t * h : 2 * (t + 1) * h] = jnp.concatenate(
                pair, axis=1
            )
    lane = lax.broadcasted_iota(jnp.int32, (z * x, y), 1)
    classes = dip[...]
    tests = [classes == q for q in range(1, coefficients.shape[0])]
    for t in range(weights.shape[1]):
        w = jnp.full((z * x, y), coefficients[0, t], F32)
        for q, test in enumerate(tests):
            w = jnp.where(test, coefficients[q + 1, t], w)
        shift = t % SIDES - RY
        if shift:
            w = pltpu.roll(w, shift % y, 1)
            w = jnp.where(lane < shift if shift > 0 else lane >= y + shift, 0.0, w)
        for half in range(HALVES):
            weights[half, t] = w[:, half * width : (half + 1) * width]


def prepare(image, coefficients, dip, slant, before, after):
    h, z, x, y = image.shape
    steps, angles, _ = slant.shape
    taps = coefficients.shape[1]
    return pl.pallas_call(
        functools.partial(prepare_kernel, before, after),
        out_shape=(
            *pack_shapes(image, before, after),
            *(struct((x // 2, z * h, 2 * y // HALVES)) for _ in range(HALVES)),
            struct((ZB * angles, (steps + ZB - 1) * h)),
            struct((HALVES, taps, z * x, y // HALVES), F32),
        ),
        in_specs=[spec(), pl.BlockSpec(memory_space=pltpu.SMEM), spec(), spec()],
        out_specs=(spec(),) * (4 + HALVES),
        compiler_params=params(14),
        cost_estimate=cost(2 * h * x * h * x * y * z, 8 << 20),
        name="prepare",
    )(image, coefficients, dip.reshape(z * x, y), slant)


def unpack(swap, source, pieces, starts, target):
    h, x = swap.shape[0] // source.shape[1], source.shape[1]
    width = source.shape[2]
    for k in range(0, len(pieces), 2):
        pair = [pieces[min(i, len(pieces) - 1)] for i in (k, k + 1)]
        planes = [source[at + n - h : at + n].reshape(h * x, width) for at, n in pair]
        moved = jnp.dot(swap, jnp.concatenate(planes, axis=1), preferred_element_type=F32)
        moved = moved.astype(BF)
        for i in range(min(2, len(pieces) - k)):
            rows = slice(starts[k + i] * h, (starts[k + i] + 1) * h)
            for c in range(x):
                at = (c % 2) * width
                target[c // 2, rows, at : at + width] = moved[
                    c * h : (c + 1) * h, i * width : (i + 1) * width
                ]


def gather_kernel(before, after, parts, matrix, up, down, mid, *rest):
    (own, *outs), (low, high) = rest[:-2], rest[-2:]
    x = up.shape[1]
    m = matrix.shape[0]
    h = matrix.shape[1] // (2 * R + ZB)
    tile = ZB * h
    swap = swap_matrix(h, x)
    unpack(swap, up, segments(before, h)[0], [R - 1 - k for k in range(R)], low)
    unpack(swap, down, segments(after, h)[0], list(range(R)), high)
    for k in range(len(after), R):
        high[:, k * h : (k + 1) * h, :] = jnp.zeros((x // 2, h, high.shape[2]), BF)
    zb = 0
    n_mid = mid.shape[1]
    for index, planes in enumerate(parts):
        for block in range(planes // ZB):
            n_low = low.shape[1] - zb * tile
            n_high = (zb + 1) * tile
            for c in range(x // 2):
                total = jnp.dot(
                    matrix[:, n_low : n_low + n_mid], mid[c], preferred_element_type=F32
                )
                total += jnp.dot(
                    matrix[:, :n_low], low[c, zb * tile :, :], preferred_element_type=F32
                )
                total += jnp.dot(
                    matrix[:, n_low + n_mid :], high[c, :n_high, :], preferred_element_type=F32
                )
                moved = total.astype(BF)
                width = moved.shape[1] // 2
                for side in range(2):
                    piece = moved[:, side * width : (side + 1) * width]
                    own[2 * c + side, zb * m : (zb + 1) * m, :] = piece
                    if outs:
                        outs[index][2 * c + side, block * m : (block + 1) * m, :] = piece
            zb += 1


def gather(matrix, up, down, mid, before, after, parts):
    pairs, rows, width = mid.shape
    per_plane = matrix.shape[0] // ZB
    sizes = (sum(parts), *(parts if len(parts) > 1 else ()))
    return pl.pallas_call(
        functools.partial(gather_kernel, before, after, parts),
        out_shape=tuple(struct((2 * pairs, n * per_plane, width // 2)) for n in sizes),
        in_specs=[spec()] * 4,
        out_specs=(spec(),) * len(sizes),
        scratch_shapes=[pltpu.VMEM((pairs, rows, width), BF)] * 2,
        compiler_params=params(14),
        cost_estimate=cost(2 * sum(parts) * per_plane * matrix.shape[1] * pairs * width, 6 << 20),
        name="gather",
    )(matrix, up, down, mid)


def mirrored(n, count, flip):
    return n + flip * (count - 1 - 2 * n)


def half_sums(weights, half, row, at, terms):
    sums = [None] * SIDES
    for source, c, step in terms:
        values = source[c, pl.ds(at, PART), :].astype(F32)
        for side in range(SIDES):
            w = weights[half, step * SIDES + side, pl.ds(row, 1), :]
            term = w * values
            sums[side] = term if sums[side] is None else sums[side] + term
    return sums


def spread(sums, half):
    zero = jnp.zeros_like(sums[0])
    total = None
    for side in range(SIDES):
        both = jnp.concatenate([sums[side], zero] if half == 0 else [zero, sums[side]], axis=1)
        if side != RY:
            both = pltpu.roll(both, (RY - side) % both.shape[1], 1)
        total = both if total is None else total + both
    return total


def beside_terms(source, n, column, x, flip):
    terms = []
    for m in range(n + 1):
        c = mirrored(m, x, flip)
        terms.append((source, c, c - column + 2 * RX * (1 - flip)))
    return terms


def early_kernel(half, angles, x, flip_ref, weights, own, near, *rest):
    totals = rest[-1]
    flip = flip_ref[0]

    def level(j, carry):
        for n in range(x):
            column = mirrored(n, x, flip)
            row = j * x + column
            terms = [(own, c, c - column + RX) for c in range(x)]
            terms += beside_terms(near, n, column, x, flip)
            for piece in range(angles // PART):
                at = pl.multiple_of(j * angles + piece * PART, PART)
                part = slice(piece * PART, (piece + 1) * PART)
                total = spread(half_sums(weights, half, row, at, terms), half)
                if len(rest) > 1:
                    total = total + rest[0][row, part, :]
                totals[row, part, :] = total
        return carry

    lax.fori_loop(0, totals.shape[0] // x, level, 0)


def scalar_spec():
    return pl.BlockSpec(memory_space=pltpu.SMEM)


def early(flip, weights, own, near, totals, half, angles, z, x, y):
    operands = [flip, weights, own, near] + ([] if totals is None else [totals])
    return pl.pallas_call(
        functools.partial(early_kernel, half, angles, x),
        out_shape=struct((z * x, angles, y), F32),
        in_specs=[scalar_spec()] + [spec()] * (len(operands) - 1),
        out_specs=spec(),
        compiler_params=params(14),
        cost_estimate=cost(weights.shape[1] * angles * z * x * y, 10 << 20),
        name="early",
    )(*operands)


def add_far_kernel(angles, x, flip_ref, weights, far, given, totals):
    flip = flip_ref[0]

    def level(j, carry):
        for n in range(x):
            column = mirrored(n, x, flip)
            row = j * x + column
            terms = beside_terms(far, n, column, x, flip)
            for piece in range(angles // PART):
                at = pl.multiple_of(j * angles + piece * PART, PART)
                part = slice(piece * PART, (piece + 1) * PART)
                sums = half_sums(weights, 0, row, at, terms)
                totals[row, part, :] = given[row, part, :] + spread(sums, 0)
        return carry

    lax.fori_loop(0, totals.shape[0] // x, level, 0)


def add_far(flip, weights, far, totals, angles, z, x, y):
    return pl.pallas_call(
        functools.partial(add_far_kernel, angles, x),
        out_shape=struct((z * x, angles, y), F32),
        in_specs=[scalar_spec()] + [spec()] * 3,
        out_specs=spec(),
        compiler_params=params(14),
        cost_estimate=cost(weights.shape[1] * angles * z * x * y // 4, 8 << 20),
        name="add_far",
    )(flip, weights, far, totals)


def finish_kernel(angles, x, first, flip_ref, weights, totals, far, *rest):
    out, scratch = rest[-2:]
    flip = flip_ref[0]
    unswap = unswap_matrix(angles, x)
    base = pl.program_id(0) * ZB

    def level(j, carry):
        for n in range(x):
            column = mirrored(n, x, flip)
            row = (first + base + j) * x + column
            terms = beside_terms(far, n, column, x, flip)
            for piece in range(angles // PART):
                at = pl.multiple_of((base + j) * angles + piece * PART, PART)
                part = slice(piece * PART, (piece + 1) * PART)
                sums = half_sums(weights, 1, row, at, terms)
                total = totals[row, part, :] + spread(sums, 1)
                to = pl.multiple_of(column * angles + piece * PART, PART)
                scratch[pl.ds(to, PART), :] = total.astype(BF)
        moved = jnp.dot(unswap, scratch[...], preferred_element_type=F32)
        out[:, j] = moved.astype(BF).reshape(angles, x, out.shape[3])
        return carry

    lax.fori_loop(0, ZB, level, 0)


def finish(flip, weights, totals, far, done, first, shape):
    angles, _, x, y = shape
    planes = far.shape[1] // angles
    in_specs = [scalar_spec()] + [spec()] * 3
    operands = [flip, weights, totals, far]
    aliases = {}
    if done is not None:
        in_specs.append(pl.BlockSpec(memory_space=pl.ANY))
        operands.append(done)
        aliases = {4: 0}
    return pl.pallas_call(
        functools.partial(finish_kernel, angles, x, first),
        grid=(planes // ZB,),
        out_shape=struct(shape),
        in_specs=in_specs,
        out_specs=pl.BlockSpec((angles, ZB, x, y), lambda i: (0, first // ZB + i, 0, 0)),
        scratch_shapes=[pltpu.VMEM((angles * x, y), BF)],
        input_output_aliases=aliases,
        compiler_params=params(14),
        cost_estimate=cost(weights.shape[1] * angles * planes * x * y // 4, 3 << 20),
        name="finish",
    )(*operands)


def slant_matrix_of(slant_taper, band_offsets, offset_count):
    offset_index = jnp.arange(offset_count, dtype=jnp.int32)
    depth_shift = jnp.floor_divide(band_offsets[:, None] * offset_index[None, :], offset_count)
    reach_index = jnp.arange(slant_taper.shape[2], dtype=jnp.int32) - R
    inside_band = jnp.abs(reach_index[None, None, :] - depth_shift[:, :, None]) <= BAND
    return jnp.where(inside_band, slant_taper, jnp.zeros_like(slant_taper))


def exchange(x_up, x_down, axis):
    count = lax.axis_size(axis)
    up = [(i, i + 1) for i in range(count - 1)]
    down = [(j, i) for i, j in up]
    return lax.ppermute(x_up, axis, up), lax.ppermute(x_down, axis, down)


def near_of(x, axis):
    count = lax.axis_size(axis)
    return lax.ppermute(x, axis, [(i, i ^ 1) for i in range(count)])


def far_of(x, axis):
    pairs = [(i, i + 1) for i in range(1, lax.axis_size(axis) - 1, 2)]
    return lax.ppermute(x, axis, pairs + [(j, i) for i, j in pairs])


def local(offset_image, dip_class, slant_taper, band_offsets, coefficients):
    h, z, x, y = offset_image.shape
    angles = slant_taper.shape[0]
    before, after = reach_tables(h, R)
    up_a, down_a = exchange(*pack(offset_image, before, after), "depth")
    slant = jnp.transpose(slant_matrix_of(slant_taper, band_offsets, h), (2, 0, 1))
    prepared = prepare(offset_image, coefficients, dip_class, slant, before, after)
    up_b, down_b, mid_a, mid_b, matrix, weights = prepared
    up_b, down_b = exchange(up_b, down_b, "depth")
    (own_a,) = gather(matrix, up_a, down_a, mid_a, before, after, (z,))
    far_a = far_of(own_a, "gx")
    near_a = near_of(own_a, "gx")
    own_b, *parts = gather(matrix, up_b, down_b, mid_b, before, after, LAST_PARTS)
    fars = []
    for part in parts:
        fars.append(far_of(part, "gx"))
    near_b = near_of(own_b, "gx")
    odd = (lax.axis_index("gx") % 2).astype(jnp.int32).reshape(1)
    totals = early(odd, weights, own_a, near_a, None, 0, angles, z, x, y)
    totals = early(odd, weights, own_b, near_b, totals, 1, angles, z, x, y)
    totals = add_far(1 - odd, weights, far_a, totals, angles, z, x, y)
    done, first = None, 0
    for far, planes in zip(fars, LAST_PARTS):
        done = finish(1 - odd, weights, totals, far, done, first, (angles, z, x, y))
        first += planes
    return done


def solution(mesh):
    return jax.shard_map(
        local,
        mesh=mesh,
        in_specs=(P(None, "depth", "gx", None), P("depth", "gx", None), P(), P(), P()),
        out_specs=P(None, "depth", "gx", None),
        check_vma=False,
    )
```

profile of v0, /device:TPU:137, one launch (start us, length us, event | category | flops | bytes accessed | tf_op | source)
XLA Modules:
  0.0 97.2 jit_solution(2611304628078269757)
XLA Ops:
  0.0 1.6 %copy-done = bf16[64,16,4,256]{3,2,1,0:T(4,128)(2,1)S(1)} copy-done((bf16[64,16,4,256]{3,2,1,0:T(4,128)(2,1)S(1)}, bf16[64,16,4,256]{3,2,1,0:T(4,128)(2,1)}, u32[]{:S(2)}) %copy-start) | copy-done | bytes 2097176
  1.6 1.4 %pack.1 = (bf16[600,4,128]{2,1,0:T(4,128)(2,1)}, bf16[538,4,128]{2,1,0:T(4,128)(2,1)}) custom-call(bf16[64,16,4,256]{3,2,1,0:T(4,128)(2,1)S(1)} %copy-done), custom_call_target="tpu_custom_call" | custom-call | tf_op jit(solution)/shard_map/pack/pallas_call | solution.py:94
  3.0 3.1 %collective-permute-start = (bf16[600,4,128]{2,1,0:T(4,128)(2,1)}, bf16[600,4,128]{2,1,0:T(4,128)(2,1)S(1)}, u32[]{:S(2)}, u32[]{:S(2)}) collective-permute-start(bf16[600,4,128]{2,1,0:T(4,128)(2,1)} %get-tuple-element.18), channel_id=1, source_target_pairs={{0,32},{32,64},{64,96},{96,128},{128,160},{160,192},{192,224},{1,3... | collective-permute-start | bytes 1843208 | tf_op jit(solution)/shard_map/ppermute | solution.py:396
  6.1 4.3 %collective-permute-start.1 = (bf16[538,4,128]{2,1,0:T(4,128)(2,1)}, bf16[538,4,128]{2,1,0:T(4,128)(2,1)}, u32[]{:S(2)}, u32[]{:S(2)}) collective-permute-start(bf16[538,4,128]{2,1,0:T(4,128)(2,1)} %get-tuple-element.19), channel_id=1, source_target_pairs={{32,0},{64,32},{96,64},{128,96},{160,128},{192,160},{224,192},{33,... | collective-permute-start | bytes 1652744 | tf_op jit(solution)/shard_map/ppermute | solution.py:396
  10.4 0.1 add_select_fusion
  10.5 0.3 fusion.1.slant
  10.9 0.0 copy-start.1
  11.0 1.6 %copy-done.1 = bf16[64,16,4,256]{3,2,1,0:T(4,128)(2,1)S(1)} copy-done((bf16[64,16,4,256]{3,2,1,0:T(4,128)(2,1)S(1)}, bf16[64,16,4,256]{3,2,1,0:T(4,128)(2,1)}, u32[]{:S(2)}) %copy-start.1) | copy-done | bytes 2097176
  12.5 2.6 %prepare.1 = (bf16[600,4,128]{2,1,0:T(4,128)(2,1)S(1)}, bf16[538,4,128]{2,1,0:T(4,128)(2,1)S(1)}, bf16[2,1024,256]{2,1,0:T(8,128)(2,1)S(1)}, bf16[2,1024,256]{2,...) custom-call(bf16[64,16,4,256]{3,2,1,0:T(4,128)(2,1)S(1)} %copy-done.1, ...), custom_call_target="tpu_custom_call" | custom-call | flops 536870912 | bytes 8388608 | tf_op jit(solution)/shard_map/prepare/pallas_call | solution.py:146
  15.1 1.9 %collective-permute-start.3 = (bf16[600,4,128]{2,1,0:T(4,128)(2,1)S(1)}, bf16[600,4,128]{2,1,0:T(4,128)(2,1)S(1)}, u32[]{:S(2)}, u32[]{:S(2)}) collective-permute-start(bf16[600,4,128]{2,1,0:T(4,128)(2,1)S(1)} %get-tuple-element.21), channel_id=1, source_target_pairs={{0,32},{32,64},{64,96},{96,128},{128,160},{160,192},{192,224},{1,3... | collective-permute-start | bytes 1843208 | tf_op jit(solution)/shard_map/ppermute | solution.py:396
  17.0 5.5 %collective-permute-start.4 = (bf16[538,4,128]{2,1,0:T(4,128)(2,1)S(1)}, bf16[538,4,128]{2,1,0:T(4,128)(2,1)S(1)}, u32[]{:S(2)}, u32[]{:S(2)}) collective-permute-start(bf16[538,4,128]{2,1,0:T(4,128)(2,1)S(1)} %get-tuple-element.22), channel_id=1, source_target_pairs={{32,0},{64,32},{96,64},{128,96},{160,128},{192,160},{224,192},{33,... | collective-permute-start | bytes 1652744 | tf_op jit(solution)/shard_map/ppermute | solution.py:396
  22.5 0.0 collective-permute-done.1.down
  22.5 0.0 collective-permute-done.up
  22.5 4.3 %gather.2.own = bf16[4,1024,128]{2,1,0:T(8,128)(2,1)S(1)} custom-call(bf16[256,2304]{1,0:T(8,128)(2,1)S(1)} %get-tuple-element.17.matrix, bf16[600,4,128]{2,1,0:T(4,128)(2,1)S(1)} %collective-permute-done.up, bf16[538,4,128]{2,1,0:T(4,128)(2,1)} %collective-permute-done.1.down, bf16[2,1024,256]{2,1,0:T(8,128)(2,1)S(1)} %get-tuple-element.20.mid), custom_call_target="tpu_custom_call" | custom-call | flops 2415919104 | bytes 6291456 | tf_op jit(solution)/shard_map/gather/pallas_call | solution.py:220
  26.8 2.2 %collective-permute-start.6 = (bf16[4,1024,128]{2,1,0:T(8,128)(2,1)S(1)}, bf16[4,1024,128]{2,1,0:T(8,128)(2,1)}, u32[]{:S(2)}, u32[]{:S(2)}) collective-permute-start(bf16[4,1024,128]{2,1,0:T(8,128)(2,1)S(1)} %gather.2.own), channel_id=1, source_target_pairs={{0,1},{1,0},{2,3},{3,2},{4,5},{5,4},{6,7},{7,6},{8,9},{9,8},{10,11... | collective-permute-start | bytes 3145736 | tf_op jit(solution)/shard_map/ppermute | solution.py:401
  29.0 4.4 %collective-permute-done.4.down = bf16[538,4,128]{2,1,0:T(4,128)(2,1)S(1)} collective-permute-done((bf16[538,4,128]{2,1,0:T(4,128)(2,1)S(1)}, bf16[538,4,128]{2,1,0:T(4,128)(2,1)S(1)}, u32[]{:S(2)}, u32[]{:S(2)}) %collective-permute-start.4) | collective-permute-done | bytes 550944 | tf_op jit(solution)/shard_map/ppermute | solution.py:396
  33.4 1.7 %collective-permute-done.3.up = bf16[600,4,128]{2,1,0:T(4,128)(2,1)S(1)} collective-permute-done((bf16[600,4,128]{2,1,0:T(4,128)(2,1)S(1)}, bf16[600,4,128]{2,1,0:T(4,128)(2,1)S(1)}, u32[]{:S(2)}, u32[]{:S(2)}) %collective-permute-start.3) | collective-permute-done | bytes 614432 | tf_op jit(solution)/shard_map/ppermute | solution.py:396
  35.1 4.4 %gather.3 = (bf16[4,1024,128]{2,1,0:T(8,128)(2,1)}, bf16[4,512,128]{2,1,0:T(8,128)(2,1)}, bf16[4,512,128]{2,1,0:T(8,128)(2,1)}) custom-call(bf16[256,2304]{1,0:T(8,128)(2,1)S(1)} %get-tuple-element.17.matrix, bf16[600,4,128]{2,1,0:T(4,128)(2,1)S(1)} %collective-permute-done.3.up, bf16[538,4,128]{2,1,0:T(4,128)(2,1)S(1)} %collective-permute-done.4.down, ...), custom_call_target="tpu_custom_call" | custom-call | flops 2415919104 | bytes 6291456 | tf_op jit(solution)/shard_map/gather/pallas_call | solution.py:220
  39.6 1.5 %collective-permute-start.5 = (bf16[4,1024,128]{2,1,0:T(8,128)(2,1)}, bf16[4,1024,128]{2,1,0:T(8,128)(2,1)}, u32[]{:S(2)}, u32[]{:S(2)}) collective-permute-start(bf16[4,1024,128]{2,1,0:T(8,128)(2,1)} %get-tuple-element.24.own), channel_id=1, source_target_pairs={{0,1},{1,0},{2,3},{3,2},{4,5},{5,4},{6,7},{7,6},{8,9},{9,8},{10,11... | collective-permute-start | bytes 3145736 | tf_op jit(solution)/shard_map/ppermute | solution.py:401
  41.1 3.8 %collective-permute-start.2 = (bf16[4,1024,128]{2,1,0:T(8,128)(2,1)S(1)}, bf16[4,1024,128]{2,1,0:T(8,128)(2,1)}, u32[]{:S(2)}, u32[]{:S(2)}) collective-permute-start(bf16[4,1024,128]{2,1,0:T(8,128)(2,1)S(1)} %gather.2.own), channel_id=1, source_target_pairs={{1,2},{3,4},{5,6},{7,8},{9,10},{11,12},{13,14},{15,16},{17,18},{19... | collective-permute-start | bytes 3145736 | tf_op jit(solution)/shard_map/ppermute | solution.py:406
  44.9 3.3 %collective-permute-start.8 = (bf16[4,512,128]{2,1,0:T(8,128)(2,1)}, bf16[4,512,128]{2,1,0:T(8,128)(2,1)S(1)}, u32[]{:S(2)}, u32[]{:S(2)}) collective-permute-start(bf16[4,512,128]{2,1,0:T(8,128)(2,1)} %get-tuple-element.26), channel_id=1, source_target_pairs={{1,2},{3,4},{5,6},{7,8},{9,10},{11,12},{13,14},{15,16},{17,18},{19... | collective-permute-start | bytes 1572872 | tf_op jit(solution)/shard_map/ppermute | solution.py:406
  48.2 3.8 %collective-permute-start.7 = (bf16[4,512,128]{2,1,0:T(8,128)(2,1)}, bf16[4,512,128]{2,1,0:T(8,128)(2,1)}, u32[]{:S(2)}, u32[]{:S(2)}) collective-permute-start(bf16[4,512,128]{2,1,0:T(8,128)(2,1)} %get-tuple-element.25), channel_id=1, source_target_pairs={{1,2},{3,4},{5,6},{7,8},{9,10},{11,12},{13,14},{15,16},{17,18},{19... | collective-permute-start | bytes 1572872 | tf_op jit(solution)/shard_map/ppermute | solution.py:406
  52.0 0.0 collective-permute-done.6.near
  52.0 4.6 %early.2.rest_0_ = f32[64,64,256]{2,1,0:T(8,128)S(1)} custom-call(s32[1]{0:T(128)} %bitcast.flip_ref, f32[2,27,64,128]{3,2,1,0:T(8,128)S(1)} %get-tuple-element.16.weights, bf16[4,1024,128]{2,1,0:T(8,128)(2,1)S(1)} %gather.2.own, bf16[4,1024,128]{2,1,0:T(8,128)(2,1)} %collective-permute-done.6.near), custom_call_target="tpu_custom_call" | custom-call | flops 28311552 | bytes 10485760 | tf_op jit(solution)/shard_map/early/pallas_call | solution.py:294
  56.6 0.0 collective-permute-done.5.near
  56.6 5.1 %early.3.given = f32[64,64,256]{2,1,0:T(8,128)S(1)} custom-call(s32[1]{0:T(128)} %bitcast.flip_ref, f32[2,27,64,128]{3,2,1,0:T(8,128)S(1)} %get-tuple-element.16.weights, bf16[4,1024,128]{2,1,0:T(8,128)(2,1)} %get-tuple-element.24.own, bf16[4,1024,128]{2,1,0:T(8,128)(2,1)} %collective-permute-done.5.near, f32[64,64,256]{2,1,0:T(8,128)S(1)} %early.2.rest_0_), custom_call_target="tpu_custom_call" | custom-call | flops 28311552 | bytes 10485760 | tf_op jit(solution)/shard_map/early/pallas_call | solution.py:294
  61.7 19.6 %collective-permute-done.2.far = bf16[4,1024,128]{2,1,0:T(8,128)(2,1)} collective-permute-done((bf16[4,1024,128]{2,1,0:T(8,128)(2,1)S(1)}, bf16[4,1024,128]{2,1,0:T(8,128)(2,1)}, u32[]{:S(2)}, u32[]{:S(2)}) %collective-permute-start.2) | collective-permute-done | bytes 1048608 | tf_op jit(solution)/shard_map/ppermute | solution.py:406
  81.3 3.5 %add_far.1.totals = f32[64,64,256]{2,1,0:T(8,128)S(1)} custom-call(s32[1]{0:T(128)S(6)} %sub.28.flip_ref, f32[2,27,64,128]{3,2,1,0:T(8,128)S(1)} %get-tuple-element.16.weights, bf16[4,1024,128]{2,1,0:T(8,128)(2,1)} %collective-permute-done.2.far, f32[64,64,256]{2,1,0:T(8,128)S(1)} %early.3.given), custom_call_target="tpu_custom_call" | custom-call | flops 7077888 | bytes 8388608 | tf_op jit(solution)/shard_map/add_far/pallas_call | solution.py:324
  84.8 2.0 %collective-permute-done.8.far = bf16[4,512,128]{2,1,0:T(8,128)(2,1)S(1)} collective-permute-done((bf16[4,512,128]{2,1,0:T(8,128)(2,1)}, bf16[4,512,128]{2,1,0:T(8,128)(2,1)S(1)}, u32[]{:S(2)}, u32[]{:S(2)}) %collective-permute-start.8) | collective-permute-done | bytes 524320 | tf_op jit(solution)/shard_map/ppermute | solution.py:406
  86.8 3.7 %finish.2.rest_0_ = bf16[64,16,4,256]{3,2,1,0:T(4,128)(2,1)} custom-call(s32[1]{0:T(128)S(6)} %sub.28.flip_ref, f32[2,27,64,128]{3,2,1,0:T(8,128)S(1)} %get-tuple-element.16.weights, f32[64,64,256]{2,1,0:T(8,128)S(1)} %add_far.1.totals, bf16[4,512,128]{2,1,0:T(8,128)(2,1)S(1)} %collective-permute-done.8.far), custom_call_target="tpu_custom_call" | custom-call | flops 3538944 | bytes 3145728 | tf_op jit(solution)/shard_map/finish/pallas_call | solution.py:370
  90.4 2.1 %collective-permute-done.7.far = bf16[4,512,128]{2,1,0:T(8,128)(2,1)} collective-permute-done((bf16[4,512,128]{2,1,0:T(8,128)(2,1)}, bf16[4,512,128]{2,1,0:T(8,128)(2,1)}, u32[]{:S(2)}, u32[]{:S(2)}) %collective-permute-start.7) | collective-permute-done | bytes 524320 | tf_op jit(solution)/shard_map/ppermute | solution.py:406
  92.5 4.7 %finish.3 = bf16[64,16,4,256]{3,2,1,0:T(4,128)(2,1)} custom-call(s32[1]{0:T(128)S(6)} %sub.28.flip_ref, f32[2,27,64,128]{3,2,1,0:T(8,128)S(1)} %get-tuple-element.16.weights, f32[64,64,256]{2,1,0:T(8,128)S(1)} %add_far.1.totals, bf16[4,512,128]{2,1,0:T(8,128)(2,1)} %collective-permute-done.7.far, ...), custom_call_target="tpu_custom_call", output_to_operand_aliasing={{}: (4, {})} | custom-call | flops 3538944 | bytes 3145728 | tf_op jit(solution)/shard_map/finish/pallas_call | solution.py:370
  (11 shorter events, 0.0 us)
Async XLA Ops:
  0.0 1.6 %copy-start = (bf16[64,16,4,256]{3,2,1,0:T(4,128)(2,1)S(1)}, bf16[64,16,4,256]{3,2,1,0:T(4,128)(2,1)}, u32[]{:S(2)}) copy-start(bf16[64,16,4,256]{3,2,1,0:T(4,128)(2,1)} %image.3) | copy-start | bytes 6291460
  1.6 8.8 %copy-start.5 = (s32[64]{0:T(128)S(1)}, s32[64]{0:T(128)}, u32[]{:S(2)}) copy-start(s32[64]{0:T(128)} %param.8) | copy-start | bytes 772
  1.6 8.9 %copy-start.3 = (bf16[64,64,33]{1,0,2:T(8,128)(2,1)S(1)}, bf16[64,64,33]{1,0,2:T(8,128)(2,1)}, u32[]{:S(2)}) copy-start(bf16[64,64,33]{1,0,2:T(8,128)(2,1)} %param.7) | copy-start | bytes 811012
  1.6 9.3 %copy-start.4 = (s32[16,4,256]{2,1,0:T(4,128)S(1)}, s32[16,4,256]{2,1,0:T(4,128)}, u32[]{:S(2)}) copy-start(s32[16,4,256]{2,1,0:T(4,128)} %param.6) | copy-start | bytes 196612
  1.6 9.3 %copy-start.2 = (f32[8,27]{1,0:T(8,128)S(1)}, f32[8,27]{1,0:T(8,128)}, u32[]{:S(2)}) copy-start(f32[8,27]{1,0:T(8,128)} %coefficients.1) | copy-start | bytes 2596
  3.0 19.5 %collective-permute-start = (bf16[600,4,128]{2,1,0:T(4,128)(2,1)}, bf16[600,4,128]{2,1,0:T(4,128)(2,1)S(1)}, u32[]{:S(2)}, u32[]{:S(2)}) collective-permute-start(bf16[600,4,128]{2,1,0:T(4,128)(2,1)} %get-tuple-element.18), channel_id=1, source_target_pairs={{0,32},{32,64},{64,96},{96,128},{128,160},{160,192},{192,224},{1,3... | collective-permute-start | bytes 1843208 | tf_op jit(solution)/shard_map/ppermute | solution.py:396
  6.1 16.4 %collective-permute-start.1 = (bf16[538,4,128]{2,1,0:T(4,128)(2,1)}, bf16[538,4,128]{2,1,0:T(4,128)(2,1)}, u32[]{:S(2)}, u32[]{:S(2)}) collective-permute-start(bf16[538,4,128]{2,1,0:T(4,128)(2,1)} %get-tuple-element.19), channel_id=1, source_target_pairs={{32,0},{64,32},{96,64},{128,96},{160,128},{192,160},{224,192},{33,... | collective-permute-start | bytes 1652744 | tf_op jit(solution)/shard_map/ppermute | solution.py:396
  10.9 1.6 %copy-start.1 = (bf16[64,16,4,256]{3,2,1,0:T(4,128)(2,1)S(1)}, bf16[64,16,4,256]{3,2,1,0:T(4,128)(2,1)}, u32[]{:S(2)}) copy-start(bf16[64,16,4,256]{3,2,1,0:T(4,128)(2,1)} %image.3) | copy-start | bytes 6291460
  15.1 20.0 %collective-permute-start.3 = (bf16[600,4,128]{2,1,0:T(4,128)(2,1)S(1)}, bf16[600,4,128]{2,1,0:T(4,128)(2,1)S(1)}, u32[]{:S(2)}, u32[]{:S(2)}) collective-permute-start(bf16[600,4,128]{2,1,0:T(4,128)(2,1)S(1)} %get-tuple-element.21), channel_id=1, source_target_pairs={{0,32},{32,64},{64,96},{96,128},{128,160},{160,192},{192,224},{1,3... | collective-permute-start | bytes 1843208 | tf_op jit(solution)/shard_map/ppermute | solution.py:396
  17.0 16.4 %collective-permute-start.4 = (bf16[538,4,128]{2,1,0:T(4,128)(2,1)S(1)}, bf16[538,4,128]{2,1,0:T(4,128)(2,1)S(1)}, u32[]{:S(2)}, u32[]{:S(2)}) collective-permute-start(bf16[538,4,128]{2,1,0:T(4,128)(2,1)S(1)} %get-tuple-element.22), channel_id=1, source_target_pairs={{32,0},{64,32},{96,64},{128,96},{160,128},{192,160},{224,192},{33,... | collective-permute-start | bytes 1652744 | tf_op jit(solution)/shard_map/ppermute | solution.py:396
  26.8 25.1 %collective-permute-start.6 = (bf16[4,1024,128]{2,1,0:T(8,128)(2,1)S(1)}, bf16[4,1024,128]{2,1,0:T(8,128)(2,1)}, u32[]{:S(2)}, u32[]{:S(2)}) collective-permute-start(bf16[4,1024,128]{2,1,0:T(8,128)(2,1)S(1)} %gather.2.own), channel_id=1, source_target_pairs={{0,1},{1,0},{2,3},{3,2},{4,5},{5,4},{6,7},{7,6},{8,9},{9,8},{10,11... | collective-permute-start | bytes 3145736 | tf_op jit(solution)/shard_map/ppermute | solution.py:401
  39.6 17.0 %collective-permute-start.5 = (bf16[4,1024,128]{2,1,0:T(8,128)(2,1)}, bf16[4,1024,128]{2,1,0:T(8,128)(2,1)}, u32[]{:S(2)}, u32[]{:S(2)}) collective-permute-start(bf16[4,1024,128]{2,1,0:T(8,128)(2,1)} %get-tuple-element.24.own), channel_id=1, source_target_pairs={{0,1},{1,0},{2,3},{3,2},{4,5},{5,4},{6,7},{7,6},{8,9},{9,8},{10,11... | collective-permute-start | bytes 3145736 | tf_op jit(solution)/shard_map/ppermute | solution.py:401
  41.1 40.2 %collective-permute-start.2 = (bf16[4,1024,128]{2,1,0:T(8,128)(2,1)S(1)}, bf16[4,1024,128]{2,1,0:T(8,128)(2,1)}, u32[]{:S(2)}, u32[]{:S(2)}) collective-permute-start(bf16[4,1024,128]{2,1,0:T(8,128)(2,1)S(1)} %gather.2.own), channel_id=1, source_target_pairs={{1,2},{3,4},{5,6},{7,8},{9,10},{11,12},{13,14},{15,16},{17,18},{19... | collective-permute-start | bytes 3145736 | tf_op jit(solution)/shard_map/ppermute | solution.py:406
  44.9 41.9 %collective-permute-start.8 = (bf16[4,512,128]{2,1,0:T(8,128)(2,1)}, bf16[4,512,128]{2,1,0:T(8,128)(2,1)S(1)}, u32[]{:S(2)}, u32[]{:S(2)}) collective-permute-start(bf16[4,512,128]{2,1,0:T(8,128)(2,1)} %get-tuple-element.26), channel_id=1, source_target_pairs={{1,2},{3,4},{5,6},{7,8},{9,10},{11,12},{13,14},{15,16},{17,18},{19... | collective-permute-start | bytes 1572872 | tf_op jit(solution)/shard_map/ppermute | solution.py:406
  48.2 44.4 %collective-permute-start.7 = (bf16[4,512,128]{2,1,0:T(8,128)(2,1)}, bf16[4,512,128]{2,1,0:T(8,128)(2,1)}, u32[]{:S(2)}, u32[]{:S(2)}) collective-permute-start(bf16[4,512,128]{2,1,0:T(8,128)(2,1)} %get-tuple-element.25), channel_id=1, source_target_pairs={{1,2},{3,4},{5,6},{7,8},{9,10},{11,12},{13,14},{15,16},{17,18},{19... | collective-permute-start | bytes 1572872 | tf_op jit(solution)/shard_map/ppermute | solution.py:406
where the time goes:
time: 98.2 us; the launch traced here: 97.2 us
  Pallas kernels  34.3 us (35%)
  waiting for transfers between devices  29.7 us (30%)
  starting transfers between devices  29.3 us (30%)
  local copies, waits for them, and re-layouts  3.22 us (3%)
    ppermute x3, waiting for transfers between devices, far_of(): return lax.ppermute(x, axis, pairs + [(j, i) for i, j in pairs])  23.6 us
    ppermute x4, starting transfers between devices, exchange(): return (lax.ppermute(x_up, axis, up), lax.ppermute(x_down, axis, down))  14.8 us
    ppermute x3, starting transfers between devices, far_of(): return lax.ppermute(x, axis, pairs + [(j, i) for i, j in pairs])  10.9 us
    pallas_call x2, Pallas kernels, early(): pl.pallas_call(functools.partial(early_kernel, half, angles, x), out_shap...  9.67 us
    pallas_call x2, Pallas kernels, gather(): pl.pallas_call(functools.partial(gather_kernel, before, after, parts), ou...  8.73 us
    pallas_call x2, Pallas kernels, finish(): pl.pallas_call(functools.partial(finish_kernel, angles, x, first), grid=(...  8.36 us
    ppermute x4, waiting for transfers between devices, exchange(): return (lax.ppermute(x_up, axis, up), lax.ppermute(x_down, axis, down))  6.12 us
    ppermute x2, starting transfers between devices, near_of(): return lax.ppermute(x, axis, [(i, i ^ 1) for i in range(count)])  3.69 us
  transfers between devices with their start and end apart: 9, of which 5 were waited for; matrix products, arithmetic and copies ran while one was open for 0% of the time, Pallas kernels for 29%

commit v1 on v0

--- a/solution.py
+++ b/solution.py
@@ -15,7 +15,7 @@
 REACH = R - BAND
 ZB = 4
 HALVES = 2
-LAST_PARTS = (8, 8)
+LAST_PARTS = (8, 4, 4)
 PART = 32
 SIDES = 2 * RY + 1
 BF = jnp.bfloat16
@@ -74,38 +74,49 @@
     return jnp.where(hit, 1.0, 0.0).astype(BF)
 
 
-def pack_half(before, after, half, image, up, down):
-    h, z, _, y = image.shape
-    width = y // HALVES
-    lanes = slice(half * width, (half + 1) * width)
+def pack_unit(before, after, image, lanes, columns, up, down):
+    h, z = image.shape[:2]
     for k, (at, n) in enumerate(segments(before, h)[0]):
-        up[at : at + n] = image[h - n : h, z - 1 - k, :, lanes]
+        up[at : at + n] = image[h - n : h, z - 1 - k, columns, lanes]
     for k, (at, n) in enumerate(segments(after, h)[0]):
-        down[at : at + n] = image[h - n : h, k, :, lanes]
-
-
-def pack_shapes(image, before, after):
-    h, _, x, y = image.shape
+        down[at : at + n] = image[h - n : h, k, columns, lanes]
+
+
+def pack_shapes(image, before, after, columns):
+    h, _, _, y = image.shape
     n_up, n_down = segments(before, h)[1], segments(after, h)[1]
-    return struct((n_up, x, y // HALVES)), struct((n_down, x, y // HALVES))
+    return struct((n_up, columns, y // HALVES)), struct((n_down, columns, y // HALVES))
+
+
+def pack_kernel(before, after, image, up, down, part, sem):
+    width = part.shape[3]
+    copy = pltpu.make_async_copy(image.at[:, :, :, pl.ds(0, width)], part, sem)
+    copy.start()
+    copy.wait()
+    columns = slice(0, part.shape[2] // 2)
+    pack_unit(before, after, part, slice(0, width), columns, up, down)
 
 
 def pack(image, before, after):
-    return pl.pallas_call(
-        functools.partial(pack_half, before, after, 0),
-        out_shape=pack_shapes(image, before, after),
-        in_specs=[spec()],
+    h, z, x, y = image.shape
+    return pl.pallas_call(
+        functools.partial(pack_kernel, before, after),
+        out_shape=pack_shapes(image, before, after, x // 2),
+        in_specs=[pl.BlockSpec(memory_space=pltpu.HBM)],
         out_specs=(spec(),) * 2,
-        compiler_params=params(14),
+        scratch_shapes=[pltpu.VMEM((h, z, x, y // HALVES), BF), pltpu.SemaphoreType.DMA],
+        compiler_params=params(62),
         name="pack",
     )(image)
 
 
-def prepare_kernel(before, after, image, coefficients, dip, slant, up, down, *outs):
-    columns, (matrix, weights) = outs[:HALVES], outs[HALVES:]
+def prepare_kernel(before, after, image, coefficients, dip, slant, *outs):
+    up_a, down_a, up_b, down_b = outs[:4]
+    columns, (matrix, weights) = outs[4 : 4 + HALVES], outs[4 + HALVES :]
     h, z, x, y = image.shape
     width = y // HALVES
-    pack_half(before, after, 1, image, up, down)
+    pack_unit(before, after, image, slice(0, width), slice(x // 2, x), up_a, down_a)
+    pack_unit(before, after, image, slice(width, y), slice(0, x), up_b, down_b)
     swap = swap_matrix(h, x)
     for level in range(z):
         plane = image[:, level].reshape(h * x, y)
@@ -146,13 +157,14 @@
     return pl.pallas_call(
         functools.partial(prepare_kernel, before, after),
         out_shape=(
-            *pack_shapes(image, before, after),
+            *pack_shapes(image, before, after, x // 2),
+            *pack_shapes(image, before, after, x),
             *(struct((x // 2, z * h, 2 * y // HALVES)) for _ in range(HALVES)),
             struct((ZB * angles, (steps + ZB - 1) * h)),
             struct((HALVES, taps, z * x, y // HALVES), F32),
         ),
         in_specs=[spec(), pl.BlockSpec(memory_space=pltpu.SMEM), spec(), spec()],
-        out_specs=(spec(),) * (4 + HALVES),
+        out_specs=(spec(),) * (6 + HALVES),
         compiler_params=params(14),
         cost_estimate=cost(2 * h * x * h * x * y * z, 8 << 20),
         name="prepare",
@@ -176,8 +188,9 @@
                 ]
 
 
-def gather_kernel(before, after, parts, matrix, up, down, mid, *rest):
-    (own, *outs), (low, high) = rest[:-2], rest[-2:]
+def gather_kernel(before, after, parts, first_pair, matrix, up, down, mid, *rest):
+    rest, (low, high) = rest[:-2], rest[-2:]
+    given, (own, *outs) = (rest[0], rest[1:]) if first_pair else (None, rest)
     x = up.shape[1]
     m = matrix.shape[0]
     h = matrix.shape[1] // (2 * R + ZB)
@@ -187,6 +200,8 @@
     unpack(swap, down, segments(after, h)[0], list(range(R)), high)
     for k in range(len(after), R):
         high[:, k * h : (k + 1) * h, :] = jnp.zeros((x // 2, h, high.shape[2]), BF)
+    if given is not None:
+        own[: 2 * first_pair] = given[...]
     zb = 0
     n_mid = mid.shape[1]
     for index, planes in enumerate(parts):
@@ -195,7 +210,7 @@
             n_high = (zb + 1) * tile
             for c in range(x // 2):
                 total = jnp.dot(
-                    matrix[:, n_low : n_low + n_mid], mid[c], preferred_element_type=F32
+                    matrix[:, n_low : n_low + n_mid], mid[first_pair + c], preferred_element_type=F32
                 )
                 total += jnp.dot(
                     matrix[:, :n_low], low[c, zb * tile :, :], preferred_element_type=F32
@@ -207,30 +222,36 @@
                 width = moved.shape[1] // 2
                 for side in range(2):
                     piece = moved[:, side * width : (side + 1) * width]
-                    own[2 * c + side, zb * m : (zb + 1) * m, :] = piece
+                    own[2 * (first_pair + c) + side, zb * m : (zb + 1) * m, :] = piece
                     if outs:
                         outs[index][2 * c + side, block * m : (block + 1) * m, :] = piece
             zb += 1
 
 
-def gather(matrix, up, down, mid, before, after, parts):
-    pairs, rows, width = mid.shape
+def gather(matrix, up, down, mid, before, after, parts, given=None):
+    rows, width = mid.shape[1:]
+    x, z = up.shape[1], sum(parts)
     per_plane = matrix.shape[0] // ZB
-    sizes = (sum(parts), *(parts if len(parts) > 1 else ()))
-    return pl.pallas_call(
-        functools.partial(gather_kernel, before, after, parts),
-        out_shape=tuple(struct((2 * pairs, n * per_plane, width // 2)) for n in sizes),
-        in_specs=[spec()] * 4,
-        out_specs=(spec(),) * len(sizes),
-        scratch_shapes=[pltpu.VMEM((pairs, rows, width), BF)] * 2,
+    first_pair = 0 if given is None else given.shape[0] // 2
+    shapes = [(2 * first_pair + x, z)]
+    if len(parts) > 1 or first_pair:
+        shapes += [(x, n) for n in parts]
+    operands = [matrix, up, down, mid] + ([] if given is None else [given])
+    return pl.pallas_call(
+        functools.partial(gather_kernel, before, after, parts, first_pair),
+        out_shape=tuple(struct((n, planes * per_plane, width // 2)) for n, planes in shapes),
+        in_specs=[spec()] * len(operands),
+        out_specs=(spec(),) * len(shapes),
+        scratch_shapes=[pltpu.VMEM((x // 2, rows, width), BF)] * 2,
         compiler_params=params(14),
-        cost_estimate=cost(2 * sum(parts) * per_plane * matrix.shape[1] * pairs * width, 6 << 20),
+        cost_estimate=cost(z * per_plane * matrix.shape[1] * x * width, 6 << 20),
         name="gather",
-    )(matrix, up, down, mid)
-
-
-def mirrored(n, count, flip):
-    return n + flip * (count - 1 - 2 * n)
+    )(*operands)
+
+
+def by_parity(flip_ref, body):
+    for value in range(2):
+        pl.when(flip_ref[0] == value)(functools.partial(body, value))
 
 
 def half_sums(weights, half, row, at, terms):
@@ -255,24 +276,24 @@
     return total
 
 
-def beside_terms(source, n, column, x, flip):
+def beside_terms(sources, column, x, flip):
     terms = []
-    for m in range(n + 1):
-        c = mirrored(m, x, flip)
-        terms.append((source, c, c - column + 2 * RX * (1 - flip)))
+    for c in range(x):
+        step = c - column + 2 * RX * (1 - flip)
+        if 0 <= step <= 2 * RX:
+            source = sources[c * len(sources) // x]
+            terms.append((source, c % source.shape[0], step))
     return terms
 
 
 def early_kernel(half, angles, x, flip_ref, weights, own, near, *rest):
     totals = rest[-1]
-    flip = flip_ref[0]
-
-    def level(j, carry):
-        for n in range(x):
-            column = mirrored(n, x, flip)
+
+    def level(flip, j, carry):
+        for column in range(x):
             row = j * x + column
             terms = [(own, c, c - column + RX) for c in range(x)]
-            terms += beside_terms(near, n, column, x, flip)
+            terms += beside_terms((near,), column, x, flip)
             for piece in range(angles // PART):
                 at = pl.multiple_of(j * angles + piece * PART, PART)
                 part = slice(piece * PART, (piece + 1) * PART)
@@ -282,7 +303,10 @@
                 totals[row, part, :] = total
         return carry
 
-    lax.fori_loop(0, totals.shape[0] // x, level, 0)
+    def run(flip):
+        lax.fori_loop(0, totals.shape[0] // x, functools.partial(level, flip), 0)
+
+    by_parity(flip_ref, run)
 
 
 def scalar_spec():
@@ -302,14 +326,11 @@
     )(*operands)
 
 
-def add_far_kernel(angles, x, flip_ref, weights, far, given, totals):
-    flip = flip_ref[0]
-
-    def level(j, carry):
-        for n in range(x):
-            column = mirrored(n, x, flip)
+def add_far_kernel(angles, x, flip_ref, weights, far_1, far_2, given, totals):
+    def level(flip, j, carry):
+        for column in range(x):
             row = j * x + column
-            terms = beside_terms(far, n, column, x, flip)
+            terms = beside_terms((far_1, far_2), column, x, flip)
             for piece in range(angles // PART):
                 at = pl.multiple_of(j * angles + piece * PART, PART)
                 part = slice(piece * PART, (piece + 1) * PART)
@@ -317,44 +338,48 @@
                 totals[row, part, :] = given[row, part, :] + spread(sums, 0)
         return carry
 
-    lax.fori_loop(0, totals.shape[0] // x, level, 0)
-
-
-def add_far(flip, weights, far, totals, angles, z, x, y):
+    def run(flip):
+        lax.fori_loop(0, totals.shape[0] // x, functools.partial(level, flip), 0)
+
+    by_parity(flip_ref, run)
+
+
+def add_far(flip, weights, far_1, far_2, totals, angles, z, x, y):
     return pl.pallas_call(
         functools.partial(add_far_kernel, angles, x),
         out_shape=struct((z * x, angles, y), F32),
-        in_specs=[scalar_spec()] + [spec()] * 3,
+        in_specs=[scalar_spec()] + [spec()] * 4,
         out_specs=spec(),
         compiler_params=params(14),
         cost_estimate=cost(weights.shape[1] * angles * z * x * y // 4, 8 << 20),
         name="add_far",
-    )(flip, weights, far, totals)
+    )(flip, weights, far_1, far_2, totals)
 
 
 def finish_kernel(angles, x, first, flip_ref, weights, totals, far, *rest):
     out, scratch = rest[-2:]
-    flip = flip_ref[0]
     unswap = unswap_matrix(angles, x)
     base = pl.program_id(0) * ZB
 
-    def level(j, carry):
-        for n in range(x):
-            column = mirrored(n, x, flip)
+    def level(flip, j, carry):
+        for column in range(x):
             row = (first + base + j) * x + column
-            terms = beside_terms(far, n, column, x, flip)
+            terms = beside_terms((far,), column, x, flip)
             for piece in range(angles // PART):
                 at = pl.multiple_of((base + j) * angles + piece * PART, PART)
                 part = slice(piece * PART, (piece + 1) * PART)
                 sums = half_sums(weights, 1, row, at, terms)
                 total = totals[row, part, :] + spread(sums, 1)
-                to = pl.multiple_of(column * angles + piece * PART, PART)
-                scratch[pl.ds(to, PART), :] = total.astype(BF)
+                to = column * angles + piece * PART
+                scratch[to : to + PART, :] = total.astype(BF)
         moved = jnp.dot(unswap, scratch[...], preferred_element_type=F32)
         out[:, j] = moved.astype(BF).reshape(angles, x, out.shape[3])
         return carry
 
-    lax.fori_loop(0, ZB, level, 0)
+    def run(flip):
+        lax.fori_loop(0, ZB, functools.partial(level, flip), 0)
+
+    by_parity(flip_ref, run)
 
 
 def finish(flip, weights, totals, far, done, first, shape):
@@ -393,7 +418,9 @@
     count = lax.axis_size(axis)
     up = [(i, i + 1) for i in range(count - 1)]
     down = [(j, i) for i, j in up]
-    return lax.ppermute(x_up, axis, up), lax.ppermute(x_down, axis, down)
+    from_up = lax.ppermute(x_up, axis, up)
+    from_down = lax.ppermute(x_down, axis, down)
+    return from_up, from_down
 
 
 def near_of(x, axis):
@@ -410,15 +437,18 @@
     h, z, x, y = offset_image.shape
     angles = slant_taper.shape[0]
     before, after = reach_tables(h, R)
-    up_a, down_a = exchange(*pack(offset_image, before, after), "depth")
+    halo_1 = exchange(*pack(offset_image, before, after), "depth")
     slant = jnp.transpose(slant_matrix_of(slant_taper, band_offsets, h), (2, 0, 1))
     prepared = prepare(offset_image, coefficients, dip_class, slant, before, after)
-    up_b, down_b, mid_a, mid_b, matrix, weights = prepared
-    up_b, down_b = exchange(up_b, down_b, "depth")
-    (own_a,) = gather(matrix, up_a, down_a, mid_a, before, after, (z,))
-    far_a = far_of(own_a, "gx")
+    mid_a, mid_b, matrix, weights = prepared[4:]
+    halo_2 = exchange(*prepared[:2], "depth")
+    halo_b = exchange(*prepared[2:4], "depth")
+    (own_1,) = gather(matrix, *halo_1, mid_a, before, after, (z,))
+    far_1 = far_of(own_1, "gx")
+    own_a, own_2 = gather(matrix, *halo_2, mid_a, before, after, (z,), own_1)
+    far_2 = far_of(own_2, "gx")
     near_a = near_of(own_a, "gx")
-    own_b, *parts = gather(matrix, up_b, down_b, mid_b, before, after, LAST_PARTS)
+    own_b, *parts = gather(matrix, *halo_b, mid_b, before, after, LAST_PARTS)
     fars = []
     for part in parts:
         fars.append(far_of(part, "gx"))
@@ -426,7 +456,7 @@
     odd = (lax.axis_index("gx") % 2).astype(jnp.int32).reshape(1)
     totals = early(odd, weights, own_a, near_a, None, 0, angles, z, x, y)
     totals = early(odd, weights, own_b, near_b, totals, 1, angles, z, x, y)
-    totals = add_far(1 - odd, weights, far_a, totals, angles, z, x, y)
+    totals = add_far(1 - odd, weights, far_1, far_2, totals, angles, z, x, y)
     done, first = None, 0
     for far, planes in zip(fars, LAST_PARTS):
         done = finish(1 - odd, weights, totals, far, done, first, (angles, z, x, y))

time: 98.2 us -> 112 us (1.14)
  starting transfers between devices: 29.3 us -> 41.6 us
  waiting for transfers between devices: 29.7 us -> 25.7 us
  Pallas kernels: 34.3 us -> 37 us
  local copies, waits for them, and re-layouts: 3.22 us -> 5.78 us
    ppermute x3 -> x5, waiting for transfers between devices: 23.6 us -> 13.6 us  [far_of(): return lax.ppermute(x, axis, pairs + [(j, i) for i, j in pairs])]
    ppermute x3 -> x5, starting transfers between devices: 10.9 us -> 18.7 us  [far_of(): return lax.ppermute(x, axis, pairs + [(j, i) for i, j in pairs])]
    ppermute x4 -> x6, starting transfers between devices: 14.8 us -> 21.1 us  [the longest x3 15.3 us: exchange(): from_down = lax.ppermute(x_down, axis, down)]
    ppermute x4 -> x6, waiting for transfers between devices: 6.12 us -> 12.1 us  [the longest x3 12.1 us: exchange(): from_up = lax.ppermute(x_up, axis, up)]
    pallas_call x3 -> x4, Pallas kernels: 10.1 us -> 13.1 us  [the longest x3 10.5 us: gather(): pl.pallas_call(functools.partial(gather_kernel, before, after, parts, fir...]
    pallas_call x2, Pallas kernels: 9.67 us -> 7.01 us  [early(): pl.pallas_call(functools.partial(early_kernel, half, angles, x), out_shap...]
    unnamed x12 -> x24, local copies, waits for them, and re-layouts: 3.19 us -> 5.76 us
    pallas_call x2 -> x3, Pallas kernels: 8.36 us -> 10.3 us  [finish(): pl.pallas_call(functools.partial(finish_kernel, angles, x, first), grid=(...]
  transfers between devices with their start and end apart: 9 -> 13, of which waited for: 5 -> 5; matrix products, arithmetic and copies ran while one was open for 0% -> 0% of each run, Pallas kernels for 29% -> 28%
where the time goes in v1:
time: 112 us; the launch traced here: 111 us
  starting transfers between devices  41.6 us (37%)
  Pallas kernels  37 us (33%)
  waiting for transfers between devices  25.7 us (23%)
  local copies, waits for them, and re-layouts  5.78 us (5%)
    ppermute x5, starting transfers between devices, far_of(): return lax.ppermute(x, axis, pairs + [(j, i) for i, j in pairs])  18.7 us
    ppermute x3, starting transfers between devices, exchange(): from_down = lax.ppermute(x_down, axis, down)  15.3 us
    ppermute x5, waiting for transfers between devices, far_of(): return lax.ppermute(x, axis, pairs + [(j, i) for i, j in pairs])  13.6 us
    ppermute x3, waiting for transfers between devices, exchange(): from_up = lax.ppermute(x_up, axis, up)  12.1 us
    pallas_call x3, Pallas kernels, gather(): pl.pallas_call(functools.partial(gather_kernel, before, after, parts, fir...  10.5 us
    pallas_call x3, Pallas kernels, finish(): pl.pallas_call(functools.partial(finish_kernel, angles, x, first), grid=(...  10.3 us
    pallas_call x2, Pallas kernels, early(): pl.pallas_call(functools.partial(early_kernel, half, angles, x), out_shap...  7.01 us
    ppermute x3, starting transfers between devices, exchange(): from_up = lax.ppermute(x_up, axis, up)  5.76 us
  transfers between devices with their start and end apart: 13, of which 5 were waited for; matrix products, arithmetic and copies ran while one was open for 0% of the time, Pallas kernels for 28%

profile of v1, /device:TPU:137, one launch (start us, length us, event | category | flops | bytes accessed | tf_op | source)
XLA Modules:
  0.0 110.9 jit_solution(767660835740955325)
XLA Ops:
  0.0 2.5 %pack.1 = (bf16[600,2,128]{2,1,0:T(2,128)(2,1)}, bf16[538,2,128]{2,1,0:T(2,128)(2,1)}) custom-call(bf16[64,16,4,256]{3,2,1,0:T(4,128)(2,1)} %image.3), custom_call_target="tpu_custom_call" | custom-call | tf_op jit(solution)/shard_map/pack/pallas_call | solution.py:102
  2.5 4.4 %collective-permute-start.1 = (bf16[538,2,128]{2,1,0:T(2,128)(2,1)}, bf16[538,2,128]{2,1,0:T(2,128)(2,1)S(1)}, u32[]{:S(2)}, u32[]{:S(2)}) collective-permute-start(bf16[538,2,128]{2,1,0:T(2,128)(2,1)} %get-tuple-element.24), channel_id=1, source_target_pairs={{32,0},{64,32},{96,64},{128,96},{160,128},{192,160},{224,192},{33,... | collective-permute-start | bytes 826376 | tf_op jit(solution)/shard_map/ppermute | solution.py:422
  7.5 1.6 %copy-done = bf16[64,16,4,256]{3,2,1,0:T(4,128)(2,1)S(1)} copy-done((bf16[64,16,4,256]{3,2,1,0:T(4,128)(2,1)S(1)}, bf16[64,16,4,256]{3,2,1,0:T(4,128)(2,1)}, u32[]{:S(2)}) %copy-start) | copy-done | bytes 2097176
  9.1 3.2 %prepare.1 = (bf16[600,2,128]{2,1,0:T(2,128)(2,1)S(1)}, bf16[538,2,128]{2,1,0:T(2,128)(2,1)S(1)}, bf16[600,4,128]{2,1,0:T(4,128)(2,1)S(1)}, bf16[538,4,128]{2,1,...) custom-call(bf16[64,16,4,256]{3,2,1,0:T(4,128)(2,1)S(1)} %copy-done,, ...), custom_call_target="tpu_custom_call" | custom-call | flops 536870912 | bytes 8388608 | tf_op jit(solution)/shard_map/prepare/pallas_call | solution.py:157
  12.3 1.9 %collective-permute-start.6 = (bf16[600,4,128]{2,1,0:T(4,128)(2,1)S(1)}, bf16[600,4,128]{2,1,0:T(4,128)(2,1)S(1)}, u32[]{:S(2)}, u32[]{:S(2)}) collective-permute-start(bf16[600,4,128]{2,1,0:T(4,128)(2,1)S(1)} %get-tuple-element.29), channel_id=1, source_target_pairs={{0,32},{32,64},{64,96},{96,128},{128,160},{160,192},{192,224},{1,3... | collective-permute-start | bytes 1843208 | tf_op jit(solution)/shard_map/ppermute | solution.py:421
  14.2 5.5 %collective-permute-start.7 = (bf16[538,4,128]{2,1,0:T(4,128)(2,1)S(1)}, bf16[538,4,128]{2,1,0:T(4,128)(2,1)S(1)}, u32[]{:S(2)}, u32[]{:S(2)}) collective-permute-start(bf16[538,4,128]{2,1,0:T(4,128)(2,1)S(1)} %get-tuple-element.30), channel_id=1, source_target_pairs={{32,0},{64,32},{96,64},{128,96},{160,128},{192,160},{224,192},{33,... | collective-permute-start | bytes 1652744 | tf_op jit(solution)/shard_map/ppermute | solution.py:422
  19.7 1.9 %collective-permute-start = (bf16[600,2,128]{2,1,0:T(2,128)(2,1)S(1)}, bf16[600,2,128]{2,1,0:T(2,128)(2,1)S(1)}, u32[]{:S(2)}, u32[]{:S(2)}) collective-permute-start(bf16[600,2,128]{2,1,0:T(2,128)(2,1)S(1)} %copy-done.11), channel_id=1, source_target_pairs={{0,32},{32,64},{64,96},{96,128},{128,160},{160,192},{192,224},{1,3... | collective-permute-start | bytes 921608 | tf_op jit(solution)/shard_map/ppermute | solution.py:421
  21.6 1.9 %collective-permute-start.3 = (bf16[600,2,128]{2,1,0:T(2,128)(2,1)S(1)}, bf16[600,2,128]{2,1,0:T(2,128)(2,1)S(1)}, u32[]{:S(2)}, u32[]{:S(2)}) collective-permute-start(bf16[600,2,128]{2,1,0:T(2,128)(2,1)S(1)} %get-tuple-element.26), channel_id=1, source_target_pairs={{0,32},{32,64},{64,96},{96,128},{128,160},{160,192},{192,224},{1,3... | collective-permute-start | bytes 921608 | tf_op jit(solution)/shard_map/ppermute | solution.py:421
  23.5 5.5 %collective-permute-start.4 = (bf16[538,2,128]{2,1,0:T(2,128)(2,1)S(1)}, bf16[538,2,128]{2,1,0:T(2,128)(2,1)S(1)}, u32[]{:S(2)}, u32[]{:S(2)}) collective-permute-start(bf16[538,2,128]{2,1,0:T(2,128)(2,1)S(1)} %get-tuple-element.27), channel_id=1, source_target_pairs={{32,0},{64,32},{96,64},{128,96},{160,128},{192,160},{224,192},{33,... | collective-permute-start | bytes 826376 | tf_op jit(solution)/shard_map/ppermute | solution.py:422
  29.0 8.3 %collective-permute-done.up = bf16[600,2,128]{2,1,0:T(2,128)(2,1)S(1)} collective-permute-done((bf16[600,2,128]{2,1,0:T(2,128)(2,1)S(1)}, bf16[600,2,128]{2,1,0:T(2,128)(2,1)S(1)}, u32[]{:S(2)}, u32[]{:S(2)}) %collective-permute-start) | collective-permute-done | bytes 307232 | tf_op jit(solution)/shard_map/ppermute | solution.py:421
  37.3 2.7 %gather.3.rest_0_ = bf16[2,1024,128]{2,1,0:T(8,128)(2,1)} custom-call(bf16[256,2304]{1,0:T(8,128)(2,1)S(1)} %get-tuple-element.22.matrix, bf16[600,2,128]{2,1,0:T(2,128)(2,1)S(1)} %collective-permute-done.up, bf16[538,2,128]{2,1,0:T(2,128)(2,1)S(1)} %collective-permute-done.1.down, bf16[2,1024,256]{2,1,0:T(8,128)(2,1)S(1)} %get-tuple-element.25.mid), custom_call_target="tpu_custom_call" | custom-call | flops 1207959552 | bytes 6291456 | tf_op jit(solution)/shard_map/gather/pallas_call | solution.py:240
  40.1 3.8 %collective-permute-done.3.up = bf16[600,2,128]{2,1,0:T(2,128)(2,1)S(1)} collective-permute-done((bf16[600,2,128]{2,1,0:T(2,128)(2,1)S(1)}, bf16[600,2,128]{2,1,0:T(2,128)(2,1)S(1)}, u32[]{:S(2)}, u32[]{:S(2)}) %collective-permute-start.3) | collective-permute-done | bytes 307232 | tf_op jit(solution)/shard_map/ppermute | solution.py:421
  43.9 3.8 %gather.4 = (bf16[4,1024,128]{2,1,0:T(8,128)(2,1)S(1)}, bf16[2,1024,128]{2,1,0:T(8,128)(2,1)}) custom-call(bf16[256,2304]{1,0:T(8,128)(2,1)S(1)} %get-tuple-element.22.matrix, bf16[600,2,128]{2,1,0:T(2,128)(2,1)S(1)} %collective-permute-done.3.up, bf16[538,2,128]{2,1,0:T(2,128)(2,1)S(1)} %collective-permute-done.4.down, ...), custom_call_target="tpu_custom_call" | custom-call | flops 1207959552 | bytes 6291456 | tf_op jit(solution)/shard_map/gather/pallas_call | solution.py:240
  47.7 1.8 %collective-permute-start.9 = (bf16[4,1024,128]{2,1,0:T(8,128)(2,1)S(1)}, bf16[4,1024,128]{2,1,0:T(8,128)(2,1)S(1)}, u32[]{:S(2)}, u32[]{:S(2)}) collective-permute-start(bf16[4,1024,128]{2,1,0:T(8,128)(2,1)S(1)} %get-tuple-element.33.own), channel_id=1, source_target_pairs={{0,1},{1,0},{2,3},{3,2},{4,5},{5,4},{6,7},{7,6},{8,9},{9,8},{10,11... | collective-permute-start | bytes 3145736 | tf_op jit(solution)/shard_map/ppermute | solution.py:428
  49.5 4.0 %gather.5 = (bf16[4,1024,128]{2,1,0:T(8,128)(2,1)S(1)}, bf16[4,512,128]{2,1,0:T(8,128)(2,1)}, bf16[4,256,128]{2,1,0:T(8,128)(2,1)}, bf16[4,256,128]{2,1,0:T(8,128)(2,1)}) custom-call(bf16[256,2304]{1,0:T(8,128)(2,1)S(1)} %get-tuple-element.22.matrix, bf16[600,4,128]{2,1,0:T(4,128)(2,1)S(1)} %collective-permute-done.6.up, ...), custom_call_target="tpu_custom_call" | custom-call | flops 2415919104 | bytes 6291456 | tf_op jit(solution)/shard_map/gather/pallas_call | solution.py:240
  53.5 1.0 copy-done.3
  54.5 4.6 %collective-permute-start.5 = (bf16[2,1024,128]{2,1,0:T(8,128)(2,1)}, bf16[2,1024,128]{2,1,0:T(8,128)(2,1)S(1)}, u32[]{:S(2)}, u32[]{:S(2)}) collective-permute-start(bf16[2,1024,128]{2,1,0:T(8,128)(2,1)} %get-tuple-element.28), channel_id=1, source_target_pairs={{1,2},{3,4},{5,6},{7,8},{9,10},{11,12},{13,14},{15,16},{17,18},{19... | collective-permute-start | bytes 1572872 | tf_op jit(solution)/shard_map/ppermute | solution.py:433
  59.1 2.5 %collective-permute-start.2 = (bf16[2,1024,128]{2,1,0:T(8,128)(2,1)}, bf16[2,1024,128]{2,1,0:T(8,128)(2,1)}, u32[]{:S(2)}, u32[]{:S(2)}) collective-permute-start(bf16[2,1024,128]{2,1,0:T(8,128)(2,1)} %gather.3.rest_0_), channel_id=1, source_target_pairs={{1,2},{3,4},{5,6},{7,8},{9,10},{11,12},{13,14},{15,16},{17,18},{19... | collective-permute-start | bytes 1572872 | tf_op jit(solution)/shard_map/ppermute | solution.py:433
  61.6 4.6 %collective-permute-start.12 = (bf16[4,512,128]{2,1,0:T(8,128)(2,1)}, bf16[4,512,128]{2,1,0:T(8,128)(2,1)}, u32[]{:S(2)}, u32[]{:S(2)}) collective-permute-start(bf16[4,512,128]{2,1,0:T(8,128)(2,1)} %get-tuple-element.36), channel_id=1, source_target_pairs={{1,2},{3,4},{5,6},{7,8},{9,10},{11,12},{13,14},{15,16},{17,18},{19... | collective-permute-start | bytes 1572872 | tf_op jit(solution)/shard_map/ppermute | solution.py:433
  66.2 1.0 copy-done.1
  67.2 2.5 %collective-permute-start.11 = (bf16[4,256,128]{2,1,0:T(8,128)(2,1)}, bf16[4,256,128]{2,1,0:T(8,128)(2,1)}, u32[]{:S(2)}, u32[]{:S(2)}) collective-permute-start(bf16[4,256,128]{2,1,0:T(8,128)(2,1)} %get-tuple-element.35), channel_id=1, source_target_pairs={{1,2},{3,4},{5,6},{7,8},{9,10},{11,12},{13,14},{15,16},{17,18},{19... | collective-permute-start | bytes 786440 | tf_op jit(solution)/shard_map/ppermute | solution.py:433
  70.6 4.6 %collective-permute-start.10 = (bf16[4,256,128]{2,1,0:T(8,128)(2,1)}, bf16[4,256,128]{2,1,0:T(8,128)(2,1)}, u32[]{:S(2)}, u32[]{:S(2)}) collective-permute-start(bf16[4,256,128]{2,1,0:T(8,128)(2,1)} %get-tuple-element.34), channel_id=1, source_target_pairs={{1,2},{3,4},{5,6},{7,8},{9,10},{11,12},{13,14},{15,16},{17,18},{19... | collective-permute-start | bytes 786440 | tf_op jit(solution)/shard_map/ppermute | solution.py:433
  75.2 1.2 %copy-done.2 = bf16[4,1024,128]{2,1,0:T(8,128)(2,1)S(1)} copy-done((bf16[4,1024,128]{2,1,0:T(8,128)(2,1)S(1)}, bf16[4,1024,128]{2,1,0:T(8,128)(2,1)}, u32[]{:S(2)}) %copy-start.2) | copy-done | bytes 1048600
  76.5 3.4 %early.2.rest_0_ = f32[64,64,256]{2,1,0:T(8,128)S(1)} custom-call(s32[1]{0:T(128)} %bitcast.flip_ref, f32[2,27,64,128]{3,2,1,0:T(8,128)S(1)} %get-tuple-element.21.weights, bf16[4,1024,128]{2,1,0:T(8,128)(2,1)S(1)} %get-tuple-element.33.own, bf16[4,1024,128]{2,1,0:T(8,128)(2,1)S(1)} %copy-done.2), custom_call_target="tpu_custom_call" | custom-call | flops 28311552 | bytes 10485760 | tf_op jit(solution)/shard_map/early/pallas_call | solution.py:318
  79.9 3.6 %early.3.given = f32[64,64,256]{2,1,0:T(8,128)S(1)} custom-call(s32[1]{0:T(128)} %bitcast.flip_ref, f32[2,27,64,128]{3,2,1,0:T(8,128)S(1)} %get-tuple-element.21.weights, bf16[4,1024,128]{2,1,0:T(8,128)(2,1)S(1)} %copy-done.4, bf16[4,1024,128]{2,1,0:T(8,128)(2,1)S(1)} %copy-done.6, f32[64,64,256]{2,1,0:T(8,128)S(1)} %early.2.rest_0_), custom_call_target="tpu_custom_call" | custom-call | flops 28311552 | bytes 10485760 | tf_op jit(solution)/shard_map/early/pallas_call | solution.py:318
  83.5 5.7 %collective-permute-done.5.far_2 = bf16[2,1024,128]{2,1,0:T(8,128)(2,1)S(1)} collective-permute-done((bf16[2,1024,128]{2,1,0:T(8,128)(2,1)}, bf16[2,1024,128]{2,1,0:T(8,128)(2,1)S(1)}, u32[]{:S(2)}, u32[]{:S(2)}) %collective-permute-start.5) | collective-permute-done | bytes 524320 | tf_op jit(solution)/shard_map/ppermute | solution.py:433
  89.2 5.7 %collective-permute-done.2.far_1 = bf16[2,1024,128]{2,1,0:T(8,128)(2,1)} collective-permute-done((bf16[2,1024,128]{2,1,0:T(8,128)(2,1)}, bf16[2,1024,128]{2,1,0:T(8,128)(2,1)}, u32[]{:S(2)}, u32[]{:S(2)}) %collective-permute-start.2) | collective-permute-done | bytes 524320 | tf_op jit(solution)/shard_map/ppermute | solution.py:433
  94.9 3.4 %add_far.1.totals = f32[64,64,256]{2,1,0:T(8,128)S(1)} custom-call(s32[1]{0:T(128)S(6)} %sub.16.flip_ref, f32[2,27,64,128]{3,2,1,0:T(8,128)S(1)} %get-tuple-element.21.weights, bf16[2,1024,128]{2,1,0:T(8,128)(2,1)} %collective-permute-done.2.far_1, bf16[2,1024,128]{2,1,0:T(8,128)(2,1)S(1)} %collective-permute-done.5.far_2, f32[64,64,256]{2,1,0:T(8,128)S(1)} %early.3.given), custom_call_target="tpu_custom_call" | custom-call | flops 7077888 | bytes 8388608 | tf_op jit(solution)/shard_map/add_far/pallas_call | solution.py:348
  98.3 2.2 %collective-permute-done.12.far = bf16[4,512,128]{2,1,0:T(8,128)(2,1)} collective-permute-done((bf16[4,512,128]{2,1,0:T(8,128)(2,1)}, bf16[4,512,128]{2,1,0:T(8,128)(2,1)}, u32[]{:S(2)}, u32[]{:S(2)}) %collective-permute-start.12) | collective-permute-done | bytes 524320 | tf_op jit(solution)/shard_map/ppermute | solution.py:433
  100.5 4.4 %finish.3.rest_0_ = bf16[64,16,4,256]{3,2,1,0:T(4,128)(2,1)} custom-call(s32[1]{0:T(128)S(6)} %sub.16.flip_ref, f32[2,27,64,128]{3,2,1,0:T(8,128)S(1)} %get-tuple-element.21.weights, f32[64,64,256]{2,1,0:T(8,128)S(1)} %add_far.1.totals, bf16[4,512,128]{2,1,0:T(8,128)(2,1)} %collective-permute-done.12.far), custom_call_target="tpu_custom_call" | custom-call | flops 3538944 | bytes 3145728 | tf_op jit(solution)/shard_map/finish/pallas_call | solution.py:395
  104.9 3.0 %finish.4.rest_0_ = bf16[64,16,4,256]{3,2,1,0:T(4,128)(2,1)} custom-call(s32[1]{0:T(128)S(6)} %sub.16.flip_ref, f32[2,27,64,128]{3,2,1,0:T(8,128)S(1)} %get-tuple-element.21.weights, f32[64,64,256]{2,1,0:T(8,128)S(1)} %add_far.1.totals, bf16[4,256,128]{2,1,0:T(8,128)(2,1)} %collective-permute-done.11.far, ...), custom_call_target="tpu_custom_call", output_to_operand_aliasing={{}: (4, {})} | custom-call | flops 1769472 | bytes 3145728 | tf_op jit(solution)/shard_map/finish/pallas_call | solution.py:395
  107.9 3.0 %finish.5 = bf16[64,16,4,256]{3,2,1,0:T(4,128)(2,1)} custom-call(s32[1]{0:T(128)S(6)} %sub.16.flip_ref, f32[2,27,64,128]{3,2,1,0:T(8,128)S(1)} %get-tuple-element.21.weights, f32[64,64,256]{2,1,0:T(8,128)S(1)} %add_far.1.totals, bf16[4,256,128]{2,1,0:T(8,128)(2,1)} %collective-permute-done.10.far, ...), custom_call_target="tpu_custom_call", output_to_operand_aliasing={{}: (4, {})} | custom-call | flops 1769472 | bytes 3145728 | tf_op jit(solution)/shard_map/finish/pallas_call | solution.py:395
  (33 shorter events, 1.5 us)
Async XLA Ops:
  0.0 7.0 %copy-start.10 = (s32[64]{0:T(128)S(1)}, s32[64]{0:T(128)}, u32[]{:S(2)}) copy-start(s32[64]{0:T(128)} %param.8) | copy-start | bytes 772
  0.0 7.1 %copy-start.9 = (s32[16,4,256]{2,1,0:T(4,128)S(1)}, s32[16,4,256]{2,1,0:T(4,128)}, u32[]{:S(2)}) copy-start(s32[16,4,256]{2,1,0:T(4,128)} %param.6) | copy-start | bytes 196612
  0.0 7.1 %copy-start.8 = (bf16[64,64,33]{1,0,2:T(8,128)(2,1)S(1)}, bf16[64,64,33]{1,0,2:T(8,128)(2,1)}, u32[]{:S(2)}) copy-start(bf16[64,64,33]{1,0,2:T(8,128)(2,1)} %param.7) | copy-start | bytes 811012
  0.0 7.5 %copy-start.7 = (f32[8,27]{1,0:T(8,128)S(1)}, f32[8,27]{1,0:T(8,128)}, u32[]{:S(2)}) copy-start(f32[8,27]{1,0:T(8,128)} %coefficients.1) | copy-start | bytes 2596
  2.5 17.1 %copy-start.11 = (bf16[600,2,128]{2,1,0:T(2,128)(2,1)S(1)}, bf16[600,2,128]{2,1,0:T(2,128)(2,1)}, u32[]{:S(2)}) copy-start(bf16[600,2,128]{2,1,0:T(2,128)(2,1)} %get-tuple-element.23) | copy-start | bytes 921604
  2.5 21.0 %collective-permute-start.1 = (bf16[538,2,128]{2,1,0:T(2,128)(2,1)}, bf16[538,2,128]{2,1,0:T(2,128)(2,1)S(1)}, u32[]{:S(2)}, u32[]{:S(2)}) collective-permute-start(bf16[538,2,128]{2,1,0:T(2,128)(2,1)} %get-tuple-element.24), channel_id=1, source_target_pairs={{32,0},{64,32},{96,64},{128,96},{160,128},{192,160},{224,192},{33,... | collective-permute-start | bytes 826376 | tf_op jit(solution)/shard_map/ppermute | solution.py:422
  7.5 1.6 %copy-start = (bf16[64,16,4,256]{3,2,1,0:T(4,128)(2,1)S(1)}, bf16[64,16,4,256]{3,2,1,0:T(4,128)(2,1)}, u32[]{:S(2)}) copy-start(bf16[64,16,4,256]{3,2,1,0:T(4,128)(2,1)} %image.3) | copy-start | bytes 6291460
  12.3 37.3 %collective-permute-start.6 = (bf16[600,4,128]{2,1,0:T(4,128)(2,1)S(1)}, bf16[600,4,128]{2,1,0:T(4,128)(2,1)S(1)}, u32[]{:S(2)}, u32[]{:S(2)}) collective-permute-start(bf16[600,4,128]{2,1,0:T(4,128)(2,1)S(1)} %get-tuple-element.29), channel_id=1, source_target_pairs={{0,32},{32,64},{64,96},{96,128},{128,160},{160,192},{192,224},{1,3... | collective-permute-start | bytes 1843208 | tf_op jit(solution)/shard_map/ppermute | solution.py:421
  14.2 35.3 %collective-permute-start.7 = (bf16[538,4,128]{2,1,0:T(4,128)(2,1)S(1)}, bf16[538,4,128]{2,1,0:T(4,128)(2,1)S(1)}, u32[]{:S(2)}, u32[]{:S(2)}) collective-permute-start(bf16[538,4,128]{2,1,0:T(4,128)(2,1)S(1)} %get-tuple-element.30), channel_id=1, source_target_pairs={{32,0},{64,32},{96,64},{128,96},{160,128},{192,160},{224,192},{33,... | collective-permute-start | bytes 1652744 | tf_op jit(solution)/shard_map/ppermute | solution.py:422
  19.7 17.6 %collective-permute-start = (bf16[600,2,128]{2,1,0:T(2,128)(2,1)S(1)}, bf16[600,2,128]{2,1,0:T(2,128)(2,1)S(1)}, u32[]{:S(2)}, u32[]{:S(2)}) collective-permute-start(bf16[600,2,128]{2,1,0:T(2,128)(2,1)S(1)} %copy-done.11), channel_id=1, source_target_pairs={{0,32},{32,64},{64,96},{96,128},{128,160},{160,192},{192,224},{1,3... | collective-permute-start | bytes 921608 | tf_op jit(solution)/shard_map/ppermute | solution.py:421
  21.6 22.3 %collective-permute-start.3 = (bf16[600,2,128]{2,1,0:T(2,128)(2,1)S(1)}, bf16[600,2,128]{2,1,0:T(2,128)(2,1)S(1)}, u32[]{:S(2)}, u32[]{:S(2)}) collective-permute-start(bf16[600,2,128]{2,1,0:T(2,128)(2,1)S(1)} %get-tuple-element.26), channel_id=1, source_target_pairs={{0,32},{32,64},{64,96},{96,128},{128,160},{160,192},{192,224},{1,3... | collective-permute-start | bytes 921608 | tf_op jit(solution)/shard_map/ppermute | solution.py:421
  23.5 16.5 %collective-permute-start.4 = (bf16[538,2,128]{2,1,0:T(2,128)(2,1)S(1)}, bf16[538,2,128]{2,1,0:T(2,128)(2,1)S(1)}, u32[]{:S(2)}, u32[]{:S(2)}) collective-permute-start(bf16[538,2,128]{2,1,0:T(2,128)(2,1)S(1)} %get-tuple-element.27), channel_id=1, source_target_pairs={{32,0},{64,32},{96,64},{128,96},{160,128},{192,160},{224,192},{33,... | collective-permute-start | bytes 826376 | tf_op jit(solution)/shard_map/ppermute | solution.py:422
  47.7 18.5 %collective-permute-start.9 = (bf16[4,1024,128]{2,1,0:T(8,128)(2,1)S(1)}, bf16[4,1024,128]{2,1,0:T(8,128)(2,1)S(1)}, u32[]{:S(2)}, u32[]{:S(2)}) collective-permute-start(bf16[4,1024,128]{2,1,0:T(8,128)(2,1)S(1)} %get-tuple-element.33.own), channel_id=1, source_target_pairs={{0,1},{1,0},{2,3},{3,2},{4,5},{5,4},{6,7},{7,6},{8,9},{9,8},{10,11... | collective-permute-start | bytes 3145736 | tf_op jit(solution)/shard_map/ppermute | solution.py:428
  53.5 16.1 %collective-permute-start.8 = (bf16[4,1024,128]{2,1,0:T(8,128)(2,1)S(1)}, bf16[4,1024,128]{2,1,0:T(8,128)(2,1)S(1)}, u32[]{:S(2)}, u32[]{:S(2)}) collective-permute-start(bf16[4,1024,128]{2,1,0:T(8,128)(2,1)S(1)} %get-tuple-element.32.own), channel_id=1, source_target_pairs={{0,1},{1,0},{2,3},{3,2},{4,5},{5,4},{6,7},{7,6},{8,9},{9,8},{10,11... | collective-permute-start | bytes 3145736 | tf_op jit(solution)/shard_map/ppermute | solution.py:428
  53.5 1.0 copy-start.3
  54.5 34.7 %collective-permute-start.5 = (bf16[2,1024,128]{2,1,0:T(8,128)(2,1)}, bf16[2,1024,128]{2,1,0:T(8,128)(2,1)S(1)}, u32[]{:S(2)}, u32[]{:S(2)}) collective-permute-start(bf16[2,1024,128]{2,1,0:T(8,128)(2,1)} %get-tuple-element.28), channel_id=1, source_target_pairs={{1,2},{3,4},{5,6},{7,8},{9,10},{11,12},{13,14},{15,16},{17,18},{19... | collective-permute-start | bytes 1572872 | tf_op jit(solution)/shard_map/ppermute | solution.py:433
  59.1 35.8 %collective-permute-start.2 = (bf16[2,1024,128]{2,1,0:T(8,128)(2,1)}, bf16[2,1024,128]{2,1,0:T(8,128)(2,1)}, u32[]{:S(2)}, u32[]{:S(2)}) collective-permute-start(bf16[2,1024,128]{2,1,0:T(8,128)(2,1)} %gather.3.rest_0_), channel_id=1, source_target_pairs={{1,2},{3,4},{5,6},{7,8},{9,10},{11,12},{13,14},{15,16},{17,18},{19... | collective-permute-start | bytes 1572872 | tf_op jit(solution)/shard_map/ppermute | solution.py:433
  61.6 38.9 %collective-permute-start.12 = (bf16[4,512,128]{2,1,0:T(8,128)(2,1)}, bf16[4,512,128]{2,1,0:T(8,128)(2,1)}, u32[]{:S(2)}, u32[]{:S(2)}) collective-permute-start(bf16[4,512,128]{2,1,0:T(8,128)(2,1)} %get-tuple-element.36), channel_id=1, source_target_pairs={{1,2},{3,4},{5,6},{7,8},{9,10},{11,12},{13,14},{15,16},{17,18},{19... | collective-permute-start | bytes 1572872 | tf_op jit(solution)/shard_map/ppermute | solution.py:433
  66.2 1.0 copy-start.1
  67.2 37.7 %collective-permute-start.11 = (bf16[4,256,128]{2,1,0:T(8,128)(2,1)}, bf16[4,256,128]{2,1,0:T(8,128)(2,1)}, u32[]{:S(2)}, u32[]{:S(2)}) collective-permute-start(bf16[4,256,128]{2,1,0:T(8,128)(2,1)} %get-tuple-element.35), channel_id=1, source_target_pairs={{1,2},{3,4},{5,6},{7,8},{9,10},{11,12},{13,14},{15,16},{17,18},{19... | collective-permute-start | bytes 786440 | tf_op jit(solution)/shard_map/ppermute | solution.py:433
  69.7 1.0 copy-start.5
  70.6 37.2 %collective-permute-start.10 = (bf16[4,256,128]{2,1,0:T(8,128)(2,1)}, bf16[4,256,128]{2,1,0:T(8,128)(2,1)}, u32[]{:S(2)}, u32[]{:S(2)}) collective-permute-start(bf16[4,256,128]{2,1,0:T(8,128)(2,1)} %get-tuple-element.34), channel_id=1, source_target_pairs={{1,2},{3,4},{5,6},{7,8},{9,10},{11,12},{13,14},{15,16},{17,18},{19... | collective-permute-start | bytes 786440 | tf_op jit(solution)/shard_map/ppermute | solution.py:433
  75.2 1.2 %copy-start.2 = (bf16[4,1024,128]{2,1,0:T(8,128)(2,1)S(1)}, bf16[4,1024,128]{2,1,0:T(8,128)(2,1)}, u32[]{:S(2)}) copy-start(bf16[4,1024,128]{2,1,0:T(8,128)(2,1)} %copy-done.1) | copy-start | bytes 3145732
  76.5 3.4 %copy-start.4 = (bf16[4,1024,128]{2,1,0:T(8,128)(2,1)S(1)}, bf16[4,1024,128]{2,1,0:T(8,128)(2,1)}, u32[]{:S(2)}) copy-start(bf16[4,1024,128]{2,1,0:T(8,128)(2,1)} %copy-done.3) | copy-start | bytes 3145732
  76.5 3.4 %copy-start.6 = (bf16[4,1024,128]{2,1,0:T(8,128)(2,1)S(1)}, bf16[4,1024,128]{2,1,0:T(8,128)(2,1)}, u32[]{:S(2)}) copy-start(bf16[4,1024,128]{2,1,0:T(8,128)(2,1)} %copy-done.5) | copy-start | bytes 3145732

commit v2 on v0

--- a/solution.py
+++ b/solution.py
@@ -75,8 +75,8 @@
 
 
 def pack_half(before, after, half, image, up, down):
-    h, z, _, y = image.shape
-    width = y // HALVES
+    h, z = image.shape[:2]
+    width = up.shape[2]
     lanes = slice(half * width, (half + 1) * width)
     for k, (at, n) in enumerate(segments(before, h)[0]):
         up[at : at + n] = image[h - n : h, z - 1 - k, :, lanes]
@@ -90,13 +90,22 @@
     return struct((n_up, x, y // HALVES)), struct((n_down, x, y // HALVES))
 
 
+def pack_kernel(before, after, image, up, down, part, sem):
+    copy = pltpu.make_async_copy(image.at[:, :, :, pl.ds(0, part.shape[3])], part, sem)
+    copy.start()
+    copy.wait()
+    pack_half(before, after, 0, part, up, down)
+
+
 def pack(image, before, after):
-    return pl.pallas_call(
-        functools.partial(pack_half, before, after, 0),
+    h, z, x, y = image.shape
+    return pl.pallas_call(
+        functools.partial(pack_kernel, before, after),
         out_shape=pack_shapes(image, before, after),
-        in_specs=[spec()],
+        in_specs=[pl.BlockSpec(memory_space=pltpu.HBM)],
         out_specs=(spec(),) * 2,
-        compiler_params=params(14),
+        scratch_shapes=[pltpu.VMEM((h, z, x, y // HALVES), BF), pltpu.SemaphoreType.DMA],
+        compiler_params=params(62),
         name="pack",
     )(image)
 
@@ -176,7 +185,33 @@
                 ]
 
 
-def gather_kernel(before, after, parts, matrix, up, down, mid, *rest):
+def partial_kernel(matrix, mid_a, mid_b, out_a, out_b):
+    h = matrix.shape[1] // (2 * R + ZB)
+    for mid, out in ((mid_a, out_a), (mid_b, out_b)):
+        n_mid = mid.shape[1]
+        for zb in range(out.shape[0]):
+            n_low = n_mid - zb * ZB * h
+            for c in range(mid.shape[0]):
+                out[zb, c] = jnp.dot(
+                    matrix[:, n_low : n_low + n_mid], mid[c], preferred_element_type=F32
+                )
+
+
+def own_part(matrix, mid_a, mid_b, z):
+    pairs, rows, width = mid_a.shape
+    m = matrix.shape[0]
+    return pl.pallas_call(
+        partial_kernel,
+        out_shape=(struct((z // ZB, pairs, m, width), F32),) * 2,
+        in_specs=[spec()] * 3,
+        out_specs=(spec(),) * 2,
+        compiler_params=params(14),
+        cost_estimate=cost(4 * (z // ZB) * m * rows * pairs * width, 9 << 20),
+        name="own_part",
+    )(matrix, mid_a, mid_b)
+
+
+def gather_kernel(before, after, parts, matrix, up, down, given, *rest):
     (own, *outs), (low, high) = rest[:-2], rest[-2:]
     x = up.shape[1]
     m = matrix.shape[0]
@@ -188,16 +223,13 @@
     for k in range(len(after), R):
         high[:, k * h : (k + 1) * h, :] = jnp.zeros((x // 2, h, high.shape[2]), BF)
     zb = 0
-    n_mid = mid.shape[1]
+    n_mid = matrix.shape[1] - ZB * h - low.shape[1]
     for index, planes in enumerate(parts):
         for block in range(planes // ZB):
             n_low = low.shape[1] - zb * tile
             n_high = (zb + 1) * tile
             for c in range(x // 2):
-                total = jnp.dot(
-                    matrix[:, n_low : n_low + n_mid], mid[c], preferred_element_type=F32
-                )
-                total += jnp.dot(
+                total = given[zb, c] + jnp.dot(
                     matrix[:, :n_low], low[c, zb * tile :, :], preferred_element_type=F32
                 )
                 total += jnp.dot(
@@ -213,8 +245,9 @@
             zb += 1
 
 
-def gather(matrix, up, down, mid, before, after, parts):
-    pairs, rows, width = mid.shape
+def gather(matrix, up, down, given, before, after, parts):
+    _, pairs, _, width = given.shape
+    rows = sum(parts) * (matrix.shape[1] // (2 * R + ZB))
     per_plane = matrix.shape[0] // ZB
     sizes = (sum(parts), *(parts if len(parts) > 1 else ()))
     return pl.pallas_call(
@@ -226,7 +259,7 @@
         compiler_params=params(14),
         cost_estimate=cost(2 * sum(parts) * per_plane * matrix.shape[1] * pairs * width, 6 << 20),
         name="gather",
-    )(matrix, up, down, mid)
+    )(matrix, up, down, given)
 
 
 def mirrored(n, count, flip):
@@ -393,7 +426,9 @@
     count = lax.axis_size(axis)
     up = [(i, i + 1) for i in range(count - 1)]
     down = [(j, i) for i, j in up]
-    return lax.ppermute(x_up, axis, up), lax.ppermute(x_down, axis, down)
+    from_up = lax.ppermute(x_up, axis, up)
+    from_down = lax.ppermute(x_down, axis, down)
+    return from_up, from_down
 
 
 def near_of(x, axis):
@@ -415,10 +450,11 @@
     prepared = prepare(offset_image, coefficients, dip_class, slant, before, after)
     up_b, down_b, mid_a, mid_b, matrix, weights = prepared
     up_b, down_b = exchange(up_b, down_b, "depth")
-    (own_a,) = gather(matrix, up_a, down_a, mid_a, before, after, (z,))
+    part_a, part_b = own_part(matrix, mid_a, mid_b, z)
+    (own_a,) = gather(matrix, up_a, down_a, part_a, before, after, (z,))
     far_a = far_of(own_a, "gx")
     near_a = near_of(own_a, "gx")
-    own_b, *parts = gather(matrix, up_b, down_b, mid_b, before, after, LAST_PARTS)
+    own_b, *parts = gather(matrix, up_b, down_b, part_b, before, after, LAST_PARTS)
     fars = []
     for part in parts:
         fars.append(far_of(part, "gx"))

time: 98.2 us -> 98 us (level)
  the two profiles are of different devices: /device:TPU:137 before, /device:TPU:135 now
where the time goes in v2:
time: 98 us; the launch traced here: 97.5 us
  Pallas kernels  35.8 us (37%)
  waiting for transfers between devices  30.2 us (31%)
  starting transfers between devices  28.1 us (29%)
  local copies, waits for them, and re-layouts  1.62 us (2%)
  other arithmetic  1.49 us (2%)
    ppermute x3, waiting for transfers between devices, far_of(): return lax.ppermute(x, axis, pairs + [(j, i) for i, j in pairs])  23.1 us
    ppermute x3, starting transfers between devices, far_of(): return lax.ppermute(x, axis, pairs + [(j, i) for i, j in pairs])  11.5 us
    pallas_call x2, Pallas kernels, early(): pl.pallas_call(functools.partial(early_kernel, half, angles, x), out_shap...  9.62 us
    ppermute x2, starting transfers between devices, exchange(): from_up = lax.ppermute(x_up, axis, up)  8.35 us
    pallas_call x2, Pallas kernels, finish(): pl.pallas_call(functools.partial(finish_kernel, angles, x, first), grid=(...  8.35 us
    ppermute x2, waiting for transfers between devices, exchange(): from_down = lax.ppermute(x_down, axis, down)  7.14 us
    pallas_call x2, Pallas kernels, gather(): pl.pallas_call(functools.partial(gather_kernel, before, after, parts), ou...  6.67 us
    ppermute x2, starting transfers between devices, near_of(): return lax.ppermute(x, axis, [(i, i ^ 1) for i in range(count)])  4.22 us
  transfers between devices with their start and end apart: 9, of which 4 were waited for; matrix products, arithmetic and copies ran while one was open for 2% of the time, Pallas kernels for 29%

profile of v2, /device:TPU:135, one launch (start us, length us, event | category | flops | bytes accessed | tf_op | source)
XLA Modules:
  0.0 97.5 jit_solution(7636072217412493393)
XLA Ops:
  0.0 2.7 %pack.1 = (bf16[600,4,128]{2,1,0:T(4,128)(2,1)}, bf16[538,4,128]{2,1,0:T(4,128)(2,1)}) custom-call(bf16[64,16,4,256]{3,2,1,0:T(4,128)(2,1)} %image.3), custom_call_target="tpu_custom_call" | custom-call | tf_op jit(solution)/shard_map/pack/pallas_call | solution.py:102
  2.7 3.1 %collective-permute-start = (bf16[600,4,128]{2,1,0:T(4,128)(2,1)}, bf16[600,4,128]{2,1,0:T(4,128)(2,1)S(1)}, u32[]{:S(2)}, u32[]{:S(2)}) collective-permute-start(bf16[600,4,128]{2,1,0:T(4,128)(2,1)} %get-tuple-element.20), channel_id=1, source_target_pairs={{0,32},{32,64},{64,96},{96,128},{128,160},{160,192},{192,224},{1,3... | collective-permute-start | bytes 1843208 | tf_op jit(solution)/shard_map/ppermute | solution.py:429
  5.8 2.2 %collective-permute-start.1 = (bf16[538,4,128]{2,1,0:T(4,128)(2,1)}, bf16[538,4,128]{2,1,0:T(4,128)(2,1)}, u32[]{:S(2)}, u32[]{:S(2)}) collective-permute-start(bf16[538,4,128]{2,1,0:T(4,128)(2,1)} %get-tuple-element.21), channel_id=1, source_target_pairs={{32,0},{64,32},{96,64},{128,96},{160,128},{192,160},{224,192},{33,... | collective-permute-start | bytes 1652744 | tf_op jit(solution)/shard_map/ppermute | solution.py:430
  8.0 0.1 add_select_fusion
  8.1 1.4 %fusion.1.slant = bf16[33,64,64]{2,1,0:T(8,128)(2,1)S(1)} fusion(bf16[64,64,33]{1,0,2:T(8,128)(2,1)} %param.7, s32[64,64]{1,0:T(8,128)S(1)} %add_select_fusion, s32[33]{0:T(128)S(1)} %iota_add_fusion), kind=kLoop, calls=%fused_computation.2 | loop fusion | flops 540672 | bytes 557188 | tf_op jit(solution)/shard_map/transpose | solution.py:449
  9.6 0.0 copy-start
  9.6 1.6 %copy-done = bf16[64,16,4,256]{3,2,1,0:T(4,128)(2,1)S(1)} copy-done((bf16[64,16,4,256]{3,2,1,0:T(4,128)(2,1)S(1)}, bf16[64,16,4,256]{3,2,1,0:T(4,128)(2,1)}, u32[]{:S(2)}) %copy-start) | copy-done | bytes 2097176
  11.2 2.6 %prepare.1 = (bf16[600,4,128]{2,1,0:T(4,128)(2,1)S(1)}, bf16[538,4,128]{2,1,0:T(4,128)(2,1)S(1)}, bf16[2,1024,256]{2,1,0:T(8,128)(2,1)S(1)}, bf16[2,1024,256]{2,...) custom-call(bf16[64,16,4,256]{3,2,1,0:T(4,128)(2,1)S(1)} %copy-done, ...), custom_call_target="tpu_custom_call" | custom-call | flops 536870912 | bytes 8388608 | tf_op jit(solution)/shard_map/prepare/pallas_call | solution.py:155
  13.8 5.2 %collective-permute-start.3 = (bf16[600,4,128]{2,1,0:T(4,128)(2,1)S(1)}, bf16[600,4,128]{2,1,0:T(4,128)(2,1)S(1)}, u32[]{:S(2)}, u32[]{:S(2)}) collective-permute-start(bf16[600,4,128]{2,1,0:T(4,128)(2,1)S(1)} %get-tuple-element.25), channel_id=1, source_target_pairs={{0,32},{32,64},{64,96},{96,128},{128,160},{160,192},{192,224},{1,3... | collective-permute-start | bytes 1843208 | tf_op jit(solution)/shard_map/ppermute | solution.py:429
  19.0 1.9 %collective-permute-start.4 = (bf16[538,4,128]{2,1,0:T(4,128)(2,1)S(1)}, bf16[538,4,128]{2,1,0:T(4,128)(2,1)S(1)}, u32[]{:S(2)}, u32[]{:S(2)}) collective-permute-start(bf16[538,4,128]{2,1,0:T(4,128)(2,1)S(1)} %get-tuple-element.26), channel_id=1, source_target_pairs={{32,0},{64,32},{96,64},{128,96},{160,128},{192,160},{224,192},{33,... | collective-permute-start | bytes 1652744 | tf_op jit(solution)/shard_map/ppermute | solution.py:430
  20.9 2.3 %own_part.1 = (f32[4,2,256,256]{3,2,1,0:T(8,128)S(1)}, f32[4,2,256,256]{3,2,1,0:T(8,128)S(1)}) custom-call(bf16[256,2304]{1,0:T(8,128)(2,1)S(1)} %get-tuple-element.19.matrix, bf16[2,1024,256]{2,1,0:T(8,128)(2,1)S(1)} %get-tuple-element.22.mid_a, bf16[2,1024,256]{2,1,0:T(8,128)(2,1)S(1)} %get-tuple-element.23.mid_b), custom_call_target="tpu_custom_call" | custom-call | flops 2147483648 | bytes 9437184 | tf_op jit(solution)/shard_map/own_part/pallas_call | solution.py:203
  23.3 0.0 collective-permute-done.1.down
  23.3 0.0 collective-permute-done.up
  23.3 3.3 %gather.2.own = bf16[4,1024,128]{2,1,0:T(8,128)(2,1)S(1)} custom-call(bf16[256,2304]{1,0:T(8,128)(2,1)S(1)} %get-tuple-element.19.matrix, bf16[600,4,128]{2,1,0:T(4,128)(2,1)S(1)} %collective-permute-done.up, bf16[538,4,128]{2,1,0:T(4,128)(2,1)} %collective-permute-done.1.down, f32[4,2,256,256]{3,2,1,0:T(8,128)S(1)} %get-tuple-element.24.given), custom_call_target="tpu_custom_call" | custom-call | flops 2415919104 | bytes 6291456 | tf_op jit(solution)/shard_map/gather/pallas_call | solution.py:253
  26.6 1.8 %collective-permute-start.6 = (bf16[4,1024,128]{2,1,0:T(8,128)(2,1)S(1)}, bf16[4,1024,128]{2,1,0:T(8,128)(2,1)}, u32[]{:S(2)}, u32[]{:S(2)}) collective-permute-start(bf16[4,1024,128]{2,1,0:T(8,128)(2,1)S(1)} %gather.2.own), channel_id=1, source_target_pairs={{0,1},{1,0},{2,3},{3,2},{4,5},{5,4},{6,7},{7,6},{8,9},{9,8},{10,11... | collective-permute-start | bytes 3145736 | tf_op jit(solution)/shard_map/ppermute | solution.py:436
  28.4 7.1 %collective-permute-done.4.down = bf16[538,4,128]{2,1,0:T(4,128)(2,1)S(1)} collective-permute-done((bf16[538,4,128]{2,1,0:T(4,128)(2,1)S(1)}, bf16[538,4,128]{2,1,0:T(4,128)(2,1)S(1)}, u32[]{:S(2)}, u32[]{:S(2)}) %collective-permute-start.4) | collective-permute-done | bytes 550944 | tf_op jit(solution)/shard_map/ppermute | solution.py:430
  35.5 0.0 collective-permute-done.3.up
  35.5 3.4 %gather.3 = (bf16[4,1024,128]{2,1,0:T(8,128)(2,1)}, bf16[4,512,128]{2,1,0:T(8,128)(2,1)}, bf16[4,512,128]{2,1,0:T(8,128)(2,1)}) custom-call(bf16[256,2304]{1,0:T(8,128)(2,1)S(1)} %get-tuple-element.19.matrix, bf16[600,4,128]{2,1,0:T(4,128)(2,1)S(1)} %collective-permute-done.3.up, bf16[538,4,128]{2,1,0:T(4,128)(2,1)S(1)} %collective-permute-done.4.down, ...), custom_call_target="tpu_custom_call" | custom-call | flops 2415919104 | bytes 6291456 | tf_op jit(solution)/shard_map/gather/pallas_call | solution.py:253
  39.0 2.4 %collective-permute-start.5 = (bf16[4,1024,128]{2,1,0:T(8,128)(2,1)}, bf16[4,1024,128]{2,1,0:T(8,128)(2,1)}, u32[]{:S(2)}, u32[]{:S(2)}) collective-permute-start(bf16[4,1024,128]{2,1,0:T(8,128)(2,1)} %get-tuple-element.28.own), channel_id=1, source_target_pairs={{0,1},{1,0},{2,3},{3,2},{4,5},{5,4},{6,7},{7,6},{8,9},{9,8},{10,11... | collective-permute-start | bytes 3145736 | tf_op jit(solution)/shard_map/ppermute | solution.py:436
  41.3 4.4 %collective-permute-start.2 = (bf16[4,1024,128]{2,1,0:T(8,128)(2,1)S(1)}, bf16[4,1024,128]{2,1,0:T(8,128)(2,1)}, u32[]{:S(2)}, u32[]{:S(2)}) collective-permute-start(bf16[4,1024,128]{2,1,0:T(8,128)(2,1)S(1)} %gather.2.own), channel_id=1, source_target_pairs={{1,2},{3,4},{5,6},{7,8},{9,10},{11,12},{13,14},{15,16},{17,18},{19... | collective-permute-start | bytes 3145736 | tf_op jit(solution)/shard_map/ppermute | solution.py:441
  45.7 2.7 %collective-permute-start.8 = (bf16[4,512,128]{2,1,0:T(8,128)(2,1)}, bf16[4,512,128]{2,1,0:T(8,128)(2,1)S(1)}, u32[]{:S(2)}, u32[]{:S(2)}) collective-permute-start(bf16[4,512,128]{2,1,0:T(8,128)(2,1)} %get-tuple-element.30), channel_id=1, source_target_pairs={{1,2},{3,4},{5,6},{7,8},{9,10},{11,12},{13,14},{15,16},{17,18},{19... | collective-permute-start | bytes 1572872 | tf_op jit(solution)/shard_map/ppermute | solution.py:441
  48.4 4.4 %collective-permute-start.7 = (bf16[4,512,128]{2,1,0:T(8,128)(2,1)}, bf16[4,512,128]{2,1,0:T(8,128)(2,1)}, u32[]{:S(2)}, u32[]{:S(2)}) collective-permute-start(bf16[4,512,128]{2,1,0:T(8,128)(2,1)} %get-tuple-element.29), channel_id=1, source_target_pairs={{1,2},{3,4},{5,6},{7,8},{9,10},{11,12},{13,14},{15,16},{17,18},{19... | collective-permute-start | bytes 1572872 | tf_op jit(solution)/shard_map/ppermute | solution.py:441
  52.8 0.0 collective-permute-done.6.near
  52.8 4.6 %early.2.rest_0_ = f32[64,64,256]{2,1,0:T(8,128)S(1)} custom-call(s32[1]{0:T(128)} %bitcast.flip_ref, f32[2,27,64,128]{3,2,1,0:T(8,128)S(1)} %get-tuple-element.18.weights, bf16[4,1024,128]{2,1,0:T(8,128)(2,1)S(1)} %gather.2.own, bf16[4,1024,128]{2,1,0:T(8,128)(2,1)} %collective-permute-done.6.near), custom_call_target="tpu_custom_call" | custom-call | flops 28311552 | bytes 10485760 | tf_op jit(solution)/shard_map/early/pallas_call | solution.py:327
  57.4 0.0 collective-permute-done.5.near
  57.5 5.0 %early.3.given = f32[64,64,256]{2,1,0:T(8,128)S(1)} custom-call(s32[1]{0:T(128)} %bitcast.flip_ref, f32[2,27,64,128]{3,2,1,0:T(8,128)S(1)} %get-tuple-element.18.weights, bf16[4,1024,128]{2,1,0:T(8,128)(2,1)} %get-tuple-element.28.own, bf16[4,1024,128]{2,1,0:T(8,128)(2,1)} %collective-permute-done.5.near, f32[64,64,256]{2,1,0:T(8,128)S(1)} %early.2.rest_0_), custom_call_target="tpu_custom_call" | custom-call | flops 28311552 | bytes 10485760 | tf_op jit(solution)/shard_map/early/pallas_call | solution.py:327
  62.5 19.0 %collective-permute-done.2.far = bf16[4,1024,128]{2,1,0:T(8,128)(2,1)} collective-permute-done((bf16[4,1024,128]{2,1,0:T(8,128)(2,1)S(1)}, bf16[4,1024,128]{2,1,0:T(8,128)(2,1)}, u32[]{:S(2)}, u32[]{:S(2)}) %collective-permute-start.2) | collective-permute-done | bytes 1048608 | tf_op jit(solution)/shard_map/ppermute | solution.py:441
  81.5 3.5 %add_far.1.totals = f32[64,64,256]{2,1,0:T(8,128)S(1)} custom-call(s32[1]{0:T(128)S(6)} %sub.28.flip_ref, f32[2,27,64,128]{3,2,1,0:T(8,128)S(1)} %get-tuple-element.18.weights, bf16[4,1024,128]{2,1,0:T(8,128)(2,1)} %collective-permute-done.2.far, f32[64,64,256]{2,1,0:T(8,128)S(1)} %early.3.given), custom_call_target="tpu_custom_call" | custom-call | flops 7077888 | bytes 8388608 | tf_op jit(solution)/shard_map/add_far/pallas_call | solution.py:357
  85.1 2.0 %collective-permute-done.8.far = bf16[4,512,128]{2,1,0:T(8,128)(2,1)S(1)} collective-permute-done((bf16[4,512,128]{2,1,0:T(8,128)(2,1)}, bf16[4,512,128]{2,1,0:T(8,128)(2,1)S(1)}, u32[]{:S(2)}, u32[]{:S(2)}) %collective-permute-start.8) | collective-permute-done | bytes 524320 | tf_op jit(solution)/shard_map/ppermute | solution.py:441
  87.0 3.6 %finish.2.rest_0_ = bf16[64,16,4,256]{3,2,1,0:T(4,128)(2,1)} custom-call(s32[1]{0:T(128)S(6)} %sub.28.flip_ref, f32[2,27,64,128]{3,2,1,0:T(8,128)S(1)} %get-tuple-element.18.weights, f32[64,64,256]{2,1,0:T(8,128)S(1)} %add_far.1.totals, bf16[4,512,128]{2,1,0:T(8,128)(2,1)S(1)} %collective-permute-done.8.far), custom_call_target="tpu_custom_call" | custom-call | flops 3538944 | bytes 3145728 | tf_op jit(solution)/shard_map/finish/pallas_call | solution.py:403
  90.7 2.1 %collective-permute-done.7.far = bf16[4,512,128]{2,1,0:T(8,128)(2,1)} collective-permute-done((bf16[4,512,128]{2,1,0:T(8,128)(2,1)}, bf16[4,512,128]{2,1,0:T(8,128)(2,1)}, u32[]{:S(2)}, u32[]{:S(2)}) %collective-permute-start.7) | collective-permute-done | bytes 524320 | tf_op jit(solution)/shard_map/ppermute | solution.py:441
  92.8 4.7 %finish.3 = bf16[64,16,4,256]{3,2,1,0:T(4,128)(2,1)} custom-call(s32[1]{0:T(128)S(6)} %sub.28.flip_ref, f32[2,27,64,128]{3,2,1,0:T(8,128)S(1)} %get-tuple-element.18.weights, f32[64,64,256]{2,1,0:T(8,128)S(1)} %add_far.1.totals, bf16[4,512,128]{2,1,0:T(8,128)(2,1)} %collective-permute-done.7.far, ...), custom_call_target="tpu_custom_call", output_to_operand_aliasing={{}: (4, {})} | custom-call | flops 3538944 | bytes 3145728 | tf_op jit(solution)/shard_map/finish/pallas_call | solution.py:403
  (8 shorter events, 0.0 us)
Async XLA Ops:
  0.0 8.0 %copy-start.3 = (s32[64]{0:T(128)S(1)}, s32[64]{0:T(128)}, u32[]{:S(2)}) copy-start(s32[64]{0:T(128)} %param.8) | copy-start | bytes 772
  0.0 9.5 %copy-start.2 = (s32[16,4,256]{2,1,0:T(4,128)S(1)}, s32[16,4,256]{2,1,0:T(4,128)}, u32[]{:S(2)}) copy-start(s32[16,4,256]{2,1,0:T(4,128)} %param.6) | copy-start | bytes 196612
  0.0 9.6 %copy-start.1 = (f32[8,27]{1,0:T(8,128)S(1)}, f32[8,27]{1,0:T(8,128)}, u32[]{:S(2)}) copy-start(f32[8,27]{1,0:T(8,128)} %coefficients.1) | copy-start | bytes 2596
  2.7 20.6 %collective-permute-start = (bf16[600,4,128]{2,1,0:T(4,128)(2,1)}, bf16[600,4,128]{2,1,0:T(4,128)(2,1)S(1)}, u32[]{:S(2)}, u32[]{:S(2)}) collective-permute-start(bf16[600,4,128]{2,1,0:T(4,128)(2,1)} %get-tuple-element.20), channel_id=1, source_target_pairs={{0,32},{32,64},{64,96},{96,128},{128,160},{160,192},{192,224},{1,3... | collective-permute-start | bytes 1843208 | tf_op jit(solution)/shard_map/ppermute | solution.py:429
  5.8 17.5 %collective-permute-start.1 = (bf16[538,4,128]{2,1,0:T(4,128)(2,1)}, bf16[538,4,128]{2,1,0:T(4,128)(2,1)}, u32[]{:S(2)}, u32[]{:S(2)}) collective-permute-start(bf16[538,4,128]{2,1,0:T(4,128)(2,1)} %get-tuple-element.21), channel_id=1, source_target_pairs={{32,0},{64,32},{96,64},{128,96},{160,128},{192,160},{224,192},{33,... | collective-permute-start | bytes 1652744 | tf_op jit(solution)/shard_map/ppermute | solution.py:430
  9.6 1.6 %copy-start = (bf16[64,16,4,256]{3,2,1,0:T(4,128)(2,1)S(1)}, bf16[64,16,4,256]{3,2,1,0:T(4,128)(2,1)}, u32[]{:S(2)}) copy-start(bf16[64,16,4,256]{3,2,1,0:T(4,128)(2,1)} %image.3) | copy-start | bytes 6291460
  13.8 21.8 %collective-permute-start.3 = (bf16[600,4,128]{2,1,0:T(4,128)(2,1)S(1)}, bf16[600,4,128]{2,1,0:T(4,128)(2,1)S(1)}, u32[]{:S(2)}, u32[]{:S(2)}) collective-permute-start(bf16[600,4,128]{2,1,0:T(4,128)(2,1)S(1)} %get-tuple-element.25), channel_id=1, source_target_pairs={{0,32},{32,64},{64,96},{96,128},{128,160},{160,192},{192,224},{1,3... | collective-permute-start | bytes 1843208 | tf_op jit(solution)/shard_map/ppermute | solution.py:429
  19.0 16.5 %collective-permute-start.4 = (bf16[538,4,128]{2,1,0:T(4,128)(2,1)S(1)}, bf16[538,4,128]{2,1,0:T(4,128)(2,1)S(1)}, u32[]{:S(2)}, u32[]{:S(2)}) collective-permute-start(bf16[538,4,128]{2,1,0:T(4,128)(2,1)S(1)} %get-tuple-element.26), channel_id=1, source_target_pairs={{32,0},{64,32},{96,64},{128,96},{160,128},{192,160},{224,192},{33,... | collective-permute-start | bytes 1652744 | tf_op jit(solution)/shard_map/ppermute | solution.py:430
  26.6 26.3 %collective-permute-start.6 = (bf16[4,1024,128]{2,1,0:T(8,128)(2,1)S(1)}, bf16[4,1024,128]{2,1,0:T(8,128)(2,1)}, u32[]{:S(2)}, u32[]{:S(2)}) collective-permute-start(bf16[4,1024,128]{2,1,0:T(8,128)(2,1)S(1)} %gather.2.own), channel_id=1, source_target_pairs={{0,1},{1,0},{2,3},{3,2},{4,5},{5,4},{6,7},{7,6},{8,9},{9,8},{10,11... | collective-permute-start | bytes 3145736 | tf_op jit(solution)/shard_map/ppermute | solution.py:436
  39.0 18.5 %collective-permute-start.5 = (bf16[4,1024,128]{2,1,0:T(8,128)(2,1)}, bf16[4,1024,128]{2,1,0:T(8,128)(2,1)}, u32[]{:S(2)}, u32[]{:S(2)}) collective-permute-start(bf16[4,1024,128]{2,1,0:T(8,128)(2,1)} %get-tuple-element.28.own), channel_id=1, source_target_pairs={{0,1},{1,0},{2,3},{3,2},{4,5},{5,4},{6,7},{7,6},{8,9},{9,8},{10,11... | collective-permute-start | bytes 3145736 | tf_op jit(solution)/shard_map/ppermute | solution.py:436
  41.3 40.2 %collective-permute-start.2 = (bf16[4,1024,128]{2,1,0:T(8,128)(2,1)S(1)}, bf16[4,1024,128]{2,1,0:T(8,128)(2,1)}, u32[]{:S(2)}, u32[]{:S(2)}) collective-permute-start(bf16[4,1024,128]{2,1,0:T(8,128)(2,1)S(1)} %gather.2.own), channel_id=1, source_target_pairs={{1,2},{3,4},{5,6},{7,8},{9,10},{11,12},{13,14},{15,16},{17,18},{19... | collective-permute-start | bytes 3145736 | tf_op jit(solution)/shard_map/ppermute | solution.py:441
  45.7 41.3 %collective-permute-start.8 = (bf16[4,512,128]{2,1,0:T(8,128)(2,1)}, bf16[4,512,128]{2,1,0:T(8,128)(2,1)S(1)}, u32[]{:S(2)}, u32[]{:S(2)}) collective-permute-start(bf16[4,512,128]{2,1,0:T(8,128)(2,1)} %get-tuple-element.30), channel_id=1, source_target_pairs={{1,2},{3,4},{5,6},{7,8},{9,10},{11,12},{13,14},{15,16},{17,18},{19... | collective-permute-start | bytes 1572872 | tf_op jit(solution)/shard_map/ppermute | solution.py:441
  48.4 44.4 %collective-permute-start.7 = (bf16[4,512,128]{2,1,0:T(8,128)(2,1)}, bf16[4,512,128]{2,1,0:T(8,128)(2,1)}, u32[]{:S(2)}, u32[]{:S(2)}) collective-permute-start(bf16[4,512,128]{2,1,0:T(8,128)(2,1)} %get-tuple-element.29), channel_id=1, source_target_pairs={{1,2},{3,4},{5,6},{7,8},{9,10},{11,12},{13,14},{15,16},{17,18},{19... | collective-permute-start | bytes 1572872 | tf_op jit(solution)/shard_map/ppermute | solution.py:441

commit v3 on v2

--- a/solution.py
+++ b/solution.py
@@ -15,7 +15,7 @@
 REACH = R - BAND
 ZB = 4
 HALVES = 2
-LAST_PARTS = (8, 8)
+LAST_PARTS = (8, 4, 4)
 PART = 32
 SIDES = 2 * RY + 1
 BF = jnp.bfloat16
@@ -296,22 +296,22 @@
     return terms
 
 
-def early_kernel(half, angles, x, flip_ref, weights, own, near, *rest):
-    totals = rest[-1]
+def early_kernel(angles, x, flip_ref, weights, own_a, near_a, own_b, near_b, totals):
     flip = flip_ref[0]
 
     def level(j, carry):
         for n in range(x):
             column = mirrored(n, x, flip)
             row = j * x + column
-            terms = [(own, c, c - column + RX) for c in range(x)]
-            terms += beside_terms(near, n, column, x, flip)
             for piece in range(angles // PART):
                 at = pl.multiple_of(j * angles + piece * PART, PART)
                 part = slice(piece * PART, (piece + 1) * PART)
-                total = spread(half_sums(weights, half, row, at, terms), half)
-                if len(rest) > 1:
-                    total = total + rest[0][row, part, :]
+                total = None
+                for half, (own, near) in enumerate(((own_a, near_a), (own_b, near_b))):
+                    terms = [(own, c, c - column + RX) for c in range(x)]
+                    terms += beside_terms(near, n, column, x, flip)
+                    term = spread(half_sums(weights, half, row, at, terms), half)
+                    total = term if total is None else total + term
                 totals[row, part, :] = total
         return carry
 
@@ -322,17 +322,16 @@
     return pl.BlockSpec(memory_space=pltpu.SMEM)
 
 
-def early(flip, weights, own, near, totals, half, angles, z, x, y):
-    operands = [flip, weights, own, near] + ([] if totals is None else [totals])
-    return pl.pallas_call(
-        functools.partial(early_kernel, half, angles, x),
+def early(flip, weights, own_a, near_a, own_b, near_b, angles, z, x, y):
+    return pl.pallas_call(
+        functools.partial(early_kernel, angles, x),
         out_shape=struct((z * x, angles, y), F32),
-        in_specs=[scalar_spec()] + [spec()] * (len(operands) - 1),
+        in_specs=[scalar_spec()] + [spec()] * 5,
         out_specs=spec(),
         compiler_params=params(14),
-        cost_estimate=cost(weights.shape[1] * angles * z * x * y, 10 << 20),
+        cost_estimate=cost(2 * weights.shape[1] * angles * z * x * y, 8 << 20),
         name="early",
-    )(*operands)
+    )(flip, weights, own_a, near_a, own_b, near_b)
 
 
 def add_far_kernel(angles, x, flip_ref, weights, far, given, totals):
@@ -359,6 +358,7 @@
         out_shape=struct((z * x, angles, y), F32),
         in_specs=[scalar_spec()] + [spec()] * 3,
         out_specs=spec(),
+        input_output_aliases={3: 0},
         compiler_params=params(14),
         cost_estimate=cost(weights.shape[1] * angles * z * x * y // 4, 8 << 20),
         name="add_far",
@@ -460,8 +460,7 @@
         fars.append(far_of(part, "gx"))
     near_b = near_of(own_b, "gx")
     odd = (lax.axis_index("gx") % 2).astype(jnp.int32).reshape(1)
-    totals = early(odd, weights, own_a, near_a, None, 0, angles, z, x, y)
-    totals = early(odd, weights, own_b, near_b, totals, 1, angles, z, x, y)
+    totals = early(odd, weights, own_a, near_a, own_b, near_b, angles, z, x, y)
     totals = add_far(1 - odd, weights, far_a, totals, angles, z, x, y)
     done, first = None, 0
     for far, planes in zip(fars, LAST_PARTS):

time: 98 us -> 105 us (1.071)
  the two profiles are of different devices: /device:TPU:135 before, /device:TPU:137 now
where the time goes in v3:
time: 105 us; the launch traced here: 104 us
  Pallas kernels  37.2 us (35%)
  starting transfers between devices  32.2 us (31%)
  waiting for transfers between devices  19.7 us (19%)
  local copies, waits for them, and re-layouts  12 us (11%)
  other arithmetic  2.14 us (2%)
    ppermute x4, waiting for transfers between devices, far_of(): return lax.ppermute(x, axis, pairs + [(j, i) for i, j in pairs])  17.2 us
    ppermute x4, starting transfers between devices, far_of(): return lax.ppermute(x, axis, pairs + [(j, i) for i, j in pairs])  14.1 us
    unnamed x22, local copies, waits for them, and re-layouts  11.2 us
    ppermute x2, starting transfers between devices, exchange(): from_down = lax.ppermute(x_down, axis, down)  9.74 us
    pallas_call x3, Pallas kernels, finish(): pl.pallas_call(functools.partial(finish_kernel, angles, x, first), grid=(...  9.06 us
    pallas_call x1, Pallas kernels, early(): pl.pallas_call(functools.partial(early_kernel, angles, x), out_shape=stru...  8.87 us
    pallas_call x2, Pallas kernels, gather(): pl.pallas_call(functools.partial(gather_kernel, before, after, parts), ou...  7.37 us
    ppermute x2, starting transfers between devices, exchange(): from_up = lax.ppermute(x_up, axis, up)  5.03 us
  transfers between devices with their start and end apart: 10, of which 4 were waited for; matrix products, arithmetic and copies ran while one was open for 0% of the time, Pallas kernels for 31%

profile of v3, /device:TPU:137, one launch (start us, length us, event | category | flops | bytes accessed | tf_op | source)
XLA Modules:
  0.0 103.6 jit_solution(5730479088838655059)
XLA Ops:
  1.6 1.4 %fusion.1.slant = bf16[33,64,64]{2,1,0:T(8,128)(2,1)S(1)} fusion(bf16[64,64,33]{1,0,2:T(8,128)(2,1)} %param.7, s32[64,64]{1,0:T(8,128)S(1)} %add_select_fusion, s32[33]{0:T(128)S(1)} %iota_add_fusion), kind=kLoop, calls=%fused_computation.2 | loop fusion | flops 540672 | bytes 557188 | tf_op jit(solution)/shard_map/transpose | solution.py:449
  3.0 1.6 %copy-done = bf16[64,16,4,256]{3,2,1,0:T(4,128)(2,1)S(1)} copy-done((bf16[64,16,4,256]{3,2,1,0:T(4,128)(2,1)S(1)}, bf16[64,16,4,256]{3,2,1,0:T(4,128)(2,1)}, u32[]{:S(2)}) %copy-start) | copy-done | bytes 2097176
  5.3 3.4 %prepare.1 = (bf16[600,4,128]{2,1,0:T(4,128)(2,1)}, bf16[538,4,128]{2,1,0:T(4,128)(2,1)}, bf16[2,1024,256]{2,1,0:T(8,128)(2,1)S(1)}, bf16[2,1024,256]{2,1,0:T(8,...) custom-call(bf16[64,16,4,256]{3,2,1,0:T(4,128)(2,1)S(1)} %copy-done, f32[8,27]{1,0:T(8,128)S(1)} %copy-done.3, ...), custom_call_target="tpu_custom_call" | custom-call | flops 536870912 | bytes 8388608 | tf_op jit(solution)/shard_map/prepare/pallas_call | solution.py:155
  8.7 1.0 copy-done.4
  9.7 1.0 copy-done.7
  11.7 3.1 %collective-permute-start.4 = (bf16[600,4,128]{2,1,0:T(4,128)(2,1)}, bf16[600,4,128]{2,1,0:T(4,128)(2,1)}, u32[]{:S(2)}, u32[]{:S(2)}) collective-permute-start(bf16[600,4,128]{2,1,0:T(4,128)(2,1)} %get-tuple-element.26), channel_id=1, source_target_pairs={{0,32},{32,64},{64,96},{96,128},{128,160},{160,192},{192,224},{1,3... | collective-permute-start | bytes 1843208 | tf_op jit(solution)/shard_map/ppermute | solution.py:429
  14.8 4.3 %collective-permute-start.5 = (bf16[538,4,128]{2,1,0:T(4,128)(2,1)}, bf16[538,4,128]{2,1,0:T(4,128)(2,1)}, u32[]{:S(2)}, u32[]{:S(2)}) collective-permute-start(bf16[538,4,128]{2,1,0:T(4,128)(2,1)} %get-tuple-element.27), channel_id=1, source_target_pairs={{32,0},{64,32},{96,64},{128,96},{160,128},{192,160},{224,192},{33,... | collective-permute-start | bytes 1652744 | tf_op jit(solution)/shard_map/ppermute | solution.py:430
  19.1 2.7 %pack.1 = (bf16[600,4,128]{2,1,0:T(4,128)(2,1)}, bf16[538,4,128]{2,1,0:T(4,128)(2,1)}) custom-call(bf16[64,16,4,256]{3,2,1,0:T(4,128)(2,1)} %image.3), custom_call_target="tpu_custom_call" | custom-call | tf_op jit(solution)/shard_map/pack/pallas_call | solution.py:102
  21.8 1.9 %collective-permute-start = (bf16[600,4,128]{2,1,0:T(4,128)(2,1)}, bf16[600,4,128]{2,1,0:T(4,128)(2,1)S(1)}, u32[]{:S(2)}, u32[]{:S(2)}) collective-permute-start(bf16[600,4,128]{2,1,0:T(4,128)(2,1)} %get-tuple-element.21), channel_id=1, source_target_pairs={{0,32},{32,64},{64,96},{96,128},{128,160},{160,192},{192,224},{1,3... | collective-permute-start | bytes 1843208 | tf_op jit(solution)/shard_map/ppermute | solution.py:429
  23.7 5.5 %collective-permute-start.1 = (bf16[538,4,128]{2,1,0:T(4,128)(2,1)}, bf16[538,4,128]{2,1,0:T(4,128)(2,1)S(1)}, u32[]{:S(2)}, u32[]{:S(2)}) collective-permute-start(bf16[538,4,128]{2,1,0:T(4,128)(2,1)} %get-tuple-element.22), channel_id=1, source_target_pairs={{32,0},{64,32},{96,64},{128,96},{160,128},{192,160},{224,192},{33,... | collective-permute-start | bytes 1652744 | tf_op jit(solution)/shard_map/ppermute | solution.py:430
  29.2 1.3 %copy-done.5 = bf16[256,2304]{1,0:T(8,128)(2,1)S(1)} copy-done((bf16[256,2304]{1,0:T(8,128)(2,1)S(1)}, bf16[256,2304]{1,0:T(8,128)(2,1)}, u32[]{:S(2)}) %copy-start.5) | copy-done | bytes 1179672
  30.5 1.2 %copy-done.8 = bf16[2,1024,256]{2,1,0:T(8,128)(2,1)S(1)} copy-done((bf16[2,1024,256]{2,1,0:T(8,128)(2,1)S(1)}, bf16[2,1024,256]{2,1,0:T(8,128)(2,1)}, u32[]{:S(2)}) %copy-start.8) | copy-done | bytes 1048600
  31.7 1.2 %copy-done.10 = bf16[2,1024,256]{2,1,0:T(8,128)(2,1)S(1)} copy-done((bf16[2,1024,256]{2,1,0:T(8,128)(2,1)S(1)}, bf16[2,1024,256]{2,1,0:T(8,128)(2,1)}, u32[]{:S(2)}) %copy-start.10) | copy-done | bytes 1048600
  32.9 2.3 %own_part.1 = (f32[4,2,256,256]{3,2,1,0:T(8,128)S(1)}, f32[4,2,256,256]{3,2,1,0:T(8,128)S(1)}) custom-call(bf16[256,2304]{1,0:T(8,128)(2,1)S(1)} %copy-done.5, bf16[2,1024,256]{2,1,0:T(8,128)(2,1)S(1)} %copy-done.8, bf16[2,1024,256]{2,1,0:T(8,128)(2,1)S(1)} %copy-done.10), custom_call_target="tpu_custom_call" | custom-call | flops 2147483648 | bytes 9437184 | tf_op jit(solution)/shard_map/own_part/pallas_call | solution.py:203
  35.3 4.2 %gather.3 = (bf16[4,1024,128]{2,1,0:T(8,128)(2,1)S(1)}, bf16[4,512,128]{2,1,0:T(8,128)(2,1)}, bf16[4,256,128]{2,1,0:T(8,128)(2,1)}, bf16[4,256,128]{2,1,0:T(8,128)(2,1)}) custom-call(bf16[256,2304]{1,0:T(8,128)(2,1)S(1)} %copy-done.6, bf16[600,4,128]{2,1,0:T(4,128)(2,1)} %collective-permute-done.4.up, bf16[538,4,128]{2,1,0:T(4,128)(2,1)} %collective-permute-done.5.down, ...), custom_call_target="tpu_custom_call" | custom-call | flops 2415919104 | bytes 6291456 | tf_op jit(solution)/shard_map/gather/pallas_call | solution.py:253
  39.4 1.8 %collective-permute-start.6 = (bf16[4,1024,128]{2,1,0:T(8,128)(2,1)S(1)}, bf16[4,1024,128]{2,1,0:T(8,128)(2,1)S(1)}, u32[]{:S(2)}, u32[]{:S(2)}) collective-permute-start(bf16[4,1024,128]{2,1,0:T(8,128)(2,1)S(1)} %get-tuple-element.29.own_b), channel_id=1, source_target_pairs={{0,1},{1,0},{2,3},{3,2},{4,5},{5,4},{6,7},{7,6},{8,9},{9,8},{10,11... | collective-permute-start | bytes 3145736 | tf_op jit(solution)/shard_map/ppermute | solution.py:436
  42.0 1.7 %collective-permute-done.up = bf16[600,4,128]{2,1,0:T(4,128)(2,1)S(1)} collective-permute-done((bf16[600,4,128]{2,1,0:T(4,128)(2,1)}, bf16[600,4,128]{2,1,0:T(4,128)(2,1)S(1)}, u32[]{:S(2)}, u32[]{:S(2)}) %collective-permute-start) | collective-permute-done | bytes 614432 | tf_op jit(solution)/shard_map/ppermute | solution.py:429
  43.8 3.2 %gather.2.own_a = bf16[4,1024,128]{2,1,0:T(8,128)(2,1)} custom-call(bf16[256,2304]{1,0:T(8,128)(2,1)S(1)} %copy-done.6, bf16[600,4,128]{2,1,0:T(4,128)(2,1)S(1)} %collective-permute-done.up, bf16[538,4,128]{2,1,0:T(4,128)(2,1)S(1)} %collective-permute-done.1.down, f32[4,2,256,256]{3,2,1,0:T(8,128)S(1)} %get-tuple-element.25.given), custom_call_target="tpu_custom_call" | custom-call | flops 2415919104 | bytes 6291456 | tf_op jit(solution)/shard_map/gather/pallas_call | solution.py:253
  47.0 1.5 %collective-permute-start.3 = (bf16[4,1024,128]{2,1,0:T(8,128)(2,1)}, bf16[4,1024,128]{2,1,0:T(8,128)(2,1)}, u32[]{:S(2)}, u32[]{:S(2)}) collective-permute-start(bf16[4,1024,128]{2,1,0:T(8,128)(2,1)} %gather.2.own_a), channel_id=1, source_target_pairs={{0,1},{1,0},{2,3},{3,2},{4,5},{5,4},{6,7},{7,6},{8,9},{9,8},{10,11... | collective-permute-start | bytes 3145736 | tf_op jit(solution)/shard_map/ppermute | solution.py:436
  48.5 3.8 %collective-permute-start.2 = (bf16[4,1024,128]{2,1,0:T(8,128)(2,1)}, bf16[4,1024,128]{2,1,0:T(8,128)(2,1)}, u32[]{:S(2)}, u32[]{:S(2)}) collective-permute-start(bf16[4,1024,128]{2,1,0:T(8,128)(2,1)} %gather.2.own_a), channel_id=1, source_target_pairs={{1,2},{3,4},{5,6},{7,8},{9,10},{11,12},{13,14},{15,16},{17,18},{19... | collective-permute-start | bytes 3145736 | tf_op jit(solution)/shard_map/ppermute | solution.py:441
  52.3 3.3 %collective-permute-start.9 = (bf16[4,512,128]{2,1,0:T(8,128)(2,1)}, bf16[4,512,128]{2,1,0:T(8,128)(2,1)}, u32[]{:S(2)}, u32[]{:S(2)}) collective-permute-start(bf16[4,512,128]{2,1,0:T(8,128)(2,1)} %get-tuple-element.32), channel_id=1, source_target_pairs={{1,2},{3,4},{5,6},{7,8},{9,10},{11,12},{13,14},{15,16},{17,18},{19... | collective-permute-start | bytes 1572872 | tf_op jit(solution)/shard_map/ppermute | solution.py:441
  55.6 3.8 %collective-permute-start.8 = (bf16[4,256,128]{2,1,0:T(8,128)(2,1)}, bf16[4,256,128]{2,1,0:T(8,128)(2,1)S(1)}, u32[]{:S(2)}, u32[]{:S(2)}) collective-permute-start(bf16[4,256,128]{2,1,0:T(8,128)(2,1)} %get-tuple-element.31), channel_id=1, source_target_pairs={{1,2},{3,4},{5,6},{7,8},{9,10},{11,12},{13,14},{15,16},{17,18},{19... | collective-permute-start | bytes 786440 | tf_op jit(solution)/shard_map/ppermute | solution.py:441
  59.4 1.0 copy-done.1
  60.4 3.2 %collective-permute-start.7 = (bf16[4,256,128]{2,1,0:T(8,128)(2,1)}, bf16[4,256,128]{2,1,0:T(8,128)(2,1)S(1)}, u32[]{:S(2)}, u32[]{:S(2)}) collective-permute-start(bf16[4,256,128]{2,1,0:T(8,128)(2,1)} %get-tuple-element.30), channel_id=1, source_target_pairs={{1,2},{3,4},{5,6},{7,8},{9,10},{11,12},{13,14},{15,16},{17,18},{19... | collective-permute-start | bytes 786440 | tf_op jit(solution)/shard_map/ppermute | solution.py:441
  63.7 1.2 %copy-done.2 = bf16[4,1024,128]{2,1,0:T(8,128)(2,1)S(1)} copy-done((bf16[4,1024,128]{2,1,0:T(8,128)(2,1)S(1)}, bf16[4,1024,128]{2,1,0:T(8,128)(2,1)}, u32[]{:S(2)}) %copy-start.2) | copy-done | bytes 1048600
  64.9 8.9 %early.1.given = f32[64,64,256]{2,1,0:T(8,128)S(1)} custom-call(s32[1]{0:T(128)} %bitcast.flip_ref, f32[2,27,64,128]{3,2,1,0:T(8,128)S(1)} %get-tuple-element.19.weights, bf16[4,1024,128]{2,1,0:T(8,128)(2,1)} %gather.2.own_a, bf16[4,1024,128]{2,1,0:T(8,128)(2,1)} %collective-permute-done.3.near_a, bf16[4,1024,128]{2,1,0:T(8,128)(2,1)S(1)} %get-tuple-element.29.own_b, ...), custom_call_target="tpu_custom_call" | custom-call | flops 56623104 | bytes 8388608 | tf_op jit(solution)/shard_map/early/pallas_call | solution.py:326
  73.8 15.1 %collective-permute-done.2.far = bf16[4,1024,128]{2,1,0:T(8,128)(2,1)} collective-permute-done((bf16[4,1024,128]{2,1,0:T(8,128)(2,1)}, bf16[4,1024,128]{2,1,0:T(8,128)(2,1)}, u32[]{:S(2)}, u32[]{:S(2)}) %collective-permute-start.2) | collective-permute-done | bytes 1048608 | tf_op jit(solution)/shard_map/ppermute | solution.py:441
  88.9 3.5 %add_far.1.totals = f32[64,64,256]{2,1,0:T(8,128)S(1)} custom-call(s32[1]{0:T(128)S(6)} %sub.16.flip_ref, f32[2,27,64,128]{3,2,1,0:T(8,128)S(1)} %get-tuple-element.19.weights, bf16[4,1024,128]{2,1,0:T(8,128)(2,1)} %collective-permute-done.2.far, f32[64,64,256]{2,1,0:T(8,128)S(1)} %early.1.given), custom_call_target="tpu_custom_call", output_to_operand_aliasing={{}: (3, {})} | custom-call | flops 7077888 | bytes 8388608 | tf_op jit(solution)/shard_map/add_far/pallas_call | solution.py:356
  92.5 2.1 %collective-permute-done.9.far = bf16[4,512,128]{2,1,0:T(8,128)(2,1)} collective-permute-done((bf16[4,512,128]{2,1,0:T(8,128)(2,1)}, bf16[4,512,128]{2,1,0:T(8,128)(2,1)}, u32[]{:S(2)}, u32[]{:S(2)}) %collective-permute-start.9) | collective-permute-done | bytes 524320 | tf_op jit(solution)/shard_map/ppermute | solution.py:441
  94.5 4.7 %finish.3.rest_0_ = bf16[64,16,4,256]{3,2,1,0:T(4,128)(2,1)} custom-call(s32[1]{0:T(128)S(6)} %sub.16.flip_ref, f32[2,27,64,128]{3,2,1,0:T(8,128)S(1)} %get-tuple-element.19.weights, f32[64,64,256]{2,1,0:T(8,128)S(1)} %add_far.1.totals, bf16[4,512,128]{2,1,0:T(8,128)(2,1)} %collective-permute-done.9.far), custom_call_target="tpu_custom_call" | custom-call | flops 3538944 | bytes 3145728 | tf_op jit(solution)/shard_map/finish/pallas_call | solution.py:403
  99.2 2.2 %finish.4.rest_0_ = bf16[64,16,4,256]{3,2,1,0:T(4,128)(2,1)} custom-call(s32[1]{0:T(128)S(6)} %sub.16.flip_ref, f32[2,27,64,128]{3,2,1,0:T(8,128)S(1)} %get-tuple-element.19.weights, f32[64,64,256]{2,1,0:T(8,128)S(1)} %add_far.1.totals, bf16[4,256,128]{2,1,0:T(8,128)(2,1)S(1)} %collective-permute-done.8.far, ...), custom_call_target="tpu_custom_call", output_to_operand_aliasing={{}: (4, {})} | custom-call | flops 1769472 | bytes 3145728 | tf_op jit(solution)/shard_map/finish/pallas_call | solution.py:403
  101.4 2.2 %finish.5 = bf16[64,16,4,256]{3,2,1,0:T(4,128)(2,1)} custom-call(s32[1]{0:T(128)S(6)} %sub.16.flip_ref, f32[2,27,64,128]{3,2,1,0:T(8,128)S(1)} %get-tuple-element.19.weights, f32[64,64,256]{2,1,0:T(8,128)S(1)} %add_far.1.totals, bf16[4,256,128]{2,1,0:T(8,128)(2,1)S(1)} %collective-permute-done.7.far, ...), custom_call_target="tpu_custom_call", output_to_operand_aliasing={{}: (4, {})} | custom-call | flops 1769472 | bytes 3145728 | tf_op jit(solution)/shard_map/finish/pallas_call | solution.py:403
  (24 shorter events, 4.1 us)
Async XLA Ops:
  3.0 1.6 %copy-start = (bf16[64,16,4,256]{3,2,1,0:T(4,128)(2,1)S(1)}, bf16[64,16,4,256]{3,2,1,0:T(4,128)(2,1)}, u32[]{:S(2)}) copy-start(bf16[64,16,4,256]{3,2,1,0:T(4,128)(2,1)} %image.3) | copy-start | bytes 6291460
  4.6 0.7 copy-start.3
  8.7 1.0 copy-start.4
  9.7 1.0 copy-start.7
  10.7 1.0 copy-start.9
  11.7 23.6 %collective-permute-start.4 = (bf16[600,4,128]{2,1,0:T(4,128)(2,1)}, bf16[600,4,128]{2,1,0:T(4,128)(2,1)}, u32[]{:S(2)}, u32[]{:S(2)}) collective-permute-start(bf16[600,4,128]{2,1,0:T(4,128)(2,1)} %get-tuple-element.26), channel_id=1, source_target_pairs={{0,32},{32,64},{64,96},{96,128},{128,160},{160,192},{192,224},{1,3... | collective-permute-start | bytes 1843208 | tf_op jit(solution)/shard_map/ppermute | solution.py:429
  14.8 20.5 %collective-permute-start.5 = (bf16[538,4,128]{2,1,0:T(4,128)(2,1)}, bf16[538,4,128]{2,1,0:T(4,128)(2,1)}, u32[]{:S(2)}, u32[]{:S(2)}) collective-permute-start(bf16[538,4,128]{2,1,0:T(4,128)(2,1)} %get-tuple-element.27), channel_id=1, source_target_pairs={{32,0},{64,32},{96,64},{128,96},{160,128},{192,160},{224,192},{33,... | collective-permute-start | bytes 1652744 | tf_op jit(solution)/shard_map/ppermute | solution.py:430
  21.8 22.0 %collective-permute-start = (bf16[600,4,128]{2,1,0:T(4,128)(2,1)}, bf16[600,4,128]{2,1,0:T(4,128)(2,1)S(1)}, u32[]{:S(2)}, u32[]{:S(2)}) collective-permute-start(bf16[600,4,128]{2,1,0:T(4,128)(2,1)} %get-tuple-element.21), channel_id=1, source_target_pairs={{0,32},{32,64},{64,96},{96,128},{128,160},{160,192},{192,224},{1,3... | collective-permute-start | bytes 1843208 | tf_op jit(solution)/shard_map/ppermute | solution.py:429
  23.7 18.3 %collective-permute-start.1 = (bf16[538,4,128]{2,1,0:T(4,128)(2,1)}, bf16[538,4,128]{2,1,0:T(4,128)(2,1)S(1)}, u32[]{:S(2)}, u32[]{:S(2)}) collective-permute-start(bf16[538,4,128]{2,1,0:T(4,128)(2,1)} %get-tuple-element.22), channel_id=1, source_target_pairs={{32,0},{64,32},{96,64},{128,96},{160,128},{192,160},{224,192},{33,... | collective-permute-start | bytes 1652744 | tf_op jit(solution)/shard_map/ppermute | solution.py:430
  29.2 1.3 %copy-start.5 = (bf16[256,2304]{1,0:T(8,128)(2,1)S(1)}, bf16[256,2304]{1,0:T(8,128)(2,1)}, u32[]{:S(2)}) copy-start(bf16[256,2304]{1,0:T(8,128)(2,1)} %copy-done.4) | copy-start | bytes 3538948
  30.4 1.2 %copy-start.8 = (bf16[2,1024,256]{2,1,0:T(8,128)(2,1)S(1)}, bf16[2,1024,256]{2,1,0:T(8,128)(2,1)}, u32[]{:S(2)}) copy-start(bf16[2,1024,256]{2,1,0:T(8,128)(2,1)} %copy-done.7) | copy-start | bytes 3145732
  31.7 1.2 %copy-start.10 = (bf16[2,1024,256]{2,1,0:T(8,128)(2,1)S(1)}, bf16[2,1024,256]{2,1,0:T(8,128)(2,1)}, u32[]{:S(2)}) copy-start(bf16[2,1024,256]{2,1,0:T(8,128)(2,1)} %copy-done.9) | copy-start | bytes 3145732
  32.9 2.4 %copy-start.6 = (bf16[256,2304]{1,0:T(8,128)(2,1)S(1)}, bf16[256,2304]{1,0:T(8,128)(2,1)}, u32[]{:S(2)}) copy-start(bf16[256,2304]{1,0:T(8,128)(2,1)} %copy-done.4) | copy-start | bytes 3538948
  39.4 20.0 %collective-permute-start.6 = (bf16[4,1024,128]{2,1,0:T(8,128)(2,1)S(1)}, bf16[4,1024,128]{2,1,0:T(8,128)(2,1)S(1)}, u32[]{:S(2)}, u32[]{:S(2)}) collective-permute-start(bf16[4,1024,128]{2,1,0:T(8,128)(2,1)S(1)} %get-tuple-element.29.own_b), channel_id=1, source_target_pairs={{0,1},{1,0},{2,3},{3,2},{4,5},{5,4},{6,7},{7,6},{8,9},{9,8},{10,11... | collective-permute-start | bytes 3145736 | tf_op jit(solution)/shard_map/ppermute | solution.py:436
  47.0 16.7 %collective-permute-start.3 = (bf16[4,1024,128]{2,1,0:T(8,128)(2,1)}, bf16[4,1024,128]{2,1,0:T(8,128)(2,1)}, u32[]{:S(2)}, u32[]{:S(2)}) collective-permute-start(bf16[4,1024,128]{2,1,0:T(8,128)(2,1)} %gather.2.own_a), channel_id=1, source_target_pairs={{0,1},{1,0},{2,3},{3,2},{4,5},{5,4},{6,7},{7,6},{8,9},{9,8},{10,11... | collective-permute-start | bytes 3145736 | tf_op jit(solution)/shard_map/ppermute | solution.py:436
  48.5 40.4 %collective-permute-start.2 = (bf16[4,1024,128]{2,1,0:T(8,128)(2,1)}, bf16[4,1024,128]{2,1,0:T(8,128)(2,1)}, u32[]{:S(2)}, u32[]{:S(2)}) collective-permute-start(bf16[4,1024,128]{2,1,0:T(8,128)(2,1)} %gather.2.own_a), channel_id=1, source_target_pairs={{1,2},{3,4},{5,6},{7,8},{9,10},{11,12},{13,14},{15,16},{17,18},{19... | collective-permute-start | bytes 3145736 | tf_op jit(solution)/shard_map/ppermute | solution.py:441
  52.3 42.2 %collective-permute-start.9 = (bf16[4,512,128]{2,1,0:T(8,128)(2,1)}, bf16[4,512,128]{2,1,0:T(8,128)(2,1)}, u32[]{:S(2)}, u32[]{:S(2)}) collective-permute-start(bf16[4,512,128]{2,1,0:T(8,128)(2,1)} %get-tuple-element.32), channel_id=1, source_target_pairs={{1,2},{3,4},{5,6},{7,8},{9,10},{11,12},{13,14},{15,16},{17,18},{19... | collective-permute-start | bytes 1572872 | tf_op jit(solution)/shard_map/ppermute | solution.py:441
  55.6 43.6 %collective-permute-start.8 = (bf16[4,256,128]{2,1,0:T(8,128)(2,1)}, bf16[4,256,128]{2,1,0:T(8,128)(2,1)S(1)}, u32[]{:S(2)}, u32[]{:S(2)}) collective-permute-start(bf16[4,256,128]{2,1,0:T(8,128)(2,1)} %get-tuple-element.31), channel_id=1, source_target_pairs={{1,2},{3,4},{5,6},{7,8},{9,10},{11,12},{13,14},{15,16},{17,18},{19... | collective-permute-start | bytes 786440 | tf_op jit(solution)/shard_map/ppermute | solution.py:441
  59.4 1.0 copy-start.1
  60.4 41.0 %collective-permute-start.7 = (bf16[4,256,128]{2,1,0:T(8,128)(2,1)}, bf16[4,256,128]{2,1,0:T(8,128)(2,1)S(1)}, u32[]{:S(2)}, u32[]{:S(2)}) collective-permute-start(bf16[4,256,128]{2,1,0:T(8,128)(2,1)} %get-tuple-element.30), channel_id=1, source_target_pairs={{1,2},{3,4},{5,6},{7,8},{9,10},{11,12},{13,14},{15,16},{17,18},{19... | collective-permute-start | bytes 786440 | tf_op jit(solution)/shard_map/ppermute | solution.py:441
  63.7 1.2 %copy-start.2 = (bf16[4,1024,128]{2,1,0:T(8,128)(2,1)S(1)}, bf16[4,1024,128]{2,1,0:T(8,128)(2,1)}, u32[]{:S(2)}) copy-start(bf16[4,1024,128]{2,1,0:T(8,128)(2,1)} %copy-done.1) | copy-start | bytes 3145732

commit v4 on v2

--- a/solution.py
+++ b/solution.py
@@ -278,14 +278,21 @@
 
 
 def spread(sums, half):
-    zero = jnp.zeros_like(sums[0])
-    total = None
+    width = sums[0].shape[1]
+    lane = lax.broadcasted_iota(jnp.int32, sums[0].shape, 1)
+    here, there = sums[RY], jnp.zeros_like(sums[0])
     for side in range(SIDES):
-        both = jnp.concatenate([sums[side], zero] if half == 0 else [zero, sums[side]], axis=1)
-        if side != RY:
-            both = pltpu.roll(both, (RY - side) % both.shape[1], 1)
-        total = both if total is None else total + both
-    return total
+        shift = RY - side
+        if shift == 0:
+            continue
+        moved = pltpu.roll(sums[side], shift % width, 1)
+        if (shift > 0) == (half == 0):
+            edge = lane < shift if shift > 0 else lane >= width + shift
+            here = here + jnp.where(edge, 0.0, moved)
+            there = there + jnp.where(edge, moved, 0.0)
+        else:
+            here = here + moved
+    return jnp.concatenate([here, there] if half == 0 else [there, here], axis=1)
 
 
 def beside_terms(source, n, column, x, flip):
@@ -366,10 +373,13 @@
 
 
 def finish_kernel(angles, x, first, flip_ref, weights, totals, far, *rest):
-    out, scratch = rest[-2:]
+    out, scratch, unswap = rest[-3:]
     flip = flip_ref[0]
-    unswap = unswap_matrix(angles, x)
     base = pl.program_id(0) * ZB
+
+    @pl.when(pl.program_id(0) == 0)
+    def _():
+        unswap[...] = unswap_matrix(angles, x)
 
     def level(j, carry):
         for n in range(x):
@@ -377,13 +387,13 @@
             row = (first + base + j) * x + column
             terms = beside_terms(far, n, column, x, flip)
             for piece in range(angles // PART):
-                at = pl.multiple_of((base + j) * angles + piece * PART, PART)
+                at = pl.multiple_of(j * angles + piece * PART, PART)
                 part = slice(piece * PART, (piece + 1) * PART)
                 sums = half_sums(weights, 1, row, at, terms)
                 total = totals[row, part, :] + spread(sums, 1)
                 to = pl.multiple_of(column * angles + piece * PART, PART)
                 scratch[pl.ds(to, PART), :] = total.astype(BF)
-        moved = jnp.dot(unswap, scratch[...], preferred_element_type=F32)
+        moved = jnp.dot(unswap[...], scratch[...], preferred_element_type=F32)
         out[:, j] = moved.astype(BF).reshape(angles, x, out.shape[3])
         return carry
 
@@ -393,7 +403,8 @@
 def finish(flip, weights, totals, far, done, first, shape):
     angles, _, x, y = shape
     planes = far.shape[1] // angles
-    in_specs = [scalar_spec()] + [spec()] * 3
+    far_spec = pl.BlockSpec((x, ZB * angles, far.shape[2]), lambda i: (0, i, 0))
+    in_specs = [scalar_spec(), spec(), spec(), far_spec]
     operands = [flip, weights, totals, far]
     aliases = {}
     if done is not None:
@@ -406,7 +417,7 @@
         out_shape=struct(shape),
         in_specs=in_specs,
         out_specs=pl.BlockSpec((angles, ZB, x, y), lambda i: (0, first // ZB + i, 0, 0)),
-        scratch_shapes=[pltpu.VMEM((angles * x, y), BF)],
+        scratch_shapes=[pltpu.VMEM((angles * x, y), BF), pltpu.VMEM((angles * x,) * 2, BF)],
         input_output_aliases=aliases,
         compiler_params=params(14),
         cost_estimate=cost(weights.shape[1] * angles * planes * x * y // 4, 3 << 20),

time: 98 us -> 97.8 us (level)
  no operation moved by 1% of the time
where the time goes in v4:
time: 97.8 us; the launch traced here: 97.3 us
  Pallas kernels  35.2 us (36%)
  waiting for transfers between devices  30.6 us (31%)
  starting transfers between devices  28.1 us (29%)
  local copies, waits for them, and re-layouts  1.62 us (2%)
  other arithmetic  1.49 us (2%)
    ppermute x3, waiting for transfers between devices, far_of(): return lax.ppermute(x, axis, pairs + [(j, i) for i, j in pairs])  23.5 us
    ppermute x3, starting transfers between devices, far_of(): return lax.ppermute(x, axis, pairs + [(j, i) for i, j in pairs])  11.5 us
    pallas_call x2, Pallas kernels, early(): pl.pallas_call(functools.partial(early_kernel, half, angles, x), out_shap...  9.29 us
    ppermute x2, starting transfers between devices, exchange(): from_up = lax.ppermute(x_up, axis, up)  8.35 us
    pallas_call x2, Pallas kernels, finish(): pl.pallas_call(functools.partial(finish_kernel, angles, x, first), grid=(...  8.17 us
    ppermute x2, waiting for transfers between devices, exchange(): from_down = lax.ppermute(x_down, axis, down)  7.14 us
    pallas_call x2, Pallas kernels, gather(): pl.pallas_call(functools.partial(gather_kernel, before, after, parts), ou...  6.67 us
    ppermute x2, starting transfers between devices, near_of(): return lax.ppermute(x, axis, [(i, i ^ 1) for i in range(count)])  4.22 us
  transfers between devices with their start and end apart: 9, of which 4 were waited for; matrix products, arithmetic and copies ran while one was open for 2% of the time, Pallas kernels for 29%

profile of v4, /device:TPU:135, one launch (start us, length us, event | category | flops | bytes accessed | tf_op | source)
XLA Modules:
  0.0 97.3 jit_solution(6225644760300597023)
XLA Ops:
  0.0 2.7 %pack.1 = (bf16[600,4,128]{2,1,0:T(4,128)(2,1)}, bf16[538,4,128]{2,1,0:T(4,128)(2,1)}) custom-call(bf16[64,16,4,256]{3,2,1,0:T(4,128)(2,1)} %image.3), custom_call_target="tpu_custom_call" | custom-call | tf_op jit(solution)/shard_map/pack/pallas_call | solution.py:102
  2.7 3.1 %collective-permute-start = (bf16[600,4,128]{2,1,0:T(4,128)(2,1)}, bf16[600,4,128]{2,1,0:T(4,128)(2,1)S(1)}, u32[]{:S(2)}, u32[]{:S(2)}) collective-permute-start(bf16[600,4,128]{2,1,0:T(4,128)(2,1)} %get-tuple-element.20), channel_id=1, source_target_pairs={{0,32},{32,64},{64,96},{96,128},{128,160},{160,192},{192,224},{1,3... | collective-permute-start | bytes 1843208 | tf_op jit(solution)/shard_map/ppermute | solution.py:440
  5.8 2.2 %collective-permute-start.1 = (bf16[538,4,128]{2,1,0:T(4,128)(2,1)}, bf16[538,4,128]{2,1,0:T(4,128)(2,1)}, u32[]{:S(2)}, u32[]{:S(2)}) collective-permute-start(bf16[538,4,128]{2,1,0:T(4,128)(2,1)} %get-tuple-element.21), channel_id=1, source_target_pairs={{32,0},{64,32},{96,64},{128,96},{160,128},{192,160},{224,192},{33,... | collective-permute-start | bytes 1652744 | tf_op jit(solution)/shard_map/ppermute | solution.py:441
  8.0 0.1 add_select_fusion
  8.1 1.4 %fusion.1.slant = bf16[33,64,64]{2,1,0:T(8,128)(2,1)S(1)} fusion(bf16[64,64,33]{1,0,2:T(8,128)(2,1)} %param.7, s32[64,64]{1,0:T(8,128)S(1)} %add_select_fusion, s32[33]{0:T(128)S(1)} %iota_add_fusion), kind=kLoop, calls=%fused_computation.2 | loop fusion | flops 540672 | bytes 557188 | tf_op jit(solution)/shard_map/transpose | solution.py:460
  9.6 0.0 copy-start
  9.6 1.6 %copy-done = bf16[64,16,4,256]{3,2,1,0:T(4,128)(2,1)S(1)} copy-done((bf16[64,16,4,256]{3,2,1,0:T(4,128)(2,1)S(1)}, bf16[64,16,4,256]{3,2,1,0:T(4,128)(2,1)}, u32[]{:S(2)}) %copy-start) | copy-done | bytes 2097176
  11.2 2.6 %prepare.1 = (bf16[600,4,128]{2,1,0:T(4,128)(2,1)S(1)}, bf16[538,4,128]{2,1,0:T(4,128)(2,1)S(1)}, bf16[2,1024,256]{2,1,0:T(8,128)(2,1)S(1)}, bf16[2,1024,256]{2,...) custom-call(bf16[64,16,4,256]{3,2,1,0:T(4,128)(2,1)S(1)} %copy-done, ...), custom_call_target="tpu_custom_call" | custom-call | flops 536870912 | bytes 8388608 | tf_op jit(solution)/shard_map/prepare/pallas_call | solution.py:155
  13.8 5.2 %collective-permute-start.3 = (bf16[600,4,128]{2,1,0:T(4,128)(2,1)S(1)}, bf16[600,4,128]{2,1,0:T(4,128)(2,1)S(1)}, u32[]{:S(2)}, u32[]{:S(2)}) collective-permute-start(bf16[600,4,128]{2,1,0:T(4,128)(2,1)S(1)} %get-tuple-element.25), channel_id=1, source_target_pairs={{0,32},{32,64},{64,96},{96,128},{128,160},{160,192},{192,224},{1,3... | collective-permute-start | bytes 1843208 | tf_op jit(solution)/shard_map/ppermute | solution.py:440
  19.0 1.9 %collective-permute-start.4 = (bf16[538,4,128]{2,1,0:T(4,128)(2,1)S(1)}, bf16[538,4,128]{2,1,0:T(4,128)(2,1)S(1)}, u32[]{:S(2)}, u32[]{:S(2)}) collective-permute-start(bf16[538,4,128]{2,1,0:T(4,128)(2,1)S(1)} %get-tuple-element.26), channel_id=1, source_target_pairs={{32,0},{64,32},{96,64},{128,96},{160,128},{192,160},{224,192},{33,... | collective-permute-start | bytes 1652744 | tf_op jit(solution)/shard_map/ppermute | solution.py:441
  20.9 2.3 %own_part.1 = (f32[4,2,256,256]{3,2,1,0:T(8,128)S(1)}, f32[4,2,256,256]{3,2,1,0:T(8,128)S(1)}) custom-call(bf16[256,2304]{1,0:T(8,128)(2,1)S(1)} %get-tuple-element.19.matrix, bf16[2,1024,256]{2,1,0:T(8,128)(2,1)S(1)} %get-tuple-element.22.mid_a, bf16[2,1024,256]{2,1,0:T(8,128)(2,1)S(1)} %get-tuple-element.23.mid_b), custom_call_target="tpu_custom_call" | custom-call | flops 2147483648 | bytes 9437184 | tf_op jit(solution)/shard_map/own_part/pallas_call | solution.py:203
  23.3 0.0 collective-permute-done.1.down
  23.3 0.0 collective-permute-done.up
  23.3 3.3 %gather.2.own = bf16[4,1024,128]{2,1,0:T(8,128)(2,1)S(1)} custom-call(bf16[256,2304]{1,0:T(8,128)(2,1)S(1)} %get-tuple-element.19.matrix, bf16[600,4,128]{2,1,0:T(4,128)(2,1)S(1)} %collective-permute-done.up, bf16[538,4,128]{2,1,0:T(4,128)(2,1)} %collective-permute-done.1.down, f32[4,2,256,256]{3,2,1,0:T(8,128)S(1)} %get-tuple-element.24.given), custom_call_target="tpu_custom_call" | custom-call | flops 2415919104 | bytes 6291456 | tf_op jit(solution)/shard_map/gather/pallas_call | solution.py:253
  26.6 1.8 %collective-permute-start.6 = (bf16[4,1024,128]{2,1,0:T(8,128)(2,1)S(1)}, bf16[4,1024,128]{2,1,0:T(8,128)(2,1)}, u32[]{:S(2)}, u32[]{:S(2)}) collective-permute-start(bf16[4,1024,128]{2,1,0:T(8,128)(2,1)S(1)} %gather.2.own), channel_id=1, source_target_pairs={{0,1},{1,0},{2,3},{3,2},{4,5},{5,4},{6,7},{7,6},{8,9},{9,8},{10,11... | collective-permute-start | bytes 3145736 | tf_op jit(solution)/shard_map/ppermute | solution.py:447
  28.4 7.1 %collective-permute-done.4.down = bf16[538,4,128]{2,1,0:T(4,128)(2,1)S(1)} collective-permute-done((bf16[538,4,128]{2,1,0:T(4,128)(2,1)S(1)}, bf16[538,4,128]{2,1,0:T(4,128)(2,1)S(1)}, u32[]{:S(2)}, u32[]{:S(2)}) %collective-permute-start.4) | collective-permute-done | bytes 550944 | tf_op jit(solution)/shard_map/ppermute | solution.py:441
  35.5 0.0 collective-permute-done.3.up
  35.5 3.4 %gather.3 = (bf16[4,1024,128]{2,1,0:T(8,128)(2,1)}, bf16[4,512,128]{2,1,0:T(8,128)(2,1)}, bf16[4,512,128]{2,1,0:T(8,128)(2,1)}) custom-call(bf16[256,2304]{1,0:T(8,128)(2,1)S(1)} %get-tuple-element.19.matrix, bf16[600,4,128]{2,1,0:T(4,128)(2,1)S(1)} %collective-permute-done.3.up, bf16[538,4,128]{2,1,0:T(4,128)(2,1)S(1)} %collective-permute-done.4.down, ...), custom_call_target="tpu_custom_call" | custom-call | flops 2415919104 | bytes 6291456 | tf_op jit(solution)/shard_map/gather/pallas_call | solution.py:253
  39.0 2.4 %collective-permute-start.5 = (bf16[4,1024,128]{2,1,0:T(8,128)(2,1)}, bf16[4,1024,128]{2,1,0:T(8,128)(2,1)}, u32[]{:S(2)}, u32[]{:S(2)}) collective-permute-start(bf16[4,1024,128]{2,1,0:T(8,128)(2,1)} %get-tuple-element.28.own), channel_id=1, source_target_pairs={{0,1},{1,0},{2,3},{3,2},{4,5},{5,4},{6,7},{7,6},{8,9},{9,8},{10,11... | collective-permute-start | bytes 3145736 | tf_op jit(solution)/shard_map/ppermute | solution.py:447
  41.3 4.4 %collective-permute-start.2 = (bf16[4,1024,128]{2,1,0:T(8,128)(2,1)S(1)}, bf16[4,1024,128]{2,1,0:T(8,128)(2,1)}, u32[]{:S(2)}, u32[]{:S(2)}) collective-permute-start(bf16[4,1024,128]{2,1,0:T(8,128)(2,1)S(1)} %gather.2.own), channel_id=1, source_target_pairs={{1,2},{3,4},{5,6},{7,8},{9,10},{11,12},{13,14},{15,16},{17,18},{19... | collective-permute-start | bytes 3145736 | tf_op jit(solution)/shard_map/ppermute | solution.py:452
  45.7 2.7 %collective-permute-start.8 = (bf16[4,512,128]{2,1,0:T(8,128)(2,1)}, bf16[4,512,128]{2,1,0:T(8,128)(2,1)S(1)}, u32[]{:S(2)}, u32[]{:S(2)}) collective-permute-start(bf16[4,512,128]{2,1,0:T(8,128)(2,1)} %get-tuple-element.30), channel_id=1, source_target_pairs={{1,2},{3,4},{5,6},{7,8},{9,10},{11,12},{13,14},{15,16},{17,18},{19... | collective-permute-start | bytes 1572872 | tf_op jit(solution)/shard_map/ppermute | solution.py:452
  48.4 4.4 %collective-permute-start.7 = (bf16[4,512,128]{2,1,0:T(8,128)(2,1)}, bf16[4,512,128]{2,1,0:T(8,128)(2,1)}, u32[]{:S(2)}, u32[]{:S(2)}) collective-permute-start(bf16[4,512,128]{2,1,0:T(8,128)(2,1)} %get-tuple-element.29), channel_id=1, source_target_pairs={{1,2},{3,4},{5,6},{7,8},{9,10},{11,12},{13,14},{15,16},{17,18},{19... | collective-permute-start | bytes 1572872 | tf_op jit(solution)/shard_map/ppermute | solution.py:452
  52.8 0.0 collective-permute-done.6.near
  52.8 4.5 %early.2.rest_0_ = f32[64,64,256]{2,1,0:T(8,128)S(1)} custom-call(s32[1]{0:T(128)} %bitcast.flip_ref, f32[2,27,64,128]{3,2,1,0:T(8,128)S(1)} %get-tuple-element.18.weights, bf16[4,1024,128]{2,1,0:T(8,128)(2,1)S(1)} %gather.2.own, bf16[4,1024,128]{2,1,0:T(8,128)(2,1)} %collective-permute-done.6.near), custom_call_target="tpu_custom_call" | custom-call | flops 28311552 | bytes 10485760 | tf_op jit(solution)/shard_map/early/pallas_call | solution.py:334
  57.3 0.0 collective-permute-done.5.near
  57.3 4.8 %early.3.given = f32[64,64,256]{2,1,0:T(8,128)S(1)} custom-call(s32[1]{0:T(128)} %bitcast.flip_ref, f32[2,27,64,128]{3,2,1,0:T(8,128)S(1)} %get-tuple-element.18.weights, bf16[4,1024,128]{2,1,0:T(8,128)(2,1)} %get-tuple-element.28.own, bf16[4,1024,128]{2,1,0:T(8,128)(2,1)} %collective-permute-done.5.near, f32[64,64,256]{2,1,0:T(8,128)S(1)} %early.2.rest_0_), custom_call_target="tpu_custom_call" | custom-call | flops 28311552 | bytes 10485760 | tf_op jit(solution)/shard_map/early/pallas_call | solution.py:334
  62.2 19.4 %collective-permute-done.2.far = bf16[4,1024,128]{2,1,0:T(8,128)(2,1)} collective-permute-done((bf16[4,1024,128]{2,1,0:T(8,128)(2,1)S(1)}, bf16[4,1024,128]{2,1,0:T(8,128)(2,1)}, u32[]{:S(2)}, u32[]{:S(2)}) %collective-permute-start.2) | collective-permute-done | bytes 1048608 | tf_op jit(solution)/shard_map/ppermute | solution.py:452
  81.5 3.5 %add_far.1.totals = f32[64,64,256]{2,1,0:T(8,128)S(1)} custom-call(s32[1]{0:T(128)S(6)} %sub.28.flip_ref, f32[2,27,64,128]{3,2,1,0:T(8,128)S(1)} %get-tuple-element.18.weights, bf16[4,1024,128]{2,1,0:T(8,128)(2,1)} %collective-permute-done.2.far, f32[64,64,256]{2,1,0:T(8,128)S(1)} %early.3.given), custom_call_target="tpu_custom_call" | custom-call | flops 7077888 | bytes 8388608 | tf_op jit(solution)/shard_map/add_far/pallas_call | solution.py:364
  85.0 2.0 %collective-permute-done.8.far = bf16[4,512,128]{2,1,0:T(8,128)(2,1)S(1)} collective-permute-done((bf16[4,512,128]{2,1,0:T(8,128)(2,1)}, bf16[4,512,128]{2,1,0:T(8,128)(2,1)S(1)}, u32[]{:S(2)}, u32[]{:S(2)}) %collective-permute-start.8) | collective-permute-done | bytes 524320 | tf_op jit(solution)/shard_map/ppermute | solution.py:452
  87.0 3.7 %finish.2.rest_0_ = bf16[64,16,4,256]{3,2,1,0:T(4,128)(2,1)} custom-call(s32[1]{0:T(128)S(6)} %sub.28.flip_ref, f32[2,27,64,128]{3,2,1,0:T(8,128)S(1)} %get-tuple-element.18.weights, f32[64,64,256]{2,1,0:T(8,128)S(1)} %add_far.1.totals, bf16[4,512,128]{2,1,0:T(8,128)(2,1)S(1)} %collective-permute-done.8.far), custom_call_target="tpu_custom_call" | custom-call | flops 3538944 | bytes 3145728 | tf_op jit(solution)/shard_map/finish/pallas_call | solution.py:414
  90.7 2.1 %collective-permute-done.7.far = bf16[4,512,128]{2,1,0:T(8,128)(2,1)} collective-permute-done((bf16[4,512,128]{2,1,0:T(8,128)(2,1)}, bf16[4,512,128]{2,1,0:T(8,128)(2,1)}, u32[]{:S(2)}, u32[]{:S(2)}) %collective-permute-start.7) | collective-permute-done | bytes 524320 | tf_op jit(solution)/shard_map/ppermute | solution.py:452
  92.8 4.5 %finish.3 = bf16[64,16,4,256]{3,2,1,0:T(4,128)(2,1)} custom-call(s32[1]{0:T(128)S(6)} %sub.28.flip_ref, f32[2,27,64,128]{3,2,1,0:T(8,128)S(1)} %get-tuple-element.18.weights, f32[64,64,256]{2,1,0:T(8,128)S(1)} %add_far.1.totals, bf16[4,512,128]{2,1,0:T(8,128)(2,1)} %collective-permute-done.7.far, ...), custom_call_target="tpu_custom_call", output_to_operand_aliasing={{}: (4, {})} | custom-call | flops 3538944 | bytes 3145728 | tf_op jit(solution)/shard_map/finish/pallas_call | solution.py:414
  (8 shorter events, 0.0 us)
Async XLA Ops:
  0.0 8.0 %copy-start.3 = (s32[64]{0:T(128)S(1)}, s32[64]{0:T(128)}, u32[]{:S(2)}) copy-start(s32[64]{0:T(128)} %param.8) | copy-start | bytes 772
  0.0 9.5 %copy-start.2 = (s32[16,4,256]{2,1,0:T(4,128)S(1)}, s32[16,4,256]{2,1,0:T(4,128)}, u32[]{:S(2)}) copy-start(s32[16,4,256]{2,1,0:T(4,128)} %param.6) | copy-start | bytes 196612
  0.0 9.6 %copy-start.1 = (f32[8,27]{1,0:T(8,128)S(1)}, f32[8,27]{1,0:T(8,128)}, u32[]{:S(2)}) copy-start(f32[8,27]{1,0:T(8,128)} %coefficients.1) | copy-start | bytes 2596
  2.7 20.6 %collective-permute-start = (bf16[600,4,128]{2,1,0:T(4,128)(2,1)}, bf16[600,4,128]{2,1,0:T(4,128)(2,1)S(1)}, u32[]{:S(2)}, u32[]{:S(2)}) collective-permute-start(bf16[600,4,128]{2,1,0:T(4,128)(2,1)} %get-tuple-element.20), channel_id=1, source_target_pairs={{0,32},{32,64},{64,96},{96,128},{128,160},{160,192},{192,224},{1,3... | collective-permute-start | bytes 1843208 | tf_op jit(solution)/shard_map/ppermute | solution.py:440
  5.8 17.5 %collective-permute-start.1 = (bf16[538,4,128]{2,1,0:T(4,128)(2,1)}, bf16[538,4,128]{2,1,0:T(4,128)(2,1)}, u32[]{:S(2)}, u32[]{:S(2)}) collective-permute-start(bf16[538,4,128]{2,1,0:T(4,128)(2,1)} %get-tuple-element.21), channel_id=1, source_target_pairs={{32,0},{64,32},{96,64},{128,96},{160,128},{192,160},{224,192},{33,... | collective-permute-start | bytes 1652744 | tf_op jit(solution)/shard_map/ppermute | solution.py:441
  9.6 1.6 %copy-start = (bf16[64,16,4,256]{3,2,1,0:T(4,128)(2,1)S(1)}, bf16[64,16,4,256]{3,2,1,0:T(4,128)(2,1)}, u32[]{:S(2)}) copy-start(bf16[64,16,4,256]{3,2,1,0:T(4,128)(2,1)} %image.3) | copy-start | bytes 6291460
  13.8 21.8 %collective-permute-start.3 = (bf16[600,4,128]{2,1,0:T(4,128)(2,1)S(1)}, bf16[600,4,128]{2,1,0:T(4,128)(2,1)S(1)}, u32[]{:S(2)}, u32[]{:S(2)}) collective-permute-start(bf16[600,4,128]{2,1,0:T(4,128)(2,1)S(1)} %get-tuple-element.25), channel_id=1, source_target_pairs={{0,32},{32,64},{64,96},{96,128},{128,160},{160,192},{192,224},{1,3... | collective-permute-start | bytes 1843208 | tf_op jit(solution)/shard_map/ppermute | solution.py:440
  19.0 16.5 %collective-permute-start.4 = (bf16[538,4,128]{2,1,0:T(4,128)(2,1)S(1)}, bf16[538,4,128]{2,1,0:T(4,128)(2,1)S(1)}, u32[]{:S(2)}, u32[]{:S(2)}) collective-permute-start(bf16[538,4,128]{2,1,0:T(4,128)(2,1)S(1)} %get-tuple-element.26), channel_id=1, source_target_pairs={{32,0},{64,32},{96,64},{128,96},{160,128},{192,160},{224,192},{33,... | collective-permute-start | bytes 1652744 | tf_op jit(solution)/shard_map/ppermute | solution.py:441
  26.6 26.3 %collective-permute-start.6 = (bf16[4,1024,128]{2,1,0:T(8,128)(2,1)S(1)}, bf16[4,1024,128]{2,1,0:T(8,128)(2,1)}, u32[]{:S(2)}, u32[]{:S(2)}) collective-permute-start(bf16[4,1024,128]{2,1,0:T(8,128)(2,1)S(1)} %gather.2.own), channel_id=1, source_target_pairs={{0,1},{1,0},{2,3},{3,2},{4,5},{5,4},{6,7},{7,6},{8,9},{9,8},{10,11... | collective-permute-start | bytes 3145736 | tf_op jit(solution)/shard_map/ppermute | solution.py:447
  39.0 18.4 %collective-permute-start.5 = (bf16[4,1024,128]{2,1,0:T(8,128)(2,1)}, bf16[4,1024,128]{2,1,0:T(8,128)(2,1)}, u32[]{:S(2)}, u32[]{:S(2)}) collective-permute-start(bf16[4,1024,128]{2,1,0:T(8,128)(2,1)} %get-tuple-element.28.own), channel_id=1, source_target_pairs={{0,1},{1,0},{2,3},{3,2},{4,5},{5,4},{6,7},{7,6},{8,9},{9,8},{10,11... | collective-permute-start | bytes 3145736 | tf_op jit(solution)/shard_map/ppermute | solution.py:447
  41.3 40.2 %collective-permute-start.2 = (bf16[4,1024,128]{2,1,0:T(8,128)(2,1)S(1)}, bf16[4,1024,128]{2,1,0:T(8,128)(2,1)}, u32[]{:S(2)}, u32[]{:S(2)}) collective-permute-start(bf16[4,1024,128]{2,1,0:T(8,128)(2,1)S(1)} %gather.2.own), channel_id=1, source_target_pairs={{1,2},{3,4},{5,6},{7,8},{9,10},{11,12},{13,14},{15,16},{17,18},{19... | collective-permute-start | bytes 3145736 | tf_op jit(solution)/shard_map/ppermute | solution.py:452
  45.7 41.3 %collective-permute-start.8 = (bf16[4,512,128]{2,1,0:T(8,128)(2,1)}, bf16[4,512,128]{2,1,0:T(8,128)(2,1)S(1)}, u32[]{:S(2)}, u32[]{:S(2)}) collective-permute-start(bf16[4,512,128]{2,1,0:T(8,128)(2,1)} %get-tuple-element.30), channel_id=1, source_target_pairs={{1,2},{3,4},{5,6},{7,8},{9,10},{11,12},{13,14},{15,16},{17,18},{19... | collective-permute-start | bytes 1572872 | tf_op jit(solution)/shard_map/ppermute | solution.py:452
  48.4 44.4 %collective-permute-start.7 = (bf16[4,512,128]{2,1,0:T(8,128)(2,1)}, bf16[4,512,128]{2,1,0:T(8,128)(2,1)}, u32[]{:S(2)}, u32[]{:S(2)}) collective-permute-start(bf16[4,512,128]{2,1,0:T(8,128)(2,1)} %get-tuple-element.29), channel_id=1, source_target_pairs={{1,2},{3,4},{5,6},{7,8},{9,10},{11,12},{13,14},{15,16},{17,18},{19... | collective-permute-start | bytes 1572872 | tf_op jit(solution)/shard_map/ppermute | solution.py:452

commit v5 on v4

--- a/solution.py
+++ b/solution.py
@@ -15,7 +15,7 @@
 REACH = R - BAND
 ZB = 4
 HALVES = 2
-LAST_PARTS = (8, 8)
+LAST_PARTS = (8, 4, 4)
 PART = 32
 SIDES = 2 * RY + 1
 BF = jnp.bfloat16
@@ -381,23 +381,20 @@
     def _():
         unswap[...] = unswap_matrix(angles, x)
 
-    def level(j, carry):
+    for j in range(ZB):
         for n in range(x):
             column = mirrored(n, x, flip)
             row = (first + base + j) * x + column
             terms = beside_terms(far, n, column, x, flip)
             for piece in range(angles // PART):
-                at = pl.multiple_of(j * angles + piece * PART, PART)
+                at = j * angles + piece * PART
                 part = slice(piece * PART, (piece + 1) * PART)
                 sums = half_sums(weights, 1, row, at, terms)
                 total = totals[row, part, :] + spread(sums, 1)
                 to = pl.multiple_of(column * angles + piece * PART, PART)
-                scratch[pl.ds(to, PART), :] = total.astype(BF)
-        moved = jnp.dot(unswap[...], scratch[...], preferred_element_type=F32)
+                scratch[j, pl.ds(to, PART), :] = total.astype(BF)
+        moved = jnp.dot(unswap[...], scratch[j], preferred_element_type=F32)
         out[:, j] = moved.astype(BF).reshape(angles, x, out.shape[3])
-        return carry
-
-    lax.fori_loop(0, ZB, level, 0)
 
 
 def finish(flip, weights, totals, far, done, first, shape):
@@ -417,7 +414,7 @@
         out_shape=struct(shape),
         in_specs=in_specs,
         out_specs=pl.BlockSpec((angles, ZB, x, y), lambda i: (0, first // ZB + i, 0, 0)),
-        scratch_shapes=[pltpu.VMEM((angles * x, y), BF), pltpu.VMEM((angles * x,) * 2, BF)],
+        scratch_shapes=[pltpu.VMEM((ZB, angles * x, y), BF), pltpu.VMEM((angles * x,) * 2, BF)],
         input_output_aliases=aliases,
         compiler_params=params(14),
         cost_estimate=cost(weights.shape[1] * angles * planes * x * y // 4, 3 << 20),

time: 97.8 us -> 95.6 us (0.978)
  the two profiles are of different devices: /device:TPU:135 before, /device:TPU:103 now
where the time goes in v5:
time: 95.6 us; the launch traced here: 95 us
  Pallas kernels  31.7 us (33%)
  starting transfers between devices  30.8 us (32%)
  waiting for transfers between devices  25.1 us (26%)
  local copies, waits for them, and re-layouts  5.66 us (6%)
  other arithmetic  1.49 us (2%)
    ppermute x4, waiting for transfers between devices, far_of(): return lax.ppermute(x, axis, pairs + [(j, i) for i, j in pairs])  18.7 us
    ppermute x4, starting transfers between devices, far_of(): return lax.ppermute(x, axis, pairs + [(j, i) for i, j in pairs])  14.3 us
    ppermute x2, starting transfers between devices, exchange(): from_up = lax.ppermute(x_up, axis, up)  8.36 us
    pallas_call x2, Pallas kernels, early(): pl.pallas_call(functools.partial(early_kernel, half, angles, x), out_shap...  8.05 us
    pallas_call x3, Pallas kernels, finish(): pl.pallas_call(functools.partial(finish_kernel, angles, x, first), grid=(...  6.96 us
    ppermute x2, waiting for transfers between devices, exchange(): from_down = lax.ppermute(x_down, axis, down)  6.4 us
    unnamed x16, local copies, waits for them, and re-layouts  5.64 us
    pallas_call x2, Pallas kernels, gather(): pl.pallas_call(functools.partial(gather_kernel, before, after, parts), ou...  5.58 us
  transfers between devices with their start and end apart: 10, of which 5 were waited for; matrix products, arithmetic and copies ran while one was open for 2% of the time, Pallas kernels for 28%

profile of v5, /device:TPU:103, one launch (start us, length us, event | category | flops | bytes accessed | tf_op | source)
XLA Modules:
  0.0 95.0 jit_solution(13672894161454230861)
XLA Ops:
  0.0 2.7 %pack.1 = (bf16[600,4,128]{2,1,0:T(4,128)(2,1)}, bf16[538,4,128]{2,1,0:T(4,128)(2,1)}) custom-call(bf16[64,16,4,256]{3,2,1,0:T(4,128)(2,1)} %image.3), custom_call_target="tpu_custom_call" | custom-call | tf_op jit(solution)/shard_map/pack/pallas_call | solution.py:102
  2.7 3.1 %collective-permute-start = (bf16[600,4,128]{2,1,0:T(4,128)(2,1)}, bf16[600,4,128]{2,1,0:T(4,128)(2,1)S(1)}, u32[]{:S(2)}, u32[]{:S(2)}) collective-permute-start(bf16[600,4,128]{2,1,0:T(4,128)(2,1)} %get-tuple-element.21), channel_id=1, source_target_pairs={{0,32},{32,64},{64,96},{96,128},{128,160},{160,192},{192,224},{1,3... | collective-permute-start | bytes 1843208 | tf_op jit(solution)/shard_map/ppermute | solution.py:437
  5.8 2.2 %collective-permute-start.1 = (bf16[538,4,128]{2,1,0:T(4,128)(2,1)}, bf16[538,4,128]{2,1,0:T(4,128)(2,1)S(1)}, u32[]{:S(2)}, u32[]{:S(2)}) collective-permute-start(bf16[538,4,128]{2,1,0:T(4,128)(2,1)} %get-tuple-element.22), channel_id=1, source_target_pairs={{32,0},{64,32},{96,64},{128,96},{160,128},{192,160},{224,192},{33,... | collective-permute-start | bytes 1652744 | tf_op jit(solution)/shard_map/ppermute | solution.py:438
  8.1 1.4 %fusion.1.slant = bf16[33,64,64]{2,1,0:T(8,128)(2,1)S(1)} fusion(bf16[64,64,33]{1,0,2:T(8,128)(2,1)} %param.7, s32[64,64]{1,0:T(8,128)S(1)} %add_select_fusion, s32[33]{0:T(128)S(1)} %iota_add_fusion), kind=kLoop, calls=%fused_computation.2 | loop fusion | flops 540672 | bytes 557188 | tf_op jit(solution)/shard_map/transpose | solution.py:457
  9.6 1.6 %copy-done = bf16[64,16,4,256]{3,2,1,0:T(4,128)(2,1)S(1)} copy-done((bf16[64,16,4,256]{3,2,1,0:T(4,128)(2,1)S(1)}, bf16[64,16,4,256]{3,2,1,0:T(4,128)(2,1)}, u32[]{:S(2)}) %copy-start) | copy-done | bytes 2097176
  11.2 2.6 %prepare.1 = (bf16[600,4,128]{2,1,0:T(4,128)(2,1)S(1)}, bf16[538,4,128]{2,1,0:T(4,128)(2,1)S(1)}, bf16[2,1024,256]{2,1,0:T(8,128)(2,1)S(1)}, bf16[2,1024,256]{2,...) custom-call(bf16[64,16,4,256]{3,2,1,0:T(4,128)(2,1)S(1)} %copy-done, ...), custom_call_target="tpu_custom_call" | custom-call | flops 536870912 | bytes 8388608 | tf_op jit(solution)/shard_map/prepare/pallas_call | solution.py:155
  13.8 5.2 %collective-permute-start.3 = (bf16[600,4,128]{2,1,0:T(4,128)(2,1)S(1)}, bf16[600,4,128]{2,1,0:T(4,128)(2,1)S(1)}, u32[]{:S(2)}, u32[]{:S(2)}) collective-permute-start(bf16[600,4,128]{2,1,0:T(4,128)(2,1)S(1)} %get-tuple-element.26), channel_id=1, source_target_pairs={{0,32},{32,64},{64,96},{96,128},{128,160},{160,192},{192,224},{1,3... | collective-permute-start | bytes 1843208 | tf_op jit(solution)/shard_map/ppermute | solution.py:437
  19.0 1.9 %collective-permute-start.4 = (bf16[538,4,128]{2,1,0:T(4,128)(2,1)S(1)}, bf16[538,4,128]{2,1,0:T(4,128)(2,1)S(1)}, u32[]{:S(2)}, u32[]{:S(2)}) collective-permute-start(bf16[538,4,128]{2,1,0:T(4,128)(2,1)S(1)} %get-tuple-element.27), channel_id=1, source_target_pairs={{32,0},{64,32},{96,64},{128,96},{160,128},{192,160},{224,192},{33,... | collective-permute-start | bytes 1652744 | tf_op jit(solution)/shard_map/ppermute | solution.py:438
  20.9 2.3 %own_part.1 = (f32[4,2,256,256]{3,2,1,0:T(8,128)S(1)}, f32[4,2,256,256]{3,2,1,0:T(8,128)S(1)}) custom-call(bf16[256,2304]{1,0:T(8,128)(2,1)S(1)} %get-tuple-element.20.matrix, bf16[2,1024,256]{2,1,0:T(8,128)(2,1)S(1)} %get-tuple-element.23.mid_a, bf16[2,1024,256]{2,1,0:T(8,128)(2,1)S(1)} %get-tuple-element.24.mid_b), custom_call_target="tpu_custom_call" | custom-call | flops 2147483648 | bytes 9437184 | tf_op jit(solution)/shard_map/own_part/pallas_call | solution.py:203
  23.3 0.8 copy-done.4
  24.1 1.1 %copy-done.5 = bf16[538,4,128]{2,1,0:T(4,128)(2,1)S(1)} copy-done((bf16[538,4,128]{2,1,0:T(4,128)(2,1)S(1)}, bf16[538,4,128]{2,1,0:T(4,128)(2,1)}, u32[]{:S(2)}) %copy-start.5) | copy-done | bytes 550936
  25.2 2.3 %gather.2.own = bf16[4,1024,128]{2,1,0:T(8,128)(2,1)S(1)} custom-call(bf16[256,2304]{1,0:T(8,128)(2,1)S(1)} %get-tuple-element.20.matrix, bf16[600,4,128]{2,1,0:T(4,128)(2,1)S(1)} %collective-permute-done.up, bf16[538,4,128]{2,1,0:T(4,128)(2,1)S(1)} %copy-done.5, f32[4,2,256,256]{3,2,1,0:T(8,128)S(1)} %get-tuple-element.25.given), custom_call_target="tpu_custom_call" | custom-call | flops 2415919104 | bytes 6291456 | tf_op jit(solution)/shard_map/gather/pallas_call | solution.py:253
  27.4 1.7 %collective-permute-start.6 = (bf16[4,1024,128]{2,1,0:T(8,128)(2,1)S(1)}, bf16[4,1024,128]{2,1,0:T(8,128)(2,1)S(1)}, u32[]{:S(2)}, u32[]{:S(2)}) collective-permute-start(bf16[4,1024,128]{2,1,0:T(8,128)(2,1)S(1)} %gather.2.own), channel_id=1, source_target_pairs={{0,1},{1,0},{2,3},{3,2},{4,5},{5,4},{6,7},{7,6},{8,9},{9,8},{10,11... | collective-permute-start | bytes 3145736 | tf_op jit(solution)/shard_map/ppermute | solution.py:444
  29.2 6.4 %collective-permute-done.4.down = bf16[538,4,128]{2,1,0:T(4,128)(2,1)S(1)} collective-permute-done((bf16[538,4,128]{2,1,0:T(4,128)(2,1)S(1)}, bf16[538,4,128]{2,1,0:T(4,128)(2,1)S(1)}, u32[]{:S(2)}, u32[]{:S(2)}) %collective-permute-start.4) | collective-permute-done | bytes 550944 | tf_op jit(solution)/shard_map/ppermute | solution.py:438
  35.6 3.3 %gather.3 = (bf16[4,1024,128]{2,1,0:T(8,128)(2,1)}, bf16[4,512,128]{2,1,0:T(8,128)(2,1)}, bf16[4,256,128]{2,1,0:T(8,128)(2,1)}, bf16[4,256,128]{2,1,0:T(8,128)(2,1)}) custom-call(bf16[256,2304]{1,0:T(8,128)(2,1)S(1)} %get-tuple-element.20.matrix, bf16[600,4,128]{2,1,0:T(4,128)(2,1)S(1)} %collective-permute-done.3.up, ...), custom_call_target="tpu_custom_call" | custom-call | flops 2415919104 | bytes 6291456 | tf_op jit(solution)/shard_map/gather/pallas_call | solution.py:253
  38.9 2.4 %collective-permute-start.5 = (bf16[4,1024,128]{2,1,0:T(8,128)(2,1)}, bf16[4,1024,128]{2,1,0:T(8,128)(2,1)}, u32[]{:S(2)}, u32[]{:S(2)}) collective-permute-start(bf16[4,1024,128]{2,1,0:T(8,128)(2,1)} %get-tuple-element.29.own), channel_id=1, source_target_pairs={{0,1},{1,0},{2,3},{3,2},{4,5},{5,4},{6,7},{7,6},{8,9},{9,8},{10,11... | collective-permute-start | bytes 3145736 | tf_op jit(solution)/shard_map/ppermute | solution.py:444
  41.2 4.4 %collective-permute-start.2 = (bf16[4,1024,128]{2,1,0:T(8,128)(2,1)S(1)}, bf16[4,1024,128]{2,1,0:T(8,128)(2,1)}, u32[]{:S(2)}, u32[]{:S(2)}) collective-permute-start(bf16[4,1024,128]{2,1,0:T(8,128)(2,1)S(1)} %gather.2.own), channel_id=1, source_target_pairs={{1,2},{3,4},{5,6},{7,8},{9,10},{11,12},{13,14},{15,16},{17,18},{19... | collective-permute-start | bytes 3145736 | tf_op jit(solution)/shard_map/ppermute | solution.py:449
  45.6 2.7 %collective-permute-start.9 = (bf16[4,512,128]{2,1,0:T(8,128)(2,1)}, bf16[4,512,128]{2,1,0:T(8,128)(2,1)S(1)}, u32[]{:S(2)}, u32[]{:S(2)}) collective-permute-start(bf16[4,512,128]{2,1,0:T(8,128)(2,1)} %get-tuple-element.32), channel_id=1, source_target_pairs={{1,2},{3,4},{5,6},{7,8},{9,10},{11,12},{13,14},{15,16},{17,18},{19... | collective-permute-start | bytes 1572872 | tf_op jit(solution)/shard_map/ppermute | solution.py:449
  48.3 4.4 %collective-permute-start.8 = (bf16[4,256,128]{2,1,0:T(8,128)(2,1)}, bf16[4,256,128]{2,1,0:T(8,128)(2,1)}, u32[]{:S(2)}, u32[]{:S(2)}) collective-permute-start(bf16[4,256,128]{2,1,0:T(8,128)(2,1)} %get-tuple-element.31), channel_id=1, source_target_pairs={{1,2},{3,4},{5,6},{7,8},{9,10},{11,12},{13,14},{15,16},{17,18},{19... | collective-permute-start | bytes 786440 | tf_op jit(solution)/shard_map/ppermute | solution.py:449
  52.7 1.0 %copy-done.1 = bf16[4,1024,128]{2,1,0:T(8,128)(2,1)} copy-done((bf16[4,1024,128]{2,1,0:T(8,128)(2,1)}, bf16[4,1024,128]{2,1,0:T(8,128)(2,1)S(1)}, u32[]{:S(2)}) %copy-start.1) | copy-done | bytes 1048600
  53.7 2.8 %collective-permute-start.7 = (bf16[4,256,128]{2,1,0:T(8,128)(2,1)}, bf16[4,256,128]{2,1,0:T(8,128)(2,1)}, u32[]{:S(2)}, u32[]{:S(2)}) collective-permute-start(bf16[4,256,128]{2,1,0:T(8,128)(2,1)} %get-tuple-element.30), channel_id=1, source_target_pairs={{1,2},{3,4},{5,6},{7,8},{9,10},{11,12},{13,14},{15,16},{17,18},{19... | collective-permute-start | bytes 786440 | tf_op jit(solution)/shard_map/ppermute | solution.py:449
  56.6 1.2 %copy-done.2 = bf16[4,1024,128]{2,1,0:T(8,128)(2,1)S(1)} copy-done((bf16[4,1024,128]{2,1,0:T(8,128)(2,1)S(1)}, bf16[4,1024,128]{2,1,0:T(8,128)(2,1)}, u32[]{:S(2)}) %copy-start.2) | copy-done | bytes 1048600
  57.8 3.2 %early.2.rest_0_ = f32[64,64,256]{2,1,0:T(8,128)S(1)} custom-call(s32[1]{0:T(128)} %bitcast.flip_ref, f32[2,27,64,128]{3,2,1,0:T(8,128)S(1)} %get-tuple-element.19.weights, bf16[4,1024,128]{2,1,0:T(8,128)(2,1)S(1)} %gather.2.own, bf16[4,1024,128]{2,1,0:T(8,128)(2,1)S(1)} %copy-done.2), custom_call_target="tpu_custom_call" | custom-call | flops 28311552 | bytes 10485760 | tf_op jit(solution)/shard_map/early/pallas_call | solution.py:334
  61.0 4.8 %early.3.given = f32[64,64,256]{2,1,0:T(8,128)S(1)} custom-call(s32[1]{0:T(128)} %bitcast.flip_ref, f32[2,27,64,128]{3,2,1,0:T(8,128)S(1)} %get-tuple-element.19.weights, bf16[4,1024,128]{2,1,0:T(8,128)(2,1)} %get-tuple-element.29.own, bf16[4,1024,128]{2,1,0:T(8,128)(2,1)} %collective-permute-done.5.near, f32[64,64,256]{2,1,0:T(8,128)S(1)} %early.2.rest_0_), custom_call_target="tpu_custom_call" | custom-call | flops 28311552 | bytes 10485760 | tf_op jit(solution)/shard_map/early/pallas_call | solution.py:334
  65.9 15.6 %collective-permute-done.2.far = bf16[4,1024,128]{2,1,0:T(8,128)(2,1)} collective-permute-done((bf16[4,1024,128]{2,1,0:T(8,128)(2,1)S(1)}, bf16[4,1024,128]{2,1,0:T(8,128)(2,1)}, u32[]{:S(2)}, u32[]{:S(2)}) %collective-permute-start.2) | collective-permute-done | bytes 1048608 | tf_op jit(solution)/shard_map/ppermute | solution.py:449
  81.4 3.5 %add_far.1.totals = f32[64,64,256]{2,1,0:T(8,128)S(1)} custom-call(s32[1]{0:T(128)S(6)} %sub.16.flip_ref, f32[2,27,64,128]{3,2,1,0:T(8,128)S(1)} %get-tuple-element.19.weights, bf16[4,1024,128]{2,1,0:T(8,128)(2,1)} %collective-permute-done.2.far, f32[64,64,256]{2,1,0:T(8,128)S(1)} %early.3.given), custom_call_target="tpu_custom_call" | custom-call | flops 7077888 | bytes 8388608 | tf_op jit(solution)/shard_map/add_far/pallas_call | solution.py:364
  84.9 2.0 %collective-permute-done.9.far = bf16[4,512,128]{2,1,0:T(8,128)(2,1)S(1)} collective-permute-done((bf16[4,512,128]{2,1,0:T(8,128)(2,1)}, bf16[4,512,128]{2,1,0:T(8,128)(2,1)S(1)}, u32[]{:S(2)}, u32[]{:S(2)}) %collective-permute-start.9) | collective-permute-done | bytes 524320 | tf_op jit(solution)/shard_map/ppermute | solution.py:449
  86.9 2.2 %finish.3.rest_0_ = bf16[64,16,4,256]{3,2,1,0:T(4,128)(2,1)} custom-call(s32[1]{0:T(128)S(6)} %sub.16.flip_ref, f32[2,27,64,128]{3,2,1,0:T(8,128)S(1)} %get-tuple-element.19.weights, f32[64,64,256]{2,1,0:T(8,128)S(1)} %add_far.1.totals, bf16[4,512,128]{2,1,0:T(8,128)(2,1)S(1)} %collective-permute-done.9.far), custom_call_target="tpu_custom_call" | custom-call | flops 3538944 | bytes 3145728 | tf_op jit(solution)/shard_map/finish/pallas_call | solution.py:411
  89.1 0.7 collective-permute-done.8.far
  89.8 2.4 %finish.4.rest_0_ = bf16[64,16,4,256]{3,2,1,0:T(4,128)(2,1)} custom-call(s32[1]{0:T(128)S(6)} %sub.16.flip_ref, f32[2,27,64,128]{3,2,1,0:T(8,128)S(1)} %get-tuple-element.19.weights, f32[64,64,256]{2,1,0:T(8,128)S(1)} %add_far.1.totals, bf16[4,256,128]{2,1,0:T(8,128)(2,1)} %collective-permute-done.8.far, ...), custom_call_target="tpu_custom_call", output_to_operand_aliasing={{}: (4, {})} | custom-call | flops 1769472 | bytes 3145728 | tf_op jit(solution)/shard_map/finish/pallas_call | solution.py:411
  92.2 0.4 collective-permute-done.7.far
  92.7 2.4 %finish.5 = bf16[64,16,4,256]{3,2,1,0:T(4,128)(2,1)} custom-call(s32[1]{0:T(128)S(6)} %sub.16.flip_ref, f32[2,27,64,128]{3,2,1,0:T(8,128)S(1)} %get-tuple-element.19.weights, f32[64,64,256]{2,1,0:T(8,128)S(1)} %add_far.1.totals, bf16[4,256,128]{2,1,0:T(8,128)(2,1)} %collective-permute-done.7.far, ...), custom_call_target="tpu_custom_call", output_to_operand_aliasing={{}: (4, {})} | custom-call | flops 1769472 | bytes 3145728 | tf_op jit(solution)/shard_map/finish/pallas_call | solution.py:411
  (19 shorter events, 0.2 us)
Async XLA Ops:
  0.0 8.0 %copy-start.7 = (s32[64]{0:T(128)S(1)}, s32[64]{0:T(128)}, u32[]{:S(2)}) copy-start(s32[64]{0:T(128)} %param.8) | copy-start | bytes 772
  0.0 8.1 %copy-start.6 = (s32[16,4,256]{2,1,0:T(4,128)S(1)}, s32[16,4,256]{2,1,0:T(4,128)}, u32[]{:S(2)}) copy-start(s32[16,4,256]{2,1,0:T(4,128)} %param.6) | copy-start | bytes 196612
  0.0 9.6 %copy-start.3 = (f32[8,27]{1,0:T(8,128)S(1)}, f32[8,27]{1,0:T(8,128)}, u32[]{:S(2)}) copy-start(f32[8,27]{1,0:T(8,128)} %coefficients.1) | copy-start | bytes 2596
  2.7 21.4 %collective-permute-start = (bf16[600,4,128]{2,1,0:T(4,128)(2,1)}, bf16[600,4,128]{2,1,0:T(4,128)(2,1)S(1)}, u32[]{:S(2)}, u32[]{:S(2)}) collective-permute-start(bf16[600,4,128]{2,1,0:T(4,128)(2,1)} %get-tuple-element.21), channel_id=1, source_target_pairs={{0,32},{32,64},{64,96},{96,128},{128,160},{160,192},{192,224},{1,3... | collective-permute-start | bytes 1843208 | tf_op jit(solution)/shard_map/ppermute | solution.py:437
  5.8 17.5 %collective-permute-start.1 = (bf16[538,4,128]{2,1,0:T(4,128)(2,1)}, bf16[538,4,128]{2,1,0:T(4,128)(2,1)S(1)}, u32[]{:S(2)}, u32[]{:S(2)}) collective-permute-start(bf16[538,4,128]{2,1,0:T(4,128)(2,1)} %get-tuple-element.22), channel_id=1, source_target_pairs={{32,0},{64,32},{96,64},{128,96},{160,128},{192,160},{224,192},{33,... | collective-permute-start | bytes 1652744 | tf_op jit(solution)/shard_map/ppermute | solution.py:438
  9.6 1.6 %copy-start = (bf16[64,16,4,256]{3,2,1,0:T(4,128)(2,1)S(1)}, bf16[64,16,4,256]{3,2,1,0:T(4,128)(2,1)}, u32[]{:S(2)}) copy-start(bf16[64,16,4,256]{3,2,1,0:T(4,128)(2,1)} %image.3) | copy-start | bytes 6291460
  13.8 21.8 %collective-permute-start.3 = (bf16[600,4,128]{2,1,0:T(4,128)(2,1)S(1)}, bf16[600,4,128]{2,1,0:T(4,128)(2,1)S(1)}, u32[]{:S(2)}, u32[]{:S(2)}) collective-permute-start(bf16[600,4,128]{2,1,0:T(4,128)(2,1)S(1)} %get-tuple-element.26), channel_id=1, source_target_pairs={{0,32},{32,64},{64,96},{96,128},{128,160},{160,192},{192,224},{1,3... | collective-permute-start | bytes 1843208 | tf_op jit(solution)/shard_map/ppermute | solution.py:437
  19.0 16.5 %collective-permute-start.4 = (bf16[538,4,128]{2,1,0:T(4,128)(2,1)S(1)}, bf16[538,4,128]{2,1,0:T(4,128)(2,1)S(1)}, u32[]{:S(2)}, u32[]{:S(2)}) collective-permute-start(bf16[538,4,128]{2,1,0:T(4,128)(2,1)S(1)} %get-tuple-element.27), channel_id=1, source_target_pairs={{32,0},{64,32},{96,64},{128,96},{160,128},{192,160},{224,192},{33,... | collective-permute-start | bytes 1652744 | tf_op jit(solution)/shard_map/ppermute | solution.py:438
  23.3 0.8 copy-start.4
  24.1 1.1 %copy-start.5 = (bf16[538,4,128]{2,1,0:T(4,128)(2,1)S(1)}, bf16[538,4,128]{2,1,0:T(4,128)(2,1)}, u32[]{:S(2)}) copy-start(bf16[538,4,128]{2,1,0:T(4,128)(2,1)} %copy-done.4) | copy-start | bytes 1652740
  27.4 25.3 %collective-permute-start.6 = (bf16[4,1024,128]{2,1,0:T(8,128)(2,1)S(1)}, bf16[4,1024,128]{2,1,0:T(8,128)(2,1)S(1)}, u32[]{:S(2)}, u32[]{:S(2)}) collective-permute-start(bf16[4,1024,128]{2,1,0:T(8,128)(2,1)S(1)} %gather.2.own), channel_id=1, source_target_pairs={{0,1},{1,0},{2,3},{3,2},{4,5},{5,4},{6,7},{7,6},{8,9},{9,8},{10,11... | collective-permute-start | bytes 3145736 | tf_op jit(solution)/shard_map/ppermute | solution.py:444
  38.9 22.2 %collective-permute-start.5 = (bf16[4,1024,128]{2,1,0:T(8,128)(2,1)}, bf16[4,1024,128]{2,1,0:T(8,128)(2,1)}, u32[]{:S(2)}, u32[]{:S(2)}) collective-permute-start(bf16[4,1024,128]{2,1,0:T(8,128)(2,1)} %get-tuple-element.29.own), channel_id=1, source_target_pairs={{0,1},{1,0},{2,3},{3,2},{4,5},{5,4},{6,7},{7,6},{8,9},{9,8},{10,11... | collective-permute-start | bytes 3145736 | tf_op jit(solution)/shard_map/ppermute | solution.py:444
  41.2 40.2 %collective-permute-start.2 = (bf16[4,1024,128]{2,1,0:T(8,128)(2,1)S(1)}, bf16[4,1024,128]{2,1,0:T(8,128)(2,1)}, u32[]{:S(2)}, u32[]{:S(2)}) collective-permute-start(bf16[4,1024,128]{2,1,0:T(8,128)(2,1)S(1)} %gather.2.own), channel_id=1, source_target_pairs={{1,2},{3,4},{5,6},{7,8},{9,10},{11,12},{13,14},{15,16},{17,18},{19... | collective-permute-start | bytes 3145736 | tf_op jit(solution)/shard_map/ppermute | solution.py:449
  45.6 41.3 %collective-permute-start.9 = (bf16[4,512,128]{2,1,0:T(8,128)(2,1)}, bf16[4,512,128]{2,1,0:T(8,128)(2,1)S(1)}, u32[]{:S(2)}, u32[]{:S(2)}) collective-permute-start(bf16[4,512,128]{2,1,0:T(8,128)(2,1)} %get-tuple-element.32), channel_id=1, source_target_pairs={{1,2},{3,4},{5,6},{7,8},{9,10},{11,12},{13,14},{15,16},{17,18},{19... | collective-permute-start | bytes 1572872 | tf_op jit(solution)/shard_map/ppermute | solution.py:449
  48.3 41.5 %collective-permute-start.8 = (bf16[4,256,128]{2,1,0:T(8,128)(2,1)}, bf16[4,256,128]{2,1,0:T(8,128)(2,1)}, u32[]{:S(2)}, u32[]{:S(2)}) collective-permute-start(bf16[4,256,128]{2,1,0:T(8,128)(2,1)} %get-tuple-element.31), channel_id=1, source_target_pairs={{1,2},{3,4},{5,6},{7,8},{9,10},{11,12},{13,14},{15,16},{17,18},{19... | collective-permute-start | bytes 786440 | tf_op jit(solution)/shard_map/ppermute | solution.py:449
  52.7 1.0 %copy-start.1 = (bf16[4,1024,128]{2,1,0:T(8,128)(2,1)}, bf16[4,1024,128]{2,1,0:T(8,128)(2,1)S(1)}, u32[]{:S(2)}) copy-start(bf16[4,1024,128]{2,1,0:T(8,128)(2,1)S(1)} %collective-permute-done.6.near) | copy-start | bytes 3145732
  53.7 38.9 %collective-permute-start.7 = (bf16[4,256,128]{2,1,0:T(8,128)(2,1)}, bf16[4,256,128]{2,1,0:T(8,128)(2,1)}, u32[]{:S(2)}, u32[]{:S(2)}) collective-permute-start(bf16[4,256,128]{2,1,0:T(8,128)(2,1)} %get-tuple-element.30), channel_id=1, source_target_pairs={{1,2},{3,4},{5,6},{7,8},{9,10},{11,12},{13,14},{15,16},{17,18},{19... | collective-permute-start | bytes 786440 | tf_op jit(solution)/shard_map/ppermute | solution.py:449
  56.6 1.2 %copy-start.2 = (bf16[4,1024,128]{2,1,0:T(8,128)(2,1)S(1)}, bf16[4,1024,128]{2,1,0:T(8,128)(2,1)}, u32[]{:S(2)}) copy-start(bf16[4,1024,128]{2,1,0:T(8,128)(2,1)} %copy-done.1) | copy-start | bytes 3145732
